TPU v7x, 32 devices: a whole 2x2x4 slice. The times are simulated.
32 devices in a mesh: groups: 2 (over y), dom: 4 (over z), sub: 2 (over x), field: 2 (over core).
Axes of the slice: x: 2, y: 2, z: 4, core: 2. Of those that a mesh axis runs over, the one named last changes fastest.
Arguments:
- background: float32 [3, 65536], P(None, ('groups', 'dom', 'sub')), parts along dimension 1, may hold values from -6 to 6
- obs_weight: float32 [65536], P(('groups', 'dom', 'sub')), parts along dimension 0, may hold values from 0.02 to 0.2
- connect: int32 [10, 32768], P(None, ('groups', 'dom', 'sub', 'field')), parts along dimension 1, may hold values from 0 to 5631, as said below
- live_blocks: int32 [32], P(('groups', 'dom', 'sub', 'field')), parts along dimension 0, may hold values from 2 to 8, as said below
- elem_scale: float32 [32768], P(('groups', 'dom', 'sub', 'field')), parts along dimension 0, may hold values from 0.5 to 2
- reg_weight: float32 [32768], P(('groups', 'dom', 'sub', 'field')), parts along dimension 0, may hold values from 0.2 to 2
- iterate: float32 [32768], P(('groups', 'dom', 'sub', 'field')), parts along dimension 0, may hold values from -6 to 6
- residual: float32 [32768], P(('groups', 'dom', 'sub', 'field')), parts along dimension 0, may hold values from -30 to 30
- direction: float32 [32768], P(('groups', 'dom', 'sub', 'field')), parts along dimension 0, may hold values from -30 to 30
- send_nodes: int32 [16, 3, 2, 256], P(('groups', 'dom', 'sub')), parts along dimension 0, may hold values from 0 to 4095, as said below
- send_count: int32 [16, 3, 2], P(('groups', 'dom', 'sub')), parts along dimension 0, may hold values from 0 to 256, as said below
- ref_stiff: float32 [30, 30], replicated, may hold values from -1.05 to 4.05, as said below
Outputs:
- iterate_next: float32 [32768], P(('groups', 'dom', 'sub', 'field')), parts along dimension 0
- residual_next: float32 [32768], P(('groups', 'dom', 'sub', 'field')), parts along dimension 0
- direction_next: float32 [32768], P(('groups', 'dom', 'sub', 'field')), parts along dimension 0
There are 2 independent parts, one for each index of `groups`. A program takes and returns all parts, laid end to end along the dimension named above; an argument that names none is the same for every part. Nothing has to cross between parts.
Inputs may be any that keep to these rules, and one draw needn't show every extreme that they name: `send_nodes`: for every link the first send_count slots hold distinct owned nodes; later slots are padding. `send_count`: links go only to partitions of dom index d - 1, d or d + 1 and never to the sender itself or past the ends of dom; some link is full with 256 slots. `connect`: entries from 4096 on name ghost slots that are live slots of their owner's link. `live_blocks`: live blocks fill a device's slots from its first one; some device has 8. `ref_stiff`: Symmetric.
All inputs are finite; a program needn't handle non-finite values.
Results may differ from a plain program's by a relative error of at most 0.00005.
Values sent between devices are 32-bit elements; how exact they have to be, the bound alone decides.
No kernel may reach another device: no remote copies, remote signals or barrier semaphores. Data moves between devices by JAX's collectives and lax.ppermute only.
A program may use at most 64 MiB of HBM per device.

v0:
```python
import jax
import jax.numpy as jnp
from jax import lax
from jax.sharding import PartitionSpec as P

BLK = 128


def extended(cells, sides, width):
    for axis, dim in sides:
        count = lax.axis_size(axis)
        ends = count - 1
        head = lax.slice_in_dim(cells, 0, width, axis=dim)
        tail = lax.slice_in_dim(cells, cells.shape[dim] - width, cells.shape[dim], axis=dim)
        cells = jnp.concatenate(
            [
                lax.ppermute(tail, axis, [(i, (i + 1) % count) for i in range(ends)]),
                cells,
                lax.ppermute(head, axis, [((i + 1) % count, i) for i in range(ends)]),
            ],
            axis=dim,
        )
    return cells


def on_device(
    background,
    obs_weight,
    connect,
    live_blocks,
    elem_scale,
    reg_weight,
    iterate,
    residual,
    direction,
    send_nodes,
    send_count,
    ref_stiff,
):
    owned_nodes = background.shape[1]
    sub_count = lax.axis_size("sub")
    link_slots = send_nodes.shape[3]
    element_count = connect.shape[1]
    ghost_slots = 3 * sub_count * link_slots
    targets = send_nodes[0].reshape(-1)
    open_slot = (
        jnp.arange(link_slots, dtype=jnp.int32)[None, None, :] < send_count[0][:, :, None]
    ).astype(jnp.float32)

    def fetch_ghosts(values):
        outbound = values[:, targets].reshape(3, 3, sub_count, link_slots) * open_slot[None]
        mixed = lax.all_to_all(outbound, "sub", split_axis=2, concat_axis=2, tiled=True)
        rimmed = extended(mixed, (("dom", 1),), 1)
        arrived = rimmed[:, 0::2]
        return jnp.concatenate([values, arrived.reshape(3, ghost_slots)], axis=1)

    element = jnp.arange(element_count, dtype=jnp.int32)
    live_mask = (element < BLK * live_blocks[0]).astype(jnp.float32)
    search = live_mask * direction
    remain = live_mask * residual
    guess = live_mask * iterate
    flat_connect = connect.reshape(-1)
    state_full = fetch_ghosts(background)
    element_state = state_full[:, connect].reshape(30, element_count)
    coupled = (live_mask * elem_scale)[None, :] * jnp.dot(
        ref_stiff, element_state, precision=lax.Precision.HIGHEST
    )
    terms = (search[None, :] * coupled).reshape(3, -1)
    accumulated = (
        jnp.zeros((3, owned_nodes + ghost_slots), jnp.float32).at[:, flat_connect].add(terms)
    )
    accumulated = lax.psum(accumulated, "field")
    returning = accumulated[:, owned_nodes:].reshape(3, 3, sub_count, link_slots)
    rimmed = extended(returning, (("dom", 1),), 1)
    landed = lax.all_to_all(rimmed[:, 0::2], "sub", split_axis=2, concat_axis=2, tiled=True)
    landed = (landed * open_slot[None]).reshape(3, -1)
    assembled = accumulated[:, :owned_nodes] + jnp.zeros((3, owned_nodes), jnp.float32).at[
        :, targets
    ].add(landed)
    weighted = obs_weight[None, :] * assembled
    weighted_full = fetch_ghosts(weighted)
    pulled = weighted_full[:, connect].reshape(30, element_count)
    hess_search = jnp.sum(coupled * pulled, axis=0) + reg_weight * search
    squared_before, curvature_sum, cross_term, image_square = lax.psum(
        (
            jnp.sum(remain * remain),
            jnp.sum(search * hess_search),
            jnp.sum(remain * hess_search),
            jnp.sum(hess_search * hess_search),
        ),
        ("dom", "sub", "field"),
    )
    step_length = squared_before / curvature_sum
    iterate_next = guess + step_length * search
    residual_next = remain - step_length * hess_search
    squared_after = (
        squared_before - 2.0 * step_length * cross_term + step_length * step_length * image_square
    )
    direction_next = residual_next + squared_after / squared_before * search
    return (iterate_next, residual_next, direction_next)


def solution(mesh):
    placed = (
        P(None, ("groups", "dom", "sub")),
        P(("groups", "dom", "sub")),
        P(None, ("groups", "dom", "sub", "field")),
        P(("groups", "dom", "sub", "field")),
        P(("groups", "dom", "sub", "field")),
        P(("groups", "dom", "sub", "field")),
        P(("groups", "dom", "sub", "field")),
        P(("groups", "dom", "sub", "field")),
        P(("groups", "dom", "sub", "field")),
        P(("groups", "dom", "sub"), None, None, None),
        P(("groups", "dom", "sub"), None, None),
        P(),
    )
    return jax.shard_map(
        on_device,
        mesh=mesh,
        in_specs=placed,
        out_specs=(
            P(("groups", "dom", "sub", "field")),
            P(("groups", "dom", "sub", "field")),
            P(("groups", "dom", "sub", "field")),
        ),
        check_vma=False,
    )
```

profile of v0, /device:TPU:0, one launch (start us, length us, event | category | flops | bytes accessed | tf_op | source)
XLA Modules:
  0.0 283.6 jit_solution(14023031561616133790)
XLA Ops:
  7.2 0.0 copy-start
  7.2 0.0 copy-start.2
  7.2 0.8 reshape_squeeze.3
  8.0 0.8 fusion.4
  8.8 1.5 copy.66
  10.3 2.6 gather_fusion
  12.9 0.3 copy.67
  13.2 0.6 broadcast_multiply_fusion.4
  13.8 4.2 %all-to-all-start = ((f32[3,3,2,256]{3,1,0,2:T(4,128)}), f32[3,3,2,256]{3,1,0,2:T(4,128)S(1)}, u32[]{:S(2)}, u32[]{:S(2)}) async-start(f32[3,3,2,256]{3,1,0,2:T(4,128)} %broadcast_multiply_fusion.4), calls=%async_computation | async-start | bytes 49152 | tf_op jit(solution)/shard_map/all_to_all | solution.py:52
  18.9 3.1 %all-to-all-done = f32[3,3,2,256]{3,1,0,2:T(4,128)S(1)} async-done(((f32[3,3,2,256]{3,1,0,2:T(4,128)}), f32[3,3,2,256]{3,1,0,2:T(4,128)S(1)}, u32[]{:S(2)}, u32[]{:S(2)}) %all-to-all-start) | async-done | bytes 18464 | tf_op jit(solution)/shard_map/all_to_all | solution.py:52
  22.0 4.0 %collective-permute-start = (f32[3,1,2,256]{3,1,0,2:T(1,128)S(1)}, f32[3,1,2,256]{3,1,0,2:T(1,128)S(1)}, u32[]{:S(2)}, u32[]{:S(2)}) collective-permute-start(f32[3,1,2,256]{3,1,0,2:T(1,128)S(1)} %get-tuple-element.18), channel_id=1, source_target_pairs={{0,4},{4,8},{8,12},{1,5},{5,9},{9,13},{2,6},{6,10},{10,14},{3,7},{... | collective-permute-start | bytes 18440 | tf_op jit(solution)/shard_map/ppermute | solution.py:17
  25.9 1.3 collective-permute-start.1
  27.3 4.1 %collective-permute-done.1 = f32[3,1,2,256]{3,1,0,2:T(1,128)S(1)} collective-permute-done((f32[3,1,2,256]{3,1,0,2:T(1,128)S(1)}, f32[3,1,2,256]{3,1,0,2:T(1,128)S(1)}, u32[]{:S(2)}, u32[]{:S(2)}) %collective-permute-start.1) | collective-permute-done | bytes 6176 | tf_op jit(solution)/shard_map/ppermute | solution.py:19
  31.6 0.8 copy.71
  32.4 34.2 %gather_fusion.1 = f32[10240,3]{1,0:T(8,128)} fusion(f32[3,5632]{0,1:T(8,128)S(1)} %copy.71, s32[10240]{0:T(1024)S(1)} %broadcast_clamp_fusion), kind=kCustom, calls=%fused_computation.1 | custom fusion | bytes 286720 | tf_op jit(solution)/shard_map/gather | solution.py:64
  66.7 4.2 %copy.72 = f32[10,1024,3]{1,0,2:T(8,128)S(1)} copy(f32[10,1024,3]{2,1,0:T(8,128)} %bitcast.28) | data formatting | bytes 245760 | tf_op jit(solution)/shard_map/gather | solution.py:64
  70.9 0.3 broadcast_multiply_fusion.1
  71.2 0.1 reshape.145
  71.3 3.1 %copy.73 = f32[3,10240]{0,1:T(8,128)} copy(f32[3,10240]{1,0:T(4,128)S(1)} %reshape.145) | data formatting | bytes 245760 | tf_op jit(solution)/shard_map/reshape | solution.py:68
  74.4 51.9 %scatter_custom_fusion = f32[3,5632]{0,1:T(8,128)} fusion(s32[10240]{0:T(1024)S(1)} %bitcast.38, f32[3,10240]{0,1:T(8,128)} %copy.73, f32[]{:T(128)} %constant.7.clone.1), kind=kCustom, calls=%fused_computation.6 | custom fusion | flops 30720 | bytes 190468 | tf_op jit(solution)/shard_map/scatter-add | solution.py:70
  126.3 0.0 all-reduce.3.cloned.1.call-update
  126.3 22.3 %all-reduce.3.cloned.1.call-done = f32[3,5632]{0,1:T(8,128)} async-done(((f32[3,5632]{0,1:T(8,128)}), f32[3,5632]{0,1:T(8,128)}) %all-reduce.3.cloned.1.call-update) | async-done | bytes 67600 | tf_op jit(solution)/shard_map/psum | solution.py:72
  148.5 1.2 slice.55
  149.7 0.3 copy.74
  150.1 3.8 %collective-permute-start.2 = (f32[3,1,2,256]{3,1,0,2:T(1,128)S(1)}, f32[3,1,2,256]{3,1,0,2:T(1,128)S(1)}, u32[]{:S(2)}, u32[]{:S(2)}) collective-permute-start(f32[3,1,2,256]{3,1,0,2:T(1,128)S(1)} %get-tuple-element.16), channel_id=1, source_target_pairs={{0,4},{4,8},{8,12},{1,5},{5,9},{9,13},{2,6},{6,10},{10,14},{3,7},{... | collective-permute-start | bytes 18440 | tf_op jit(solution)/shard_map/ppermute | solution.py:17
  153.9 1.3 collective-permute-start.3
  155.2 0.0 collective-permute-done.2
  155.2 4.2 %collective-permute-done.3 = f32[3,1,2,256]{3,1,0,2:T(1,128)S(1)} collective-permute-done((f32[3,1,2,256]{3,1,0,2:T(1,128)S(1)}, f32[3,1,2,256]{3,1,0,2:T(1,128)S(1)}, u32[]{:S(2)}, u32[]{:S(2)}) %collective-permute-start.3) | collective-permute-done | bytes 6176 | tf_op jit(solution)/shard_map/ppermute | solution.py:19
  159.5 0.7 slice.40
  160.1 3.2 %all-to-all-start.1 = ((f32[3,3,2,256]{3,1,0,2:T(4,128)}), f32[3,3,2,256]{3,1,0,2:T(4,128)S(1)}, u32[]{:S(2)}, u32[]{:S(2)}) async-start(f32[3,3,2,256]{3,1,0,2:T(4,128)} %slice.40), calls=%async_computation.1 | async-start | bytes 49152 | tf_op jit(solution)/shard_map/all_to_all | solution.py:75
  163.4 3.9 %all-to-all-done.1 = f32[3,3,2,256]{3,1,0,2:T(4,128)S(1)} async-done(((f32[3,3,2,256]{3,1,0,2:T(4,128)}), f32[3,3,2,256]{3,1,0,2:T(4,128)S(1)}, u32[]{:S(2)}, u32[]{:S(2)}) %all-to-all-start.1) | async-done | bytes 18464 | tf_op jit(solution)/shard_map/all_to_all | solution.py:75
  167.3 0.3 copy.78
  167.6 9.5 %scatter_fusion = f32[3,4096]{0,1:T(8,128)S(1)} fusion(f32[3,4096]{0,1:T(8,128)S(1)} %slice-done, s32[1536]{0:T(1024)S(1)} %fusion.5, f32[1536,3]{1,0:T(8,128)S(1)} %copy.78), kind=kCustom, calls=%fused_computation.5 | custom fusion | flops 4608 | bytes 61440 | tf_op jit(solution)/shard_map/scatter-add | solution.py:79
  177.2 1.9 broadcast_multiply_fusion
  179.1 4.3 %gather_fusion.2 = f32[1536,3]{1,0:T(8,128)S(1)} fusion(f32[3,4096]{0,1:T(8,128)} %broadcast_multiply_fusion, s32[2048]{0:T(1024)S(1)} %pad_clamp_fusion), kind=kCustom, calls=%fused_computation.2 | custom fusion | bytes 43008 | tf_op jit(solution)/shard_map/gather | solution.py:51
  183.4 0.3 copy.79
  183.8 6.3 %all_to_all.15 = f32[3,3,2,256]{3,1,0,2:T(4,128)S(1)} all-to-all(f32[3,3,2,256]{3,1,0,2:T(4,128)S(1)} %broadcast_multiply_fusion.2), channel_id=1, replica_groups=mesh['groups'=2,'dom'=4,'sub'=2,'field'=2] {'sub'}, dimensions={2} | all-to-all | bytes 36864 | tf_op jit(solution)/shard_map/all_to_all | solution.py:52
  190.1 3.4 %collective-permute-start.4 = (f32[3,1,2,256]{3,1,0,2:T(1,128)S(1)}, f32[3,1,2,256]{3,1,0,2:T(1,128)S(1)}, u32[]{:S(2)}, u32[]{:S(2)}) collective-permute-start(f32[3,1,2,256]{3,1,0,2:T(1,128)S(1)} %get-tuple-element.14), channel_id=1, source_target_pairs={{0,4},{4,8},{8,12},{1,5},{5,9},{9,13},{2,6},{6,10},{10,14},{3,7},{... | collective-permute-start | bytes 18440 | tf_op jit(solution)/shard_map/ppermute | solution.py:17
  193.5 1.3 collective-permute-start.5
  194.8 0.0 collective-permute-done.4
  194.8 4.2 %collective-permute-done.5 = f32[3,1,2,256]{3,1,0,2:T(1,128)S(1)} collective-permute-done((f32[3,1,2,256]{3,1,0,2:T(1,128)S(1)}, f32[3,1,2,256]{3,1,0,2:T(1,128)S(1)}, u32[]{:S(2)}, u32[]{:S(2)}) %collective-permute-start.5) | collective-permute-done | bytes 6176 | tf_op jit(solution)/shard_map/ppermute | solution.py:19
  199.0 0.3 copy.83
  199.3 1.7 pad_maximum_fusion
  201.1 36.1 %gather_fusion.3 = f32[10240,3]{1,0:T(8,128)} fusion(f32[3,5632]{0,1:T(8,128)} %pad_maximum_fusion, s32[10240]{0:T(1024)S(1)} %broadcast_clamp_fusion), kind=kCustom, calls=%fused_computation.3 | custom fusion | bytes 286720 | tf_op jit(solution)/shard_map/gather | solution.py:82
  237.1 4.2 %copy.84 = f32[10,1024,3]{1,0,2:T(8,128)S(1)} copy(f32[10,1024,3]{2,1,0:T(8,128)} %bitcast.27) | data formatting | bytes 245760 | tf_op jit(solution)/shard_map/gather | solution.py:82
  241.4 0.6 multiply_reduce_fusion.1
  242.1 30.1 %all-reduce = (f32[]{:T(128)}, f32[]{:T(128)}, f32[]{:T(128)}, f32[]{:T(128)}) all-reduce(f32[]{:T(128)} %get-tuple-element.5, f32[]{:T(128)} %get-tuple-element.6, f32[]{:T(128)} %get-tuple-element.4, f32[]{:T(128)} %get-tuple-element.3), channel_id=1, replica_groups=mesh['groups'=2,'dom'=4,'sub'=2,'field'=2] {'dom','sub','field'}, use_global_device_ids=true, to_apply=%region_1.0 | all-reduce | flops 4 | bytes 32 | tf_op jit(solution)/shard_map/psum | solution.py:84
  276.2 0.6 multiply_add_fusion
  (53 shorter events, 0.5 us)
Async XLA Ops:
  7.2 63.7 %copy-start = (f32[30,30]{1,0:T(8,128)S(1)}, f32[30,30]{1,0:T(8,128)}, u32[]{:S(2)}) copy-start(f32[30,30]{1,0:T(8,128)} %param.23) | copy-start | bytes 10804
  7.2 24.4 %copy-start.2 = (f32[3,4096]{1,0:T(4,128)S(1)}, f32[3,4096]{1,0:T(4,128)}, u32[]{:S(2)}) copy-start(f32[3,4096]{1,0:T(4,128)} %param.12) | copy-start | bytes 147460
  7.2 10.9 %copy-start.3 = (s32[10,1024]{1,0:T(8,128)S(1)}, s32[10,1024]{1,0:T(8,128)}, u32[]{:S(2)}) copy-start(s32[10,1024]{1,0:T(8,128)} %param.14) | copy-start | bytes 122884
  7.2 20.0 %copy-start.7 = (f32[1024]{0:T(1024)S(1)}, f32[1024]{0:T(1024)}, u32[]{:S(2)}) copy-start(f32[1024]{0:T(1024)} %param.20) | copy-start | bytes 12292
  7.2 20.0 %copy-start.6 = (f32[1024]{0:T(1024)S(1)}, f32[1024]{0:T(1024)}, u32[]{:S(2)}) copy-start(f32[1024]{0:T(1024)} %param.16) | copy-start | bytes 12292
  13.8 8.1 %all-to-all-start = ((f32[3,3,2,256]{3,1,0,2:T(4,128)}), f32[3,3,2,256]{3,1,0,2:T(4,128)S(1)}, u32[]{:S(2)}, u32[]{:S(2)}) async-start(f32[3,3,2,256]{3,1,0,2:T(4,128)} %broadcast_multiply_fusion.4), calls=%async_computation | async-start | bytes 49152 | tf_op jit(solution)/shard_map/all_to_all | solution.py:52
  18.1 130.5 %all-reduce.3.cloned.1.call-start = ((), (), s32[]{:S(2)}) async-start(), calls=%async_computation.3 | async-start | bytes 5767168 | tf_op jit(solution)/shard_map/psum | solution.py:72
  22.0 5.3 %collective-permute-start = (f32[3,1,2,256]{3,1,0,2:T(1,128)S(1)}, f32[3,1,2,256]{3,1,0,2:T(1,128)S(1)}, u32[]{:S(2)}, u32[]{:S(2)}) collective-permute-start(f32[3,1,2,256]{3,1,0,2:T(1,128)S(1)} %get-tuple-element.18), channel_id=1, source_target_pairs={{0,4},{4,8},{8,12},{1,5},{5,9},{9,13},{2,6},{6,10},{10,14},{3,7},{... | collective-permute-start | bytes 18440 | tf_op jit(solution)/shard_map/ppermute | solution.py:17
  25.9 5.5 %collective-permute-start.1 = (f32[3,1,2,256]{3,1,0,2:T(1,128)S(1)}, f32[3,1,2,256]{3,1,0,2:T(1,128)S(1)}, u32[]{:S(2)}, u32[]{:S(2)}) collective-permute-start(f32[3,1,2,256]{3,1,0,2:T(1,128)S(1)} %get-tuple-element.19), channel_id=1, source_target_pairs={{4,0},{8,4},{12,8},{5,1},{9,5},{13,9},{6,2},{10,6},{14,10},{7,3},{... | collective-permute-start | bytes 18440 | tf_op jit(solution)/shard_map/ppermute | solution.py:19
  150.1 17.5 %slice-start = ((f32[3,5632]{0,1:T(8,128)}), f32[3,4096]{0,1:T(8,128)S(1)}, s32[]{:S(2)}) async-start(f32[3,5632]{0,1:T(8,128)} %all-reduce.3.cloned.1.call-done), calls=%async_computation.4 | async-start | bytes 4194304 | tf_op jit(solution)/shard_map/slice | solution.py:77
  150.1 27.0 %copy-start.4 = (f32[4096]{0:T(1024)S(1)}, f32[4096]{0:T(1024)}, u32[]{:S(2)}) copy-start(f32[4096]{0:T(1024)} %param.13) | copy-start | bytes 49156
  150.1 5.1 %collective-permute-start.2 = (f32[3,1,2,256]{3,1,0,2:T(1,128)S(1)}, f32[3,1,2,256]{3,1,0,2:T(1,128)S(1)}, u32[]{:S(2)}, u32[]{:S(2)}) collective-permute-start(f32[3,1,2,256]{3,1,0,2:T(1,128)S(1)} %get-tuple-element.16), channel_id=1, source_target_pairs={{0,4},{4,8},{8,12},{1,5},{5,9},{9,13},{2,6},{6,10},{10,14},{3,7},{... | collective-permute-start | bytes 18440 | tf_op jit(solution)/shard_map/ppermute | solution.py:17
  153.9 5.5 %collective-permute-start.3 = (f32[3,1,2,256]{3,1,0,2:T(1,128)S(1)}, f32[3,1,2,256]{3,1,0,2:T(1,128)S(1)}, u32[]{:S(2)}, u32[]{:S(2)}) collective-permute-start(f32[3,1,2,256]{3,1,0,2:T(1,128)S(1)} %get-tuple-element.17), channel_id=1, source_target_pairs={{4,0},{8,4},{12,8},{5,1},{9,5},{13,9},{6,2},{10,6},{14,10},{7,3},{... | collective-permute-start | bytes 18440 | tf_op jit(solution)/shard_map/ppermute | solution.py:19
  160.1 7.1 %all-to-all-start.1 = ((f32[3,3,2,256]{3,1,0,2:T(4,128)}), f32[3,3,2,256]{3,1,0,2:T(4,128)S(1)}, u32[]{:S(2)}, u32[]{:S(2)}) async-start(f32[3,3,2,256]{3,1,0,2:T(4,128)} %slice.40), calls=%async_computation.1 | async-start | bytes 49152 | tf_op jit(solution)/shard_map/all_to_all | solution.py:75
  179.1 20.2 %copy-start.1 = (f32[3,4096]{0,1:T(8,128)S(1)}, f32[3,4096]{0,1:T(8,128)}, u32[]{:S(2)}) copy-start(f32[3,4096]{0,1:T(8,128)} %broadcast_multiply_fusion) | copy-start | bytes 147460
  190.1 4.7 %collective-permute-start.4 = (f32[3,1,2,256]{3,1,0,2:T(1,128)S(1)}, f32[3,1,2,256]{3,1,0,2:T(1,128)S(1)}, u32[]{:S(2)}, u32[]{:S(2)}) collective-permute-start(f32[3,1,2,256]{3,1,0,2:T(1,128)S(1)} %get-tuple-element.14), channel_id=1, source_target_pairs={{0,4},{4,8},{8,12},{1,5},{5,9},{9,13},{2,6},{6,10},{10,14},{3,7},{... | collective-permute-start | bytes 18440 | tf_op jit(solution)/shard_map/ppermute | solution.py:17
  193.5 5.5 %collective-permute-start.5 = (f32[3,1,2,256]{3,1,0,2:T(1,128)S(1)}, f32[3,1,2,256]{3,1,0,2:T(1,128)S(1)}, u32[]{:S(2)}, u32[]{:S(2)}) collective-permute-start(f32[3,1,2,256]{3,1,0,2:T(1,128)S(1)} %get-tuple-element.15), channel_id=1, source_target_pairs={{4,0},{8,4},{12,8},{5,1},{9,5},{13,9},{6,2},{10,6},{14,10},{7,3},{... | collective-permute-start | bytes 18440 | tf_op jit(solution)/shard_map/ppermute | solution.py:19
  237.1 4.3 %copy-start.5 = (f32[1024]{0:T(1024)S(1)}, f32[1024]{0:T(1024)}, u32[]{:S(2)}) copy-start(f32[1024]{0:T(1024)} %param.19) | copy-start | bytes 12292
  237.1 4.3 %copy-start.8 = (f32[1024]{0:T(1024)S(1)}, f32[1024]{0:T(1024)}, u32[]{:S(2)}) copy-start(f32[1024]{0:T(1024)} %param.17) | copy-start | bytes 12292
  237.1 39.0 %copy-start.9 = (f32[1024]{0:T(1024)S(1)}, f32[1024]{0:T(1024)}, u32[]{:S(2)}) copy-start(f32[1024]{0:T(1024)} %param.18) | copy-start | bytes 12292
Sparse Core Ops, SparseCore 0:
  126.4 22.0 all-reduce.2
where the time goes:
time: 284 us
  local copies, waits for them, and re-layouts  95.7 us (34%)
  other arithmetic  67.9 us (24%)
  waiting for transfers between devices  41.8 us (15%)
  blocking collectives  36.4 us (13%)
  starting transfers between devices  22.5 us (8%)
  between operations  19.1 us (7%)
    scatter-add x1, other arithmetic, on_device(): jnp.zeros((3, owned_nodes + ghost_slots), jnp.float32).at[:, flat_connect]  51.9 us
    gather x2, local copies, waits for them, and re-layouts, on_device(): pulled = weighted_full[:, connect].reshape(30, element_count)  40.3 us
    gather x2, local copies, waits for them, and re-layouts, on_device(): element_state = state_full[:, connect].reshape(30, element_count)  38.4 us
    psum x1, blocking collectives, on_device(): lax.psum((jnp.sum(remain * remain), jnp.sum(search * hess_search), jnp.su...  30.1 us
    psum x1, waiting for transfers between devices, on_device(): accumulated = lax.psum(accumulated, 'field')  22.3 us
    ppermute x3, waiting for transfers between devices, extended(): lax.ppermute(head, axis, [((i + 1) % count, i) for i in range(ends)])  12.5 us
    ppermute x3, starting transfers between devices, extended(): lax.ppermute(tail, axis, [(i, (i + 1) % count) for i in range(ends)])  11.1 us
    scatter-add x1, other arithmetic, on_device(): assembled = accumulated[:, :owned_nodes] + jnp.zeros((3, owned_nodes), jn...  9.52 us
  transfers between devices with their start and end apart: 9, of which 6 were waited for; matrix products, arithmetic and copies ran while one was open for 0% of the time, Pallas kernels for 0%

commit v1 on v0

v1 whole, which is shorter than its diff:
```python
import functools

import jax
import jax.numpy as jnp
from jax import lax
from jax.experimental import pallas as pl
from jax.experimental.pallas import tpu as pltpu
from jax.sharding import PartitionSpec as P

BLK = 128
LANES = 128
SUBS = 8
PARTS = 3

VMEM = pl.BlockSpec(memory_space=pltpu.VMEM)
SMEM = pl.BlockSpec(memory_space=pltpu.SMEM)


def up_to(count, step):
    return -(-count // step) * step


def lookup(table, rows, index, unroll):
    high = [i // LANES for i in index]
    low = [i % LANES for i in index]
    zero = jnp.zeros(index[0].shape, jnp.float32)

    def step(row, found):
        lines = [
            jnp.broadcast_to(table[c, pl.ds(row, 1), :], zero.shape) for c in range(3)
        ]
        out = []
        for i in range(len(index)):
            here = high[i] == row
            for c in range(3):
                value = jnp.take_along_axis(
                    lines[c], low[i], axis=1, mode="promise_in_bounds"
                )
                out.append(jnp.where(here, value, found[3 * i + c]))
        return tuple(out)

    found = lax.fori_loop(0, rows, step, (zero,) * (3 * len(index)), unroll=unroll)
    return [found[3 * i : 3 * i + 3] for i in range(len(index))]


def split_parts(value):
    pieces = []
    for _ in range(PARTS - 1):
        piece = value.astype(jnp.bfloat16).astype(jnp.float32)
        pieces.append(piece)
        value = value - piece
    pieces.append(value.astype(jnp.bfloat16).astype(jnp.float32))
    return pieces


def one_hot_pair(lines, index, rows, width):
    high = index // width
    low = index % width
    row = lax.broadcasted_iota(jnp.int32, (rows, LANES), 0)
    here = row == jnp.broadcast_to(high, (rows, LANES))
    left = jnp.concatenate(
        [jnp.where(here, jnp.broadcast_to(x, (rows, LANES)), 0.0) for x in lines], axis=0
    ).astype(jnp.bfloat16)
    spot = lax.broadcasted_iota(jnp.int32, (width, LANES), 0)
    right = jnp.where(
        spot == jnp.broadcast_to(low, (width, LANES)), 1.0, 0.0
    ).astype(jnp.bfloat16)
    return left, right


def contract(left, right):
    return lax.dot_general(
        left, right, (((1,), (1,)), ((), ())), preferred_element_type=jnp.float32
    )


def link_rows(sub_count, halves):
    return [
        (o, t, h, (o * sub_count + t) * halves + h)
        for o in range(3)
        for t in range(sub_count)
        for h in range(halves)
    ]


def load_links(nodes, index, sub_count, halves):
    for o, t, h, row in link_rows(sub_count, halves):
        index[row : row + 1, :] = nodes[0, o, t : t + 1, h * LANES : (h + 1) * LANES]
    used = 3 * sub_count * halves
    if index.shape[0] > used:
        index[used:, :] = jnp.zeros((index.shape[0] - used, LANES), jnp.int32)


def open_lanes(counts, o, t, h):
    lane = lax.broadcasted_iota(jnp.int32, (1, LANES), 1) + h * LANES
    return lane < counts[0, o, t]


def send_links(table, table_rows, counts, index, values, out, dom_count, sub_count, halves):
    tiles = index.shape[0] // SUBS
    found = lookup(
        table, table_rows, [index[i * SUBS : (i + 1) * SUBS, :] for i in range(tiles)], 4
    )
    for i in range(tiles):
        for c in range(3):
            values[c, i * SUBS : (i + 1) * SUBS, :] = found[i][c]

    def clear(p, carry):
        out[p] = jnp.zeros(out.shape[1:], jnp.float32)
        return carry

    lax.fori_loop(0, out.shape[0], clear, 0)
    dom = lax.axis_index("dom")
    for o in range(3):
        place = dom + o - 1

        @pl.when((place >= 0) & (place < dom_count))
        def _():
            for t in range(sub_count):
                for h in range(halves):
                    row = (o * sub_count + t) * halves + h
                    here = open_lanes(counts, o, t, h)
                    for c in range(3):
                        line = values[c, row : row + 1, :]
                        out[place * sub_count + t, c * halves + h : c * halves + h + 1, :] = (
                            jnp.where(here, line, 0.0)
                        )


def fill_ghosts(table, first, arrived, dom_count, sub_count, halves):
    dom = lax.axis_index("dom")
    for o in range(3):
        place = dom + o - 1
        inside = (place >= 0) & (place < dom_count)
        safe = jnp.clip(place, 0, dom_count - 1)
        for t in range(sub_count):
            chunk = arrived[safe * sub_count + t]
            chunk = jnp.where(inside, chunk, 0.0)
            for c in range(3):
                row = first + (o * sub_count + t) * halves
                table[c, row : row + halves, :] = chunk[c * halves : (c + 1) * halves, :]


def start_kernel(dims, counts, nodes, background, out, index, values, table):
    dom_count, sub_count, halves = dims
    rows = background.shape[1] // LANES
    for c in range(3):
        for r in range(rows):
            table[c, r : r + 1, :] = background[c : c + 1, r * LANES : (r + 1) * LANES]
    load_links(nodes, index, sub_count, halves)
    send_links(table, rows, counts, index, values, out, dom_count, sub_count, halves)


def forward_kernel(
    dims,
    live,
    stiff,
    background,
    arrived,
    connect,
    scale,
    direction,
    coupled,
    owned,
    outbound,
    table,
    index,
    state,
    pieces,
    left,
    right,
    total,
):
    dom_count, sub_count, halves = dims
    width = halves * LANES
    rows = background.shape[1] // LANES
    owned_high = background.shape[1] // width
    ghost_rows = 3 * sub_count * halves
    for c in range(3):
        for r in range(rows):
            table[c, r : r + 1, :] = background[c : c + 1, r * LANES : (r + 1) * LANES]
    fill_ghosts(table, rows, arrived, dom_count, sub_count, halves)
    for k in range(10):
        for b in range(SUBS):
            index[k, b : b + 1, :] = connect[k : k + 1, b * LANES : (b + 1) * LANES]
    found = lookup(table, rows + ghost_rows, [index[k] for k in range(10)], 2)
    for c in range(3):
        for k in range(10):
            state[c * 10 + k] = found[k][c]
    element = (
        lax.broadcasted_iota(jnp.int32, (SUBS, LANES), 0) * LANES
        + lax.broadcasted_iota(jnp.int32, (SUBS, LANES), 1)
    )
    mask = (element < BLK * live[0]).astype(jnp.float32)
    search = mask * direction[...]
    factor = mask * scale[...]
    for c in range(3):
        sums = [None] * 10
        for j in range(30):
            value = state[j]
            for k in range(10):
                term = stiff[c * 10 + k, j] * value
                sums[k] = term if j == 0 else sums[k] + term
        for k in range(10):
            result = factor * sums[k]
            coupled[c * 10 + k] = result
            for part, piece in enumerate(split_parts(search * result)):
                pieces[part * 3 + c, k] = piece

    high_rows = left.shape[0] // (3 * PARTS)

    def scatter(k, carry):
        for b in range(SUBS):
            lines = [pieces[q, k, b : b + 1, :] for q in range(3 * PARTS)]
            a, m = one_hot_pair(lines, index[k, b : b + 1, :], high_rows, width)
            left[:, b * LANES : (b + 1) * LANES] = a
            right[:, b * LANES : (b + 1) * LANES] = m
        total[...] += contract(left[...], right[...])
        return carry

    total[...] = jnp.zeros_like(total)
    lax.fori_loop(0, 10, scatter, 0)

    def summed(c, low, count):
        value = None
        for part in reversed(range(PARTS)):
            base = (part * 3 + c) * high_rows
            piece = total[base + low : base + low + count, :]
            value = piece if value is None else value + piece
        return value

    def clear(p, carry):
        outbound[p] = jnp.zeros(outbound.shape[1:], jnp.float32)
        return carry

    lax.fori_loop(0, outbound.shape[0], clear, 0)
    dom = lax.axis_index("dom")
    fields = outbound.shape[0] // (dom_count * sub_count)
    ghost = [None] * 3
    for c in range(3):
        owned[c] = summed(c, 0, owned_high)
        ghost[c] = summed(c, owned_high, 3 * sub_count)
    for o in range(3):
        place = dom + o - 1

        @pl.when((place >= 0) & (place < dom_count))
        def _():
            for t in range(sub_count):
                for c in range(3):
                    for h in range(halves):
                        line = ghost[c][
                            o * sub_count + t : o * sub_count + t + 1,
                            h * LANES : (h + 1) * LANES,
                        ]
                        spot = c * halves + h
                        for f in range(fields):
                            outbound[
                                (place * sub_count + t) * fields + f, spot : spot + 1, :
                            ] = line


def owner_kernel(
    dims,
    counts,
    nodes,
    mine,
    other,
    arrived,
    obs,
    weighted,
    out,
    index,
    values,
    left,
    right,
):
    dom_count, sub_count, halves = dims
    width = halves * LANES
    fields = arrived.shape[0] // (dom_count * sub_count)
    owned_high = mine.shape[1]
    load_links(nodes, index, sub_count, halves)
    dom = lax.axis_index("dom")
    for o in range(3):
        place = dom + o - 1
        inside = (place >= 0) & (place < dom_count)
        safe = jnp.clip(place, 0, dom_count - 1)
        for t in range(sub_count):
            chunk = arrived[(safe * sub_count + t) * fields]
            for f in range(1, fields):
                chunk = chunk + arrived[(safe * sub_count + t) * fields + f]
            chunk = jnp.where(inside, chunk, 0.0)
            split = split_parts(chunk)
            for h in range(halves):
                row = (o * sub_count + t) * halves + h
                here = open_lanes(counts, o, t, h)
                lines = [
                    jnp.where(here, split[part][c * halves + h : c * halves + h + 1, :], 0.0)
                    for part in range(PARTS)
                    for c in range(3)
                ]
                a, m = one_hot_pair(lines, index[row : row + 1, :], owned_high, width)
                left[:, row * LANES : (row + 1) * LANES] = a
                right[:, row * LANES : (row + 1) * LANES] = m
    total = contract(left[...], right[...])
    for c in range(3):
        value = mine[c] + other[c]
        landed = None
        for part in reversed(range(PARTS)):
            base = (part * 3 + c) * owned_high
            piece = total[base : base + owned_high, :]
            landed = piece if landed is None else landed + piece
        value = value + landed
        for h in range(halves):
            weight = obs[pl.ds(h, owned_high, stride=halves), :]
            weighted[c, pl.ds(h, owned_high, stride=halves), :] = (
                weight * value[:, h * LANES : (h + 1) * LANES]
            )
    rows = owned_high * halves
    send_links(weighted, rows, counts, index, values, out, dom_count, sub_count, halves)


def adjoint_kernel(
    dims,
    live,
    weighted,
    arrived,
    connect,
    coupled,
    direction,
    residual,
    reg,
    hess,
    sums,
    table,
    index,
):
    dom_count, sub_count, halves = dims
    rows = weighted.shape[1]
    table[:, 0:rows, :] = weighted[...]
    fill_ghosts(table, rows, arrived, dom_count, sub_count, halves)
    for k in range(10):
        for b in range(SUBS):
            index[k, b : b + 1, :] = connect[k : k + 1, b * LANES : (b + 1) * LANES]
    found = lookup(
        table, rows + 3 * sub_count * halves, [index[k] for k in range(10)], 2
    )
    element = (
        lax.broadcasted_iota(jnp.int32, (SUBS, LANES), 0) * LANES
        + lax.broadcasted_iota(jnp.int32, (SUBS, LANES), 1)
    )
    mask = (element < BLK * live[0]).astype(jnp.float32)
    search = mask * direction[...]
    remain = mask * residual[...]
    image = None
    for c in range(3):
        for k in range(10):
            term = coupled[c * 10 + k] * found[k][c]
            image = term if image is None else image + term
    image = image + reg[...] * search
    hess[...] = image
    for i, product in enumerate(
        (remain * remain, search * image, remain * image, image * image)
    ):
        line = jnp.sum(product, axis=0, keepdims=True)
        sums[:, i * LANES : (i + 1) * LANES] = jnp.broadcast_to(
            line, (sums.shape[0], LANES)
        )


def update_kernel(
    live, sums, hess, iterate, residual, direction, iterate_out, residual_out, direction_out
):
    totals = []
    for i in range(4):
        line = jnp.sum(sums[:, i * LANES : (i + 1) * LANES], axis=0, keepdims=True)
        line = jnp.sum(line, axis=1, keepdims=True)
        totals.append(jnp.broadcast_to(line, (SUBS, LANES)))
    squared_before, curvature_sum, cross_term, image_square = totals
    element = (
        lax.broadcasted_iota(jnp.int32, (SUBS, LANES), 0) * LANES
        + lax.broadcasted_iota(jnp.int32, (SUBS, LANES), 1)
    )
    mask = (element < BLK * live[0]).astype(jnp.float32)
    search = mask * direction[...]
    step_length = squared_before / curvature_sum
    squared_after = (
        squared_before
        - 2.0 * step_length * cross_term
        + step_length * step_length * image_square
    )
    residual_next = mask * residual[...] - step_length * hess[...]
    iterate_out[...] = mask * iterate[...] + step_length * search
    residual_out[...] = residual_next
    direction_out[...] = residual_next + squared_after / squared_before * search


def on_device(
    background,
    obs_weight,
    connect,
    live_blocks,
    elem_scale,
    reg_weight,
    iterate,
    residual,
    direction,
    send_nodes,
    send_count,
    ref_stiff,
):
    f32, i32, bf16 = jnp.float32, jnp.int32, jnp.bfloat16
    shape = jax.ShapeDtypeStruct
    dom_count = lax.axis_size("dom")
    sub_count = lax.axis_size("sub")
    field_count = lax.axis_size("field")
    owned_nodes = background.shape[1]
    link_slots = send_nodes.shape[3]
    halves = link_slots // LANES
    width = link_slots
    owned_high = owned_nodes // width
    owned_rows = owned_nodes // LANES
    ghost_rows = 3 * sub_count * halves
    table_rows = owned_rows + ghost_rows
    partitions = dom_count * sub_count
    devices = partitions * field_count
    chunk = up_to(3 * halves, SUBS)
    link_tiles = up_to(ghost_rows, SUBS)
    high_rows = up_to(owned_high + 3 * sub_count, SUBS)
    dims = (dom_count, sub_count, halves)
    tiled = lambda x: x.reshape(-1, LANES)
    scale, reg, guess, remain, search = map(
        tiled, (elem_scale, reg_weight, iterate, residual, direction)
    )
    obs = tiled(obs_weight)
    links = ("dom", "sub")
    cores = ("dom", "sub", "field")

    outbound = pl.pallas_call(
        functools.partial(start_kernel, dims),
        out_shape=shape((partitions, chunk, LANES), f32),
        in_specs=[SMEM, VMEM, VMEM],
        out_specs=VMEM,
        scratch_shapes=[
            pltpu.VMEM((link_tiles, LANES), i32),
            pltpu.VMEM((3, link_tiles, LANES), f32),
            pltpu.VMEM((3, owned_rows, LANES), f32),
        ],
    )(send_count, send_nodes, background)
    arrived = lax.all_to_all(outbound, links, 0, 0, tiled=True)

    coupled, owned, outbound = pl.pallas_call(
        functools.partial(forward_kernel, dims),
        out_shape=(
            shape((30, SUBS, LANES), f32),
            shape((3, owned_high, width), f32),
            shape((devices, chunk, LANES), f32),
        ),
        in_specs=[SMEM, SMEM] + [VMEM] * 5,
        out_specs=(VMEM,) * 3,
        scratch_shapes=[
            pltpu.VMEM((3, table_rows, LANES), f32),
            pltpu.VMEM((10, SUBS, LANES), i32),
            pltpu.VMEM((30, SUBS, LANES), f32),
            pltpu.VMEM((3 * PARTS, 10, SUBS, LANES), f32),
            pltpu.VMEM((3 * PARTS * high_rows, SUBS * LANES), bf16),
            pltpu.VMEM((width, SUBS * LANES), bf16),
            pltpu.VMEM((3 * PARTS * high_rows, width), f32),
        ],
    )(live_blocks, ref_stiff, background, arrived, connect, scale, search)
    swapped = lax.ppermute(
        owned, "field", [(i, (i + 1) % field_count) for i in range(field_count)]
    )
    arrived = lax.all_to_all(outbound, cores, 0, 0, tiled=True)

    weighted, outbound = pl.pallas_call(
        functools.partial(owner_kernel, dims),
        out_shape=(
            shape((3, owned_rows, LANES), f32),
            shape((partitions, chunk, LANES), f32),
        ),
        in_specs=[SMEM] + [VMEM] * 5,
        out_specs=(VMEM,) * 2,
        scratch_shapes=[
            pltpu.VMEM((link_tiles, LANES), i32),
            pltpu.VMEM((3, link_tiles, LANES), f32),
            pltpu.VMEM((3 * PARTS * owned_high, ghost_rows * LANES), bf16),
            pltpu.VMEM((width, ghost_rows * LANES), bf16),
        ],
    )(send_count, send_nodes, owned, swapped, arrived, obs)
    arrived = lax.all_to_all(outbound, links, 0, 0, tiled=True)

    hess, sums = pl.pallas_call(
        functools.partial(adjoint_kernel, dims),
        out_shape=(shape((SUBS, LANES), f32), shape((devices, 4 * LANES), f32)),
        in_specs=[SMEM] + [VMEM] * 7,
        out_specs=(VMEM,) * 2,
        scratch_shapes=[
            pltpu.VMEM((3, table_rows, LANES), f32),
            pltpu.VMEM((10, SUBS, LANES), i32),
        ],
    )(live_blocks, weighted, arrived, connect, coupled, search, remain, reg)
    sums = lax.all_to_all(sums, cores, 0, 0, tiled=True)

    results = pl.pallas_call(
        update_kernel,
        out_shape=(shape((SUBS, LANES), f32),) * 3,
        in_specs=[SMEM] + [VMEM] * 5,
        out_specs=(VMEM,) * 3,
    )(live_blocks, sums, hess, guess, remain, search)
    return tuple(x.reshape(-1) for x in results)


def solution(mesh):
    placed = (
        P(None, ("groups", "dom", "sub")),
        P(("groups", "dom", "sub")),
        P(None, ("groups", "dom", "sub", "field")),
        P(("groups", "dom", "sub", "field")),
        P(("groups", "dom", "sub", "field")),
        P(("groups", "dom", "sub", "field")),
        P(("groups", "dom", "sub", "field")),
        P(("groups", "dom", "sub", "field")),
        P(("groups", "dom", "sub", "field")),
        P(("groups", "dom", "sub"), None, None, None),
        P(("groups", "dom", "sub"), None, None),
        P(),
    )
    return jax.shard_map(
        on_device,
        mesh=mesh,
        in_specs=placed,
        out_specs=(
            P(("groups", "dom", "sub", "field")),
            P(("groups", "dom", "sub", "field")),
            P(("groups", "dom", "sub", "field")),
        ),
        check_vma=False,
    )
```

time: 284 us -> 74.1 us (0.26)
  local copies, waits for them, and re-layouts: 95.7 us -> 3.98 us
  other arithmetic: 67.9 us -> 0 us
  waiting for transfers between devices: 41.8 us -> 12.5 us
  Pallas kernels: 0 us -> 24.4 us
  between operations: 19.1 us -> 1.31 us
  blocking collectives: 36.4 us -> 19.8 us
  starting transfers between devices: 22.5 us -> 11.3 us
    gather x6 -> x0, local copies, waits for them, and re-layouts: 85.7 us -> none  [the longest x2 40.3 us: on_device(): pulled = weighted_full[:, connect].reshape(30, element_count)]
    scatter-add x2 -> x0, other arithmetic: 61.4 us -> none  [the longest x1 51.9 us: on_device(): jnp.zeros((3, owned_nodes + ghost_slots), jnp.float32).at[:, flat_connect]]
    psum x1 -> x0, blocking collectives: 30.1 us -> none  [on_device(): lax.psum((jnp.sum(remain * remain), jnp.sum(search * hess_search), jnp.su...]
    pallas_call x0 -> x5, Pallas kernels: none -> 24.4 us  [the longest x1 11.4 us: on_device(): pl.pallas_call(functools.partial(forward_kernel, dims), out_shape=(shape(...]
    psum x1 -> x0, waiting for transfers between devices: 22.3 us -> none  [on_device(): accumulated = lax.psum(accumulated, 'field')]
    ppermute x6 -> x1, starting transfers between devices: 15 us -> 0.35 us  [on_device(): lax.ppermute(owned, 'field', [(i, (i + 1) % field_count) for i in range(f...]
    all_to_all x1 -> x2, blocking collectives: 6.25 us -> 19.8 us  [the longest x1 10.6 us: on_device(): arrived = lax.all_to_all(outbound, links, 0, 0, tiled=True)]
    ppermute x6 -> x1, waiting for transfers between devices: 12.6 us -> 0.94 us  [on_device(): lax.ppermute(owned, 'field', [(i, (i + 1) % field_count) for i in range(f...]
  transfers between devices with their start and end apart: 9 -> 3, of which waited for: 6 -> 3; matrix products, arithmetic and copies ran while one was open for 0% -> 0% of each run, Pallas kernels for 0% -> 0%
where the time goes in v1:
time: 74.1 us; the launch traced here: 73.3 us
  Pallas kernels  24.4 us (33%)
  blocking collectives  19.8 us (27%)
  waiting for transfers between devices  12.5 us (17%)
  starting transfers between devices  11.3 us (15%)
  local copies, waits for them, and re-layouts  3.98 us (5%)
  between operations  1.31 us (2%)
    pallas_call x1, Pallas kernels, on_device(): pl.pallas_call(functools.partial(forward_kernel, dims), out_shape=(shape(...  11.4 us
    all_to_all x1, blocking collectives, on_device(): arrived = lax.all_to_all(outbound, links, 0, 0, tiled=True)  10.6 us
    all_to_all x1, blocking collectives, on_device(): sums = lax.all_to_all(sums, cores, 0, 0, tiled=True)  9.2 us
    all_to_all x1, starting transfers between devices, on_device(): arrived = lax.all_to_all(outbound, links, 0, 0, tiled=True)  7.28 us
    all_to_all x1, waiting for transfers between devices, on_device(): arrived = lax.all_to_all(outbound, links, 0, 0, tiled=True)  6.03 us
    pallas_call x1, Pallas kernels, on_device(): pl.pallas_call(functools.partial(adjoint_kernel, dims), out_shape=(shape(...  5.98 us
    all_to_all x1, waiting for transfers between devices, on_device(): arrived = lax.all_to_all(outbound, cores, 0, 0, tiled=True)  5.55 us
    all_to_all x1, starting transfers between devices, on_device(): arrived = lax.all_to_all(outbound, cores, 0, 0, tiled=True)  3.62 us
  transfers between devices with their start and end apart: 3, of which 3 were waited for; matrix products, arithmetic and copies ran while one was open for 0% of the time, Pallas kernels for 0%

profile of v1, /device:TPU:0, one launch (start us, length us, event | category | flops | bytes accessed | tf_op | source)
XLA Modules:
  0.0 73.3 jit_solution(18035346334453118001)
XLA Ops:
  0.6 1.3 %copy.18.counts = s32[1,3,2]{2,1,0:T(4,128)} copy(s32[1,3,2]{1,2,0:T(2,128)} %param.22) | data formatting | bytes 48 | tf_op args[10]
  2.0 2.5 %shard_map.139 = f32[8,8,128]{2,1,0:T(8,128)} custom-call(s32[1,3,2]{2,1,0:T(4,128)} %copy.18.counts, s32[1,3,2,256]{3,2,1,0:T(2,128)} %nodes.3, f32[3,4096]{1,0:T(4,128)} %background.3), custom_call_target="tpu_custom_call" | custom-call | tf_op jit(solution)/shard_map/pallas_call | solution.py:438
  4.5 7.3 %all-to-all-start = ((f32[8,8,128]{2,1,0:T(8,128)}), f32[8,8,128]{2,1,0:T(8,128)S(1)}, u32[]{:S(2)}, u32[]{:S(2)}) async-start(f32[8,8,128]{2,1,0:T(8,128)} %shard_map.139), calls=%async_computation | async-start | bytes 65536 | tf_op jit(solution)/shard_map/all_to_all | solution.py:449
  12.4 6.0 %all-to-all-done.arrived = f32[8,8,128]{2,1,0:T(8,128)S(1)} async-done(((f32[8,8,128]{2,1,0:T(8,128)}), f32[8,8,128]{2,1,0:T(8,128)S(1)}, u32[]{:S(2)}, u32[]{:S(2)}) %all-to-all-start) | async-done | bytes 32800 | tf_op jit(solution)/shard_map/all_to_all | solution.py:449
  18.5 0.0 copy-start.1
  18.5 0.6 copy-done.1
  19.1 11.4 %shard_map.140 = (f32[30,8,128]{2,1,0:T(8,128)}, f32[3,16,256]{2,1,0:T(8,128)}, f32[16,8,128]{2,1,0:T(8,128)}) custom-call(s32[1]{0:T(128)S(6)} %copy.23.live, f32[30,30]{1,0:T(8,128)} %stiff.1, f32[3,4096]{1,0:T(4,128)} %background.3, f32[8,8,128]{2,1,0:T(8,128)} %copy-done.1, s32[10,1024]{1,0:T(8,128)} %connect.3, f32[8,128]{1,0:T(8,128)} %bitcast.22, ...), custom_call_target="tpu_custom_call" | custom-call | tf_op jit(solution)/shard_map/pallas_call | solution.py:451
  30.5 0.0 copy-start.2
  30.5 3.6 %all-to-all-start.1 = ((f32[16,8,128]{2,1,0:T(8,128)}), f32[16,8,128]{2,1,0:T(8,128)S(1)}, u32[]{:S(2)}, u32[]{:S(2)}) async-start(f32[16,8,128]{2,1,0:T(8,128)} %get-tuple-element.14), calls=%async_computation.1 | async-start | bytes 131072 | tf_op jit(solution)/shard_map/all_to_all | solution.py:473
  34.1 0.0 copy-done.2
  34.1 0.4 collective-permute-start
  34.4 0.9 %collective-permute-done.other = f32[3,16,256]{2,1,0:T(8,128)S(1)} collective-permute-done((f32[3,16,256]{2,1,0:T(8,128)S(1)}, f32[3,16,256]{2,1,0:T(8,128)S(1)}, u32[]{:S(2)}, u32[]{:S(2)}) %collective-permute-start) | collective-permute-done | bytes 49184 | tf_op jit(solution)/shard_map/ppermute | solution.py:470
  35.4 0.0 copy-start.3
  35.4 5.5 %all-to-all-done.1.arrived = f32[16,8,128]{2,1,0:T(8,128)S(1)} async-done(((f32[16,8,128]{2,1,0:T(8,128)}), f32[16,8,128]{2,1,0:T(8,128)S(1)}, u32[]{:S(2)}, u32[]{:S(2)}) %all-to-all-start.1) | async-done | bytes 65568 | tf_op jit(solution)/shard_map/all_to_all | solution.py:473
  40.9 0.0 copy-start
  40.9 0.0 copy-done.3
  40.9 0.6 copy-done
  41.6 3.1 %shard_map.141 = (f32[3,32,128]{2,1,0:T(8,128)}, f32[8,8,128]{2,1,0:T(8,128)}) custom-call(s32[1,3,2]{2,1,0:T(4,128)} %copy.18.counts, s32[1,3,2,256]{3,2,1,0:T(2,128)} %nodes.3, f32[3,16,256]{2,1,0:T(8,128)} %get-tuple-element.13.mine, f32[3,16,256]{2,1,0:T(8,128)} %copy-done.3, f32[16,8,128]{2,1,0:T(8,128)} %copy-done, f32[32,128]{1,0:T(8,128)} %bitcast.20), custom_call_target="tpu_custom_call" | custom-call | tf_op jit(solution)/shard_map/pallas_call | solution.py:475
  44.6 10.6 %all_to_all.26.arrived = f32[8,8,128]{2,1,0:T(8,128)} all-to-all(f32[8,8,128]{2,1,0:T(8,128)} %get-tuple-element.16), channel_id=1, replica_groups=mesh['groups'=2,'dom'=4,'sub'=2,'field'=2] {'dom','sub'}, dimensions={0} | all-to-all | bytes 65536 | tf_op jit(solution)/shard_map/all_to_all | solution.py:490
  55.3 6.0 %shard_map.142 = (f32[8,128]{1,0:T(8,128)}, f32[16,512]{1,0:T(8,128)}) custom-call(s32[1]{0:T(128)S(6)} %copy.23.live, f32[3,32,128]{2,1,0:T(8,128)} %get-tuple-element.15.weighted, f32[8,8,128]{2,1,0:T(8,128)} %all_to_all.26.arrived, s32[10,1024]{1,0:T(8,128)} %connect.3, f32[30,8,128]{2,1,0:T(8,128)} %get-tuple-element.17.coupled, f32[8,128]{1,0:T(8,128)} %bitcast.15, ...), custom_call_target="tpu_custom_call" | custom-call | tf_op jit(solution)/shard_map/pallas_call | solution.py:492
  61.2 0.8 %copy.19 = f32[16,1,512]{2,1,0:T(1,128)S(1)} copy(f32[16,1,512]{2,0,1:T(8,128)} %bitcast.17) | data formatting | bytes 65536 | tf_op jit(solution)/shard_map/all_to_all | solution.py:502
  62.0 9.2 %all_to_all.27 = f32[16,1,512]{2,1,0:T(1,128)S(1)} all-to-all(f32[16,1,512]{2,1,0:T(1,128)S(1)} %copy.19), channel_id=1, replica_groups=mesh['groups'=2,'dom'=4,'sub'=2,'field'=2] {'dom','sub','field'}, dimensions={0} | all-to-all | bytes 65536 | tf_op jit(solution)/shard_map/all_to_all | solution.py:502
  71.2 0.6 copy.22
  71.9 1.5 %shard_map.143 = (f32[8,128]{1,0:T(8,128)}, f32[8,128]{1,0:T(8,128)}, f32[8,128]{1,0:T(8,128)}) custom-call(s32[1]{0:T(128)S(6)} %copy.23.live, f32[16,512]{1,0:T(8,128)} %bitcast.13, f32[8,128]{1,0:T(8,128)} %get-tuple-element.19.hess, f32[8,128]{1,0:T(8,128)} %bitcast.23, f32[8,128]{1,0:T(8,128)} %bitcast.19, f32[8,128]{1,0:T(8,128)} %bitcast.16), custom_call_target="tpu_custom_call" | custom-call | tf_op jit(solution)/shard_map/pallas_call | solution.py:504
Async XLA Ops:
  4.5 14.0 %all-to-all-start = ((f32[8,8,128]{2,1,0:T(8,128)}), f32[8,8,128]{2,1,0:T(8,128)S(1)}, u32[]{:S(2)}, u32[]{:S(2)}) async-start(f32[8,8,128]{2,1,0:T(8,128)} %shard_map.139), calls=%async_computation | async-start | bytes 65536 | tf_op jit(solution)/shard_map/all_to_all | solution.py:449
  18.5 0.6 copy-start.1
  30.5 3.6 %copy-start.2 = (f32[3,16,256]{2,1,0:T(8,128)S(1)}, f32[3,16,256]{2,1,0:T(8,128)}, u32[]{:S(2)}) copy-start(f32[3,16,256]{2,1,0:T(8,128)} %get-tuple-element.13.mine) | copy-start | bytes 147460
  30.5 10.5 %all-to-all-start.1 = ((f32[16,8,128]{2,1,0:T(8,128)}), f32[16,8,128]{2,1,0:T(8,128)S(1)}, u32[]{:S(2)}, u32[]{:S(2)}) async-start(f32[16,8,128]{2,1,0:T(8,128)} %get-tuple-element.14), calls=%async_computation.1 | async-start | bytes 131072 | tf_op jit(solution)/shard_map/all_to_all | solution.py:473
  34.1 1.3 %collective-permute-start = (f32[3,16,256]{2,1,0:T(8,128)S(1)}, f32[3,16,256]{2,1,0:T(8,128)S(1)}, u32[]{:S(2)}, u32[]{:S(2)}) collective-permute-start(f32[3,16,256]{2,1,0:T(8,128)S(1)} %copy-done.2), channel_id=1, source_target_pairs={{0,1},{1,0},{2,3},{3,2},{4,5},{5,4},{6,7},{7,6},{8,9},{9,8},{10,11... | collective-permute-start | bytes 147464 | tf_op jit(solution)/shard_map/ppermute | solution.py:470
  35.4 5.6 %copy-start.3 = (f32[3,16,256]{2,1,0:T(8,128)}, f32[3,16,256]{2,1,0:T(8,128)S(1)}, u32[]{:S(2)}) copy-start(f32[3,16,256]{2,1,0:T(8,128)S(1)} %collective-permute-done.other) | copy-start | bytes 147460
  40.9 0.6 copy-start

commit v2 on v1

--- a/solution.py
+++ b/solution.py
@@ -11,36 +11,52 @@
 LANES = 128
 SUBS = 8
 PARTS = 3
+GROUP = 1
+UNROLL = 10
+SUMS = 4
+LANE_BITS = 7
 
 VMEM = pl.BlockSpec(memory_space=pltpu.VMEM)
 SMEM = pl.BlockSpec(memory_space=pltpu.SMEM)
+PARAMS = pltpu.CompilerParams(vmem_limit_bytes=16 * 2**20)
 
 
 def up_to(count, step):
     return -(-count // step) * step
 
 
-def lookup(table, rows, index, unroll):
-    high = [i // LANES for i in index]
-    low = [i % LANES for i in index]
-    zero = jnp.zeros(index[0].shape, jnp.float32)
-
-    def step(row, found):
-        lines = [
-            jnp.broadcast_to(table[c, pl.ds(row, 1), :], zero.shape) for c in range(3)
-        ]
-        out = []
-        for i in range(len(index)):
-            here = high[i] == row
+def lookup(table, rows, index, store):
+    def pair(first, count):
+        entries = [index[first + i] for i in range(count)]
+        high = [lax.shift_right_logical(x, LANE_BITS) for x in entries]
+        low = [x & (LANES - 1) for x in entries]
+        found = [[None] * 3 for _ in entries]
+        for row in range(rows):
+            lines = [
+                jnp.broadcast_to(table[c, row : row + 1, :], (SUBS, LANES))
+                for c in range(3)
+            ]
+            for i in range(count):
+                here = high[i] == row
+                for c in range(3):
+                    value = jnp.take_along_axis(
+                        lines[c], low[i], axis=1, mode="promise_in_bounds"
+                    )
+                    found[i][c] = jnp.where(
+                        here, value, 0.0 if row == 0 else found[i][c]
+                    )
+        for i in range(count):
             for c in range(3):
-                value = jnp.take_along_axis(
-                    lines[c], low[i], axis=1, mode="promise_in_bounds"
-                )
-                out.append(jnp.where(here, value, found[3 * i + c]))
-        return tuple(out)
-
-    found = lax.fori_loop(0, rows, step, (zero,) * (3 * len(index)), unroll=unroll)
-    return [found[3 * i : 3 * i + 3] for i in range(len(index))]
+                store(first + i, c, found[i][c])
+
+    def step(p, carry):
+        pair(p * GROUP, GROUP)
+        return carry
+
+    tiles = index.shape[0]
+    lax.fori_loop(0, tiles // GROUP, step, 0)
+    if tiles % GROUP:
+        pair(tiles // GROUP * GROUP, tiles % GROUP)
 
 
 def split_parts(value):
@@ -53,18 +69,32 @@
     return pieces
 
 
-def one_hot_pair(lines, index, rows, width):
+def spread(line, rows):
+    return jnp.broadcast_to(line, (rows, LANES)).astype(jnp.bfloat16)
+
+
+def row_numbers(rows):
+    row = lax.broadcasted_iota(jnp.int32, (rows, LANES), 0)
+    return row.astype(jnp.float32).astype(jnp.bfloat16)
+
+
+def one_hot_pair(lines, index, owned_high, ghost_high, width):
+    none = jnp.zeros((), jnp.bfloat16)
+    unit = jnp.ones((), jnp.bfloat16)
     high = index // width
-    low = index % width
-    row = lax.broadcasted_iota(jnp.int32, (rows, LANES), 0)
-    here = row == jnp.broadcast_to(high, (rows, LANES))
-    left = jnp.concatenate(
-        [jnp.where(here, jnp.broadcast_to(x, (rows, LANES)), 0.0) for x in lines], axis=0
-    ).astype(jnp.bfloat16)
-    spot = lax.broadcasted_iota(jnp.int32, (width, LANES), 0)
-    right = jnp.where(
-        spot == jnp.broadcast_to(low, (width, LANES)), 1.0, 0.0
-    ).astype(jnp.bfloat16)
+    low = (index & (width - 1)).astype(jnp.float32)
+    here = row_numbers(owned_high) == spread(high.astype(jnp.float32), owned_high)
+    blocks = [jnp.where(here, spread(x, owned_high), none) for x in lines]
+    if ghost_high:
+        row = lax.broadcasted_iota(jnp.int32, (ghost_high, LANES), 0) + owned_high
+        here = row == jnp.broadcast_to(high, row.shape)
+        rest = [jnp.where(here, jnp.broadcast_to(x, row.shape), 0.0) for x in lines]
+        spare = up_to(len(lines) * ghost_high, 16) - len(lines) * ghost_high
+        if spare:
+            rest.append(jnp.zeros((spare, LANES), jnp.float32))
+        blocks.append(jnp.concatenate(rest, axis=0).astype(jnp.bfloat16))
+    left = jnp.concatenate(blocks, axis=0)
+    right = jnp.where(row_numbers(width) == spread(low, width), unit, none)
     return left, right
 
 
@@ -85,25 +115,23 @@
 
 def load_links(nodes, index, sub_count, halves):
     for o, t, h, row in link_rows(sub_count, halves):
-        index[row : row + 1, :] = nodes[0, o, t : t + 1, h * LANES : (h + 1) * LANES]
-    used = 3 * sub_count * halves
-    if index.shape[0] > used:
-        index[used:, :] = jnp.zeros((index.shape[0] - used, LANES), jnp.int32)
+        index[row // SUBS, row % SUBS : row % SUBS + 1, :] = nodes[
+            0, o, t : t + 1, h * LANES : (h + 1) * LANES
+        ]
+    for row in range(3 * sub_count * halves, index.shape[0] * SUBS):
+        index[row // SUBS, row % SUBS : row % SUBS + 1, :] = jnp.zeros((1, LANES), jnp.int32)
 
 
 def open_lanes(counts, o, t, h):
     lane = lax.broadcasted_iota(jnp.int32, (1, LANES), 1) + h * LANES
-    return lane < counts[0, o, t]
+    return lane < counts[0, t, o]
 
 
 def send_links(table, table_rows, counts, index, values, out, dom_count, sub_count, halves):
-    tiles = index.shape[0] // SUBS
-    found = lookup(
-        table, table_rows, [index[i * SUBS : (i + 1) * SUBS, :] for i in range(tiles)], 4
-    )
-    for i in range(tiles):
-        for c in range(3):
-            values[c, i * SUBS : (i + 1) * SUBS, :] = found[i][c]
+    def store(tile, c, value):
+        values[c, tile] = value
+
+    lookup(table, table_rows, index, store)
 
     def clear(p, carry):
         out[p] = jnp.zeros(out.shape[1:], jnp.float32)
@@ -121,7 +149,7 @@
                     row = (o * sub_count + t) * halves + h
                     here = open_lanes(counts, o, t, h)
                     for c in range(3):
-                        line = values[c, row : row + 1, :]
+                        line = values[c, row // SUBS, row % SUBS : row % SUBS + 1, :]
                         out[place * sub_count + t, c * halves + h : c * halves + h + 1, :] = (
                             jnp.where(here, line, 0.0)
                         )
@@ -160,15 +188,17 @@
     connect,
     scale,
     direction,
+    residual,
+    iterate,
+    reg,
     coupled,
+    vectors,
     owned,
     outbound,
     table,
     index,
     state,
     pieces,
-    left,
-    right,
     total,
 ):
     dom_count, sub_count, halves = dims
@@ -183,10 +213,11 @@
     for k in range(10):
         for b in range(SUBS):
             index[k, b : b + 1, :] = connect[k : k + 1, b * LANES : (b + 1) * LANES]
-    found = lookup(table, rows + ghost_rows, [index[k] for k in range(10)], 2)
-    for c in range(3):
-        for k in range(10):
-            state[c * 10 + k] = found[k][c]
+
+    def keep(k, c, value):
+        state[c * 10 + k] = value
+
+    lookup(table, rows + ghost_rows, index, keep)
     element = (
         lax.broadcasted_iota(jnp.int32, (SUBS, LANES), 0) * LANES
         + lax.broadcasted_iota(jnp.int32, (SUBS, LANES), 1)
@@ -194,6 +225,10 @@
     mask = (element < BLK * live[0]).astype(jnp.float32)
     search = mask * direction[...]
     factor = mask * scale[...]
+    vectors[0] = search
+    vectors[1] = mask * residual[...]
+    vectors[2] = mask * iterate[...]
+    vectors[3] = reg[...] * search
     for c in range(3):
         sums = [None] * 10
         for j in range(30):
@@ -207,25 +242,31 @@
             for part, piece in enumerate(split_parts(search * result)):
                 pieces[part * 3 + c, k] = piece
 
-    high_rows = left.shape[0] // (3 * PARTS)
+    lines_count = 3 * PARTS
+    ghost_high = up_to(3 * sub_count, SUBS)
+    total[...] = jnp.zeros_like(total)
 
     def scatter(k, carry):
-        for b in range(SUBS):
-            lines = [pieces[q, k, b : b + 1, :] for q in range(3 * PARTS)]
-            a, m = one_hot_pair(lines, index[k, b : b + 1, :], high_rows, width)
-            left[:, b * LANES : (b + 1) * LANES] = a
-            right[:, b * LANES : (b + 1) * LANES] = m
-        total[...] += contract(left[...], right[...])
+        pairs = [
+            one_hot_pair(
+                [pieces[q, k, b : b + 1, :] for q in range(lines_count)],
+                index[k, b : b + 1, :],
+                owned_high,
+                ghost_high,
+                width,
+            )
+            for b in range(SUBS)
+        ]
+        total[...] += contract(*[jnp.concatenate(x, axis=1) for x in zip(*pairs)])
         return carry
 
-    total[...] = jnp.zeros_like(total)
-    lax.fori_loop(0, 10, scatter, 0)
-
-    def summed(c, low, count):
+    lax.fori_loop(0, 10, scatter, 0, unroll=UNROLL)
+
+    def summed(first, step, count):
         value = None
         for part in reversed(range(PARTS)):
-            base = (part * 3 + c) * high_rows
-            piece = total[base + low : base + low + count, :]
+            base = first + part * 3 * step
+            piece = total[base : base + count, :]
             value = piece if value is None else value + piece
         return value
 
@@ -238,8 +279,10 @@
     fields = outbound.shape[0] // (dom_count * sub_count)
     ghost = [None] * 3
     for c in range(3):
-        owned[c] = summed(c, 0, owned_high)
-        ghost[c] = summed(c, owned_high, 3 * sub_count)
+        owned[c] = summed(c * owned_high, owned_high, owned_high)
+        ghost[c] = summed(
+            lines_count * owned_high + c * ghost_high, ghost_high, 3 * sub_count
+        )
     for o in range(3):
         place = dom + o - 1
 
@@ -271,8 +314,6 @@
     out,
     index,
     values,
-    left,
-    right,
 ):
     dom_count, sub_count, halves = dims
     width = halves * LANES
@@ -280,6 +321,7 @@
     owned_high = mine.shape[1]
     load_links(nodes, index, sub_count, halves)
     dom = lax.axis_index("dom")
+    pairs = []
     for o in range(3):
         place = dom + o - 1
         inside = (place >= 0) & (place < dom_count)
@@ -298,10 +340,9 @@
                     for part in range(PARTS)
                     for c in range(3)
                 ]
-                a, m = one_hot_pair(lines, index[row : row + 1, :], owned_high, width)
-                left[:, row * LANES : (row + 1) * LANES] = a
-                right[:, row * LANES : (row + 1) * LANES] = m
-    total = contract(left[...], right[...])
+                a, m = one_hot_pair(lines, index[row // SUBS, row % SUBS : row % SUBS + 1, :], owned_high, 0, width)
+                pairs.append((a, m))
+    total = contract(*[jnp.concatenate(x, axis=1) for x in zip(*pairs)])
     for c in range(3):
         value = mine[c] + other[c]
         landed = None
@@ -320,19 +361,7 @@
 
 
 def adjoint_kernel(
-    dims,
-    live,
-    weighted,
-    arrived,
-    connect,
-    coupled,
-    direction,
-    residual,
-    reg,
-    hess,
-    sums,
-    table,
-    index,
+    dims, weighted, arrived, connect, coupled, vectors, hess, sums, table, index, pulled
 ):
     dom_count, sub_count, halves = dims
     rows = weighted.shape[1]
@@ -341,55 +370,45 @@
     for k in range(10):
         for b in range(SUBS):
             index[k, b : b + 1, :] = connect[k : k + 1, b * LANES : (b + 1) * LANES]
-    found = lookup(
-        table, rows + 3 * sub_count * halves, [index[k] for k in range(10)], 2
-    )
-    element = (
-        lax.broadcasted_iota(jnp.int32, (SUBS, LANES), 0) * LANES
-        + lax.broadcasted_iota(jnp.int32, (SUBS, LANES), 1)
-    )
-    mask = (element < BLK * live[0]).astype(jnp.float32)
-    search = mask * direction[...]
-    remain = mask * residual[...]
+
+    def keep(k, c, value):
+        pulled[k, c] = value
+
+    lookup(table, rows + 3 * sub_count * halves, index, keep)
+    search, remain = vectors[0], vectors[1]
     image = None
     for c in range(3):
         for k in range(10):
-            term = coupled[c * 10 + k] * found[k][c]
+            term = coupled[c * 10 + k] * pulled[k, c]
             image = term if image is None else image + term
-    image = image + reg[...] * search
+    image = image + vectors[3]
     hess[...] = image
     for i, product in enumerate(
         (remain * remain, search * image, remain * image, image * image)
     ):
         line = jnp.sum(product, axis=0, keepdims=True)
-        sums[:, i * LANES : (i + 1) * LANES] = jnp.broadcast_to(
-            line, (sums.shape[0], LANES)
-        )
-
-
-def update_kernel(
-    live, sums, hess, iterate, residual, direction, iterate_out, residual_out, direction_out
-):
+        for p in range(sums.shape[0]):
+            sums[p, i : i + 1, :] = line
+
+
+def update_kernel(sums, hess, vectors, iterate_out, residual_out, direction_out):
     totals = []
     for i in range(4):
-        line = jnp.sum(sums[:, i * LANES : (i + 1) * LANES], axis=0, keepdims=True)
+        line = sums[0, i : i + 1, :]
+        for p in range(1, sums.shape[0]):
+            line = line + sums[p, i : i + 1, :]
         line = jnp.sum(line, axis=1, keepdims=True)
         totals.append(jnp.broadcast_to(line, (SUBS, LANES)))
     squared_before, curvature_sum, cross_term, image_square = totals
-    element = (
-        lax.broadcasted_iota(jnp.int32, (SUBS, LANES), 0) * LANES
-        + lax.broadcasted_iota(jnp.int32, (SUBS, LANES), 1)
-    )
-    mask = (element < BLK * live[0]).astype(jnp.float32)
-    search = mask * direction[...]
+    search, remain, guess = vectors[0], vectors[1], vectors[2]
     step_length = squared_before / curvature_sum
     squared_after = (
         squared_before
         - 2.0 * step_length * cross_term
         + step_length * step_length * image_square
     )
-    residual_next = mask * residual[...] - step_length * hess[...]
-    iterate_out[...] = mask * iterate[...] + step_length * search
+    residual_next = remain - step_length * hess[...]
+    iterate_out[...] = guess + step_length * search
     residual_out[...] = residual_next
     direction_out[...] = residual_next + squared_after / squared_before * search
 
@@ -408,7 +427,7 @@
     send_count,
     ref_stiff,
 ):
-    f32, i32, bf16 = jnp.float32, jnp.int32, jnp.bfloat16
+    f32, i32 = jnp.float32, jnp.int32
     shape = jax.ShapeDtypeStruct
     dom_count = lax.axis_size("dom")
     sub_count = lax.axis_size("sub")
@@ -424,14 +443,15 @@
     partitions = dom_count * sub_count
     devices = partitions * field_count
     chunk = up_to(3 * halves, SUBS)
-    link_tiles = up_to(ghost_rows, SUBS)
-    high_rows = up_to(owned_high + 3 * sub_count, SUBS)
+    link_tiles = up_to(ghost_rows, SUBS) // SUBS
+    left_rows = 3 * PARTS * owned_high + up_to(3 * PARTS * up_to(3 * sub_count, SUBS), 16)
     dims = (dom_count, sub_count, halves)
     tiled = lambda x: x.reshape(-1, LANES)
     scale, reg, guess, remain, search = map(
         tiled, (elem_scale, reg_weight, iterate, residual, direction)
     )
     obs = tiled(obs_weight)
+    counts = jnp.swapaxes(send_count, 1, 2)
     links = ("dom", "sub")
     cores = ("dom", "sub", "field")
 
@@ -441,32 +461,43 @@
         in_specs=[SMEM, VMEM, VMEM],
         out_specs=VMEM,
         scratch_shapes=[
-            pltpu.VMEM((link_tiles, LANES), i32),
-            pltpu.VMEM((3, link_tiles, LANES), f32),
+            pltpu.VMEM((link_tiles, SUBS, LANES), i32),
+            pltpu.VMEM((3, link_tiles, SUBS, LANES), f32),
             pltpu.VMEM((3, owned_rows, LANES), f32),
         ],
-    )(send_count, send_nodes, background)
+    )(counts, send_nodes, background)
     arrived = lax.all_to_all(outbound, links, 0, 0, tiled=True)
 
-    coupled, owned, outbound = pl.pallas_call(
+    coupled, vectors, owned, outbound = pl.pallas_call(
         functools.partial(forward_kernel, dims),
+        compiler_params=PARAMS,
         out_shape=(
             shape((30, SUBS, LANES), f32),
+            shape((4, SUBS, LANES), f32),
             shape((3, owned_high, width), f32),
             shape((devices, chunk, LANES), f32),
         ),
-        in_specs=[SMEM, SMEM] + [VMEM] * 5,
-        out_specs=(VMEM,) * 3,
+        in_specs=[SMEM, SMEM] + [VMEM] * 8,
+        out_specs=(VMEM,) * 4,
         scratch_shapes=[
             pltpu.VMEM((3, table_rows, LANES), f32),
             pltpu.VMEM((10, SUBS, LANES), i32),
             pltpu.VMEM((30, SUBS, LANES), f32),
             pltpu.VMEM((3 * PARTS, 10, SUBS, LANES), f32),
-            pltpu.VMEM((3 * PARTS * high_rows, SUBS * LANES), bf16),
-            pltpu.VMEM((width, SUBS * LANES), bf16),
-            pltpu.VMEM((3 * PARTS * high_rows, width), f32),
+            pltpu.VMEM((left_rows, width), f32),
         ],
-    )(live_blocks, ref_stiff, background, arrived, connect, scale, search)
+    )(
+        live_blocks,
+        ref_stiff,
+        background,
+        arrived,
+        connect,
+        scale,
+        search,
+        remain,
+        guess,
+        reg,
+    )
     swapped = lax.ppermute(
         owned, "field", [(i, (i + 1) % field_count) for i in range(field_count)]
     )
@@ -474,6 +505,7 @@
 
     weighted, outbound = pl.pallas_call(
         functools.partial(owner_kernel, dims),
+        compiler_params=PARAMS,
         out_shape=(
             shape((3, owned_rows, LANES), f32),
             shape((partitions, chunk, LANES), f32),
@@ -481,32 +513,33 @@
         in_specs=[SMEM] + [VMEM] * 5,
         out_specs=(VMEM,) * 2,
         scratch_shapes=[
-            pltpu.VMEM((link_tiles, LANES), i32),
-            pltpu.VMEM((3, link_tiles, LANES), f32),
-            pltpu.VMEM((3 * PARTS * owned_high, ghost_rows * LANES), bf16),
-            pltpu.VMEM((width, ghost_rows * LANES), bf16),
+            pltpu.VMEM((link_tiles, SUBS, LANES), i32),
+            pltpu.VMEM((3, link_tiles, SUBS, LANES), f32),
         ],
-    )(send_count, send_nodes, owned, swapped, arrived, obs)
+    )(counts, send_nodes, owned, swapped, arrived, obs)
     arrived = lax.all_to_all(outbound, links, 0, 0, tiled=True)
 
     hess, sums = pl.pallas_call(
         functools.partial(adjoint_kernel, dims),
-        out_shape=(shape((SUBS, LANES), f32), shape((devices, 4 * LANES), f32)),
-        in_specs=[SMEM] + [VMEM] * 7,
+        compiler_params=PARAMS,
+        out_shape=(shape((SUBS, LANES), f32), shape((devices, SUMS, LANES), f32)),
+        in_specs=[VMEM] * 5,
         out_specs=(VMEM,) * 2,
         scratch_shapes=[
             pltpu.VMEM((3, table_rows, LANES), f32),
             pltpu.VMEM((10, SUBS, LANES), i32),
+            pltpu.VMEM((10, 3, SUBS, LANES), f32),
         ],
-    )(live_blocks, weighted, arrived, connect, coupled, search, remain, reg)
+    )(weighted, arrived, connect, coupled, vectors)
     sums = lax.all_to_all(sums, cores, 0, 0, tiled=True)
 
     results = pl.pallas_call(
         update_kernel,
+        compiler_params=PARAMS,
         out_shape=(shape((SUBS, LANES), f32),) * 3,
-        in_specs=[SMEM] + [VMEM] * 5,
+        in_specs=[VMEM] * 3,
         out_specs=(VMEM,) * 3,
-    )(live_blocks, sums, hess, guess, remain, search)
+    )(sums, hess, vectors)
     return tuple(x.reshape(-1) for x in results)
 
 

time: 74.1 us -> 56.5 us (0.76)
  Pallas kernels: 24.4 us -> 11.7 us
  local copies, waits for them, and re-layouts: 3.98 us -> 0.69 us
  blocking collectives: 19.8 us -> 18.3 us
    pallas_call x4, Pallas kernels: 21.9 us -> 9.76 us  [the longest x1 5.48 us: on_device(): pl.pallas_call(functools.partial(forward_kernel, dims), compiler_params=P...]
    unnamed x10 -> x22, local copies, waits for them, and re-layouts: 3.19 us -> 0.69 us
    all_to_all x1, blocking collectives: 10.6 us -> 9.06 us  [on_device(): arrived = lax.all_to_all(outbound, links, 0, 0, tiled=True)]
    all_to_all x1 -> x0, local copies, waits for them, and re-layouts: 0.79 us -> none  [on_device(): sums = lax.all_to_all(sums, cores, 0, 0, tiled=True)]
where the time goes in v2:
time: 56.5 us; the launch traced here: 56 us
  blocking collectives  18.3 us (32%)
  waiting for transfers between devices  12.5 us (22%)
  Pallas kernels  11.7 us (21%)
  starting transfers between devices  11.4 us (20%)
  between operations  1.38 us (2%)
  local copies, waits for them, and re-layouts  0.69 us (1%)
    all_to_all x1, blocking collectives, on_device(): sums = lax.all_to_all(sums, cores, 0, 0, tiled=True)  9.2 us
    all_to_all x1, blocking collectives, on_device(): arrived = lax.all_to_all(outbound, links, 0, 0, tiled=True)  9.06 us
    all_to_all x1, starting transfers between devices, on_device(): arrived = lax.all_to_all(outbound, links, 0, 0, tiled=True)  7.42 us
    all_to_all x1, waiting for transfers between devices, on_device(): arrived = lax.all_to_all(outbound, links, 0, 0, tiled=True)  6.03 us
    all_to_all x1, waiting for transfers between devices, on_device(): arrived = lax.all_to_all(outbound, cores, 0, 0, tiled=True)  5.55 us
    pallas_call x1, Pallas kernels, on_device(): pl.pallas_call(functools.partial(forward_kernel, dims), compiler_params=P...  5.48 us
    all_to_all x1, starting transfers between devices, on_device(): arrived = lax.all_to_all(outbound, cores, 0, 0, tiled=True)  3.62 us
    pallas_call x1, Pallas kernels, on_device(): pl.pallas_call(functools.partial(adjoint_kernel, dims), compiler_params=P...  2.21 us
  transfers between devices with their start and end apart: 3, of which 3 were waited for; matrix products, arithmetic and copies ran while one was open for 0% of the time, Pallas kernels for 0%

profile of v2, /device:TPU:0, one launch (start us, length us, event | category | flops | bytes accessed | tf_op | source)
XLA Modules:
  0.0 56.0 jit_solution(72626304688967475)
XLA Ops:
  0.6 0.0 copy-start
  0.6 0.0 copy-start.1
  0.6 2.0 %shard_map.139 = f32[8,8,128]{2,1,0:T(8,128)} custom-call(s32[1,2,3]{2,1,0:T(2,128)} %bitcast.11, s32[1,3,2,256]{3,2,1,0:T(2,128)} %nodes.3, f32[3,4096]{1,0:T(4,128)} %background.3), custom_call_target="tpu_custom_call" | custom-call | tf_op jit(solution)/shard_map/pallas_call | solution.py:458
  2.6 0.0 copy-start.3
  2.6 0.0 copy-start.8
  2.6 0.0 copy-start.9
  2.6 0.0 copy-start.10
  2.6 7.4 %all-to-all-start = ((f32[8,8,128]{2,1,0:T(8,128)}), f32[8,8,128]{2,1,0:T(8,128)S(1)}, u32[]{:S(2)}, u32[]{:S(2)}) async-start(f32[8,8,128]{2,1,0:T(8,128)} %shard_map.139), calls=%async_computation | async-start | bytes 65536 | tf_op jit(solution)/shard_map/all_to_all | solution.py:469
  10.7 6.0 %all-to-all-done.arrived = f32[8,8,128]{2,1,0:T(8,128)S(1)} async-done(((f32[8,8,128]{2,1,0:T(8,128)}), f32[8,8,128]{2,1,0:T(8,128)S(1)}, u32[]{:S(2)}, u32[]{:S(2)}) %all-to-all-start) | async-done | bytes 32800 | tf_op jit(solution)/shard_map/all_to_all | solution.py:469
  16.7 0.0 copy-start.7
  16.7 0.0 copy-start.6
  16.7 0.0 copy-done
  16.8 0.0 copy-done.1
  16.8 0.0 copy-done.3
  16.8 0.0 copy-done.8
  16.8 0.0 copy-done.9
  16.8 0.0 copy-done.10
  16.8 0.6 %copy-done.7 = f32[1024]{0:T(1024)S(1)} copy-done((f32[1024]{0:T(1024)S(1)}, f32[1024]{0:T(1024)}, u32[]{:S(2)}) %copy-start.7) | copy-done | bytes 4120
  17.4 0.0 copy-done.6
  17.4 5.5 %shard_map.140 = (f32[30,8,128]{2,1,0:T(8,128)S(1)}, f32[4,8,128]{2,1,0:T(8,128)S(1)}, f32[3,16,256]{2,1,0:T(8,128)S(1)}, f32[16,8,128]{2,1,0:T(8,128)}) custom-call(s32[1]{0:T(128)S(6)} %copy.15.live, f32[30,30]{1,0:T(8,128)S(1)} %copy-done.3, f32[3,4096]{1,0:T(4,128)S(1)} %copy-done, f32[8,8,128]{2,1,0:T(8,128)S(1)} %all-to-all-done.arrived, ...), custom_call_target="tpu_custom_call" | custom-call | tf_op jit(solution)/shard_map/pallas_call | solution.py:471
  22.9 0.0 copy-start.2
  22.9 0.0 copy-start.4
  22.9 3.6 %all-to-all-start.1 = ((f32[16,8,128]{2,1,0:T(8,128)}), f32[16,8,128]{2,1,0:T(8,128)S(1)}, u32[]{:S(2)}, u32[]{:S(2)}) async-start(f32[16,8,128]{2,1,0:T(8,128)} %get-tuple-element.15), calls=%async_computation.1 | async-start | bytes 131072 | tf_op jit(solution)/shard_map/all_to_all | solution.py:504
  26.6 0.0 copy-start.5
  26.6 0.4 collective-permute-start
  26.9 0.9 %collective-permute-done.other = f32[3,16,256]{2,1,0:T(8,128)S(1)} collective-permute-done((f32[3,16,256]{2,1,0:T(8,128)S(1)}, f32[3,16,256]{2,1,0:T(8,128)S(1)}, u32[]{:S(2)}, u32[]{:S(2)}) %collective-permute-start) | collective-permute-done | bytes 49184 | tf_op jit(solution)/shard_map/ppermute | solution.py:501
  27.9 5.5 %all-to-all-done.1.arrived = f32[16,8,128]{2,1,0:T(8,128)S(1)} async-done(((f32[16,8,128]{2,1,0:T(8,128)}), f32[16,8,128]{2,1,0:T(8,128)S(1)}, u32[]{:S(2)}, u32[]{:S(2)}) %all-to-all-start.1) | async-done | bytes 65568 | tf_op jit(solution)/shard_map/all_to_all | solution.py:504
  33.4 0.0 copy-done.2
  33.4 0.0 copy-done.4
  33.4 0.0 copy-done.5
  33.4 1.4 %shard_map.141 = (f32[3,32,128]{2,1,0:T(8,128)S(1)}, f32[8,8,128]{2,1,0:T(8,128)S(1)}) custom-call(s32[1,2,3]{2,1,0:T(2,128)S(1)} %bitcast.12, s32[1,3,2,256]{3,2,1,0:T(2,128)S(1)} %copy-done.2, f32[3,16,256]{2,1,0:T(8,128)S(1)} %get-tuple-element.14.mine, f32[3,16,256]{2,1,0:T(8,128)S(1)} %collective-permute-done.other, ...), custom_call_target="tpu_custom_call" | custom-call | tf_op jit(solution)/shard_map/pallas_call | solution.py:506
  34.8 9.1 %all_to_all.20.arrived = f32[8,8,128]{2,1,0:T(8,128)S(1)} all-to-all(f32[8,8,128]{2,1,0:T(8,128)S(1)} %get-tuple-element.17), channel_id=1, replica_groups=mesh['groups'=2,'dom'=4,'sub'=2,'field'=2] {'dom','sub'}, dimensions={0} | all-to-all | bytes 65536 | tf_op jit(solution)/shard_map/all_to_all | solution.py:520
  43.9 2.2 %shard_map.142 = (f32[8,128]{1,0:T(8,128)S(1)}, f32[16,4,128]{2,1,0:T(4,128)S(1)}) custom-call(f32[3,32,128]{2,1,0:T(8,128)S(1)} %get-tuple-element.16.weighted, f32[8,8,128]{2,1,0:T(8,128)S(1)} %all_to_all.20.arrived, s32[10,1024]{1,0:T(8,128)S(1)} %copy-done.1, f32[30,8,128]{2,1,0:T(8,128)S(1)} %get-tuple-element.18.coupled, ...), custom_call_target="tpu_custom_call" | custom-call | tf_op jit(solution)/shard_map/pallas_call | solution.py:522
  46.1 9.2 %all_to_all.21.sums = f32[16,4,128]{2,1,0:T(4,128)S(1)} all-to-all(f32[16,4,128]{2,1,0:T(4,128)S(1)} %get-tuple-element.20), channel_id=1, replica_groups=mesh['groups'=2,'dom'=4,'sub'=2,'field'=2] {'dom','sub','field'}, dimensions={0} | all-to-all | bytes 65536 | tf_op jit(solution)/shard_map/all_to_all | solution.py:534
  55.3 0.7 %shard_map.143 = (f32[8,128]{1,0:T(8,128)}, f32[8,128]{1,0:T(8,128)}, f32[8,128]{1,0:T(8,128)}) custom-call(f32[16,4,128]{2,1,0:T(4,128)S(1)} %all_to_all.21.sums, f32[8,128]{1,0:T(8,128)S(1)} %get-tuple-element.21.hess, f32[4,8,128]{2,1,0:T(8,128)S(1)} %get-tuple-element.19.vectors), custom_call_target="tpu_custom_call" | custom-call | tf_op jit(solution)/shard_map/pallas_call | solution.py:536
Async XLA Ops:
  0.6 16.1 %copy-start = (f32[3,4096]{1,0:T(4,128)S(1)}, f32[3,4096]{1,0:T(4,128)}, u32[]{:S(2)}) copy-start(f32[3,4096]{1,0:T(4,128)} %background.3) | copy-start | bytes 147460
  0.6 16.1 %copy-start.1 = (s32[10,1024]{1,0:T(8,128)S(1)}, s32[10,1024]{1,0:T(8,128)}, u32[]{:S(2)}) copy-start(s32[10,1024]{1,0:T(8,128)} %connect.3) | copy-start | bytes 122884
  2.6 14.1 %copy-start.3 = (f32[30,30]{1,0:T(8,128)S(1)}, f32[30,30]{1,0:T(8,128)}, u32[]{:S(2)}) copy-start(f32[30,30]{1,0:T(8,128)} %stiff.1) | copy-start | bytes 10804
  2.6 14.1 %copy-start.8 = (f32[1024]{0:T(1024)S(1)}, f32[1024]{0:T(1024)}, u32[]{:S(2)}) copy-start(f32[1024]{0:T(1024)} %param.19) | copy-start | bytes 12292
  2.6 14.2 %copy-start.9 = (f32[1024]{0:T(1024)S(1)}, f32[1024]{0:T(1024)}, u32[]{:S(2)}) copy-start(f32[1024]{0:T(1024)} %param.18) | copy-start | bytes 12292
  2.6 14.2 %copy-start.10 = (f32[1024]{0:T(1024)S(1)}, f32[1024]{0:T(1024)}, u32[]{:S(2)}) copy-start(f32[1024]{0:T(1024)} %param.17) | copy-start | bytes 12292
  2.6 14.1 %all-to-all-start = ((f32[8,8,128]{2,1,0:T(8,128)}), f32[8,8,128]{2,1,0:T(8,128)S(1)}, u32[]{:S(2)}, u32[]{:S(2)}) async-start(f32[8,8,128]{2,1,0:T(8,128)} %shard_map.139), calls=%async_computation | async-start | bytes 65536 | tf_op jit(solution)/shard_map/all_to_all | solution.py:469
  16.7 0.7 %copy-start.7 = (f32[1024]{0:T(1024)S(1)}, f32[1024]{0:T(1024)}, u32[]{:S(2)}) copy-start(f32[1024]{0:T(1024)} %param.20) | copy-start | bytes 12292
  16.7 0.7 %copy-start.6 = (f32[1024]{0:T(1024)S(1)}, f32[1024]{0:T(1024)}, u32[]{:S(2)}) copy-start(f32[1024]{0:T(1024)} %param.16) | copy-start | bytes 12292
  22.9 10.5 %copy-start.2 = (s32[1,3,2,256]{3,2,1,0:T(2,128)S(1)}, s32[1,3,2,256]{3,2,1,0:T(2,128)}, u32[]{:S(2)}) copy-start(s32[1,3,2,256]{3,2,1,0:T(2,128)} %nodes.3) | copy-start | bytes 18436
  22.9 10.5 %copy-start.4 = (f32[4096]{0:T(1024)S(1)}, f32[4096]{0:T(1024)}, u32[]{:S(2)}) copy-start(f32[4096]{0:T(1024)} %param.13) | copy-start | bytes 49156
  22.9 10.5 %all-to-all-start.1 = ((f32[16,8,128]{2,1,0:T(8,128)}), f32[16,8,128]{2,1,0:T(8,128)S(1)}, u32[]{:S(2)}, u32[]{:S(2)}) async-start(f32[16,8,128]{2,1,0:T(8,128)} %get-tuple-element.15), calls=%async_computation.1 | async-start | bytes 131072 | tf_op jit(solution)/shard_map/all_to_all | solution.py:504
  26.6 6.9 %copy-start.5 = (s32[1,3,2]{1,2,0:T(2,128)S(1)}, s32[1,3,2]{1,2,0:T(2,128)}, u32[]{:S(2)}) copy-start(s32[1,3,2]{1,2,0:T(2,128)} %param.22) | copy-start | bytes 76
  26.6 1.3 %collective-permute-start = (f32[3,16,256]{2,1,0:T(8,128)S(1)}, f32[3,16,256]{2,1,0:T(8,128)S(1)}, u32[]{:S(2)}, u32[]{:S(2)}) collective-permute-start(f32[3,16,256]{2,1,0:T(8,128)S(1)} %get-tuple-element.14.mine), channel_id=1, source_target_pairs={{0,1},{1,0},{2,3},{3,2},{4,5},{5,4},{6,7},{7,6},{8,9},{9,8},{10,11... | collective-permute-start | bytes 147464 | tf_op jit(solution)/shard_map/ppermute | solution.py:501

commit v3 on v2

--- a/solution.py
+++ b/solution.py
@@ -11,7 +11,6 @@
 LANES = 128
 SUBS = 8
 PARTS = 3
-GROUP = 1
 UNROLL = 10
 SUMS = 4
 LANE_BITS = 7
@@ -25,38 +24,31 @@
     return -(-count // step) * step
 
 
-def lookup(table, rows, index, store):
-    def pair(first, count):
-        entries = [index[first + i] for i in range(count)]
-        high = [lax.shift_right_logical(x, LANE_BITS) for x in entries]
-        low = [x & (LANES - 1) for x in entries]
-        found = [[None] * 3 for _ in entries]
+def lookup(table, rows, index, store, begin=None, first=0, comps=3):
+    def one(tile):
+        entry = index[tile]
+        high = lax.shift_right_logical(entry, LANE_BITS)
+        low = entry & (LANES - 1)
+        found = [0.0 if begin is None else begin(tile, c) for c in range(comps)]
         for row in range(rows):
-            lines = [
-                jnp.broadcast_to(table[c, row : row + 1, :], (SUBS, LANES))
-                for c in range(3)
-            ]
-            for i in range(count):
-                here = high[i] == row
-                for c in range(3):
-                    value = jnp.take_along_axis(
-                        lines[c], low[i], axis=1, mode="promise_in_bounds"
-                    )
-                    found[i][c] = jnp.where(
-                        here, value, 0.0 if row == 0 else found[i][c]
-                    )
-        for i in range(count):
-            for c in range(3):
-                store(first + i, c, found[i][c])
-
-    def step(p, carry):
-        pair(p * GROUP, GROUP)
+            here = high == first + row
+            for c in range(comps):
+                line = jnp.broadcast_to(table[c, row : row + 1, :], (SUBS, LANES))
+                value = jnp.take_along_axis(
+                    line, low, axis=1, mode="promise_in_bounds"
+                )
+                found[c] = jnp.where(here, value, found[c])
+        for c in range(comps):
+            store(tile, c, found[c])
+
+    def step(tile, carry):
+        one(tile)
         return carry
 
-    tiles = index.shape[0]
-    lax.fori_loop(0, tiles // GROUP, step, 0)
-    if tiles % GROUP:
-        pair(tiles // GROUP * GROUP, tiles % GROUP)
+    if index.shape[0] == 1:
+        one(0)
+    else:
+        lax.fori_loop(0, index.shape[0], step, 0, unroll=min(2 if rows > 16 else 5, index.shape[0]))
 
 
 def split_parts(value):
@@ -177,6 +169,77 @@
             table[c, r : r + 1, :] = background[c : c + 1, r * LANES : (r + 1) * LANES]
     load_links(nodes, index, sub_count, halves)
     send_links(table, rows, counts, index, values, out, dom_count, sub_count, halves)
+
+
+def load_index(connect, index):
+    for k in range(10):
+        for b in range(SUBS):
+            index[k, b : b + 1, :] = connect[k : k + 1, b * LANES : (b + 1) * LANES]
+
+
+def couple(live, stiff, scale, others, state, coupled, vectors, pieces):
+    element_vectors(live, scale, others, vectors)
+    forward_terms(stiff, state, coupled, vectors, pieces)
+
+
+def element_vectors(live, scale, others, vectors):
+    direction, residual, iterate, reg = others
+    element = (
+        lax.broadcasted_iota(jnp.int32, (SUBS, LANES), 0) * LANES
+        + lax.broadcasted_iota(jnp.int32, (SUBS, LANES), 1)
+    )
+    mask = (element < BLK * live[0]).astype(jnp.float32)
+    search = mask * direction[...]
+    vectors[0] = search
+    vectors[1] = mask * residual[...]
+    vectors[2] = mask * iterate[...]
+    vectors[3] = reg[...] * search
+    vectors[4] = mask * scale[...]
+
+
+def forward_terms(stiff, state, coupled, vectors, pieces):
+    search, factor = vectors[0], vectors[4]
+    for c in range(3):
+        sums = [None] * 10
+        for j in range(30):
+            value = state[j]
+            for k in range(10):
+                term = stiff[c * 10 + k, j] * value
+                sums[k] = term if j == 0 else sums[k] + term
+        for k in range(10):
+            result = factor * sums[k]
+            coupled[c * 10 + k] = result
+            for part, piece in enumerate(split_parts(search * result)):
+                pieces[part * 3 + c, k] = piece
+
+
+def assemble(pieces, index, total, owned_high, ghost_high, width):
+    total[...] = jnp.zeros_like(total)
+
+    def scatter(k, carry):
+        pairs = [
+            one_hot_pair(
+                [pieces[q, k, b : b + 1, :] for q in range(3 * PARTS)],
+                index[k, b : b + 1, :],
+                owned_high,
+                ghost_high,
+                width,
+            )
+            for b in range(SUBS)
+        ]
+        total[...] += contract(*[jnp.concatenate(x, axis=1) for x in zip(*pairs)])
+        return carry
+
+    lax.fori_loop(0, 10, scatter, 0, unroll=UNROLL)
+
+
+def summed(total, first, step, count):
+    value = None
+    for part in reversed(range(PARTS)):
+        base = first + part * 3 * step
+        piece = total[base : base + count, :]
+        value = piece if value is None else value + piece
+    return value
 
 
 def forward_kernel(
@@ -210,65 +273,24 @@
         for r in range(rows):
             table[c, r : r + 1, :] = background[c : c + 1, r * LANES : (r + 1) * LANES]
     fill_ghosts(table, rows, arrived, dom_count, sub_count, halves)
-    for k in range(10):
-        for b in range(SUBS):
-            index[k, b : b + 1, :] = connect[k : k + 1, b * LANES : (b + 1) * LANES]
+    load_index(connect, index)
 
     def keep(k, c, value):
         state[c * 10 + k] = value
 
     lookup(table, rows + ghost_rows, index, keep)
-    element = (
-        lax.broadcasted_iota(jnp.int32, (SUBS, LANES), 0) * LANES
-        + lax.broadcasted_iota(jnp.int32, (SUBS, LANES), 1)
-    )
-    mask = (element < BLK * live[0]).astype(jnp.float32)
-    search = mask * direction[...]
-    factor = mask * scale[...]
-    vectors[0] = search
-    vectors[1] = mask * residual[...]
-    vectors[2] = mask * iterate[...]
-    vectors[3] = reg[...] * search
-    for c in range(3):
-        sums = [None] * 10
-        for j in range(30):
-            value = state[j]
-            for k in range(10):
-                term = stiff[c * 10 + k, j] * value
-                sums[k] = term if j == 0 else sums[k] + term
-        for k in range(10):
-            result = factor * sums[k]
-            coupled[c * 10 + k] = result
-            for part, piece in enumerate(split_parts(search * result)):
-                pieces[part * 3 + c, k] = piece
-
-    lines_count = 3 * PARTS
+    couple(
+        live,
+        stiff,
+        scale,
+        (direction, residual, iterate, reg),
+        state,
+        coupled,
+        vectors,
+        pieces,
+    )
     ghost_high = up_to(3 * sub_count, SUBS)
-    total[...] = jnp.zeros_like(total)
-
-    def scatter(k, carry):
-        pairs = [
-            one_hot_pair(
-                [pieces[q, k, b : b + 1, :] for q in range(lines_count)],
-                index[k, b : b + 1, :],
-                owned_high,
-                ghost_high,
-                width,
-            )
-            for b in range(SUBS)
-        ]
-        total[...] += contract(*[jnp.concatenate(x, axis=1) for x in zip(*pairs)])
-        return carry
-
-    lax.fori_loop(0, 10, scatter, 0, unroll=UNROLL)
-
-    def summed(first, step, count):
-        value = None
-        for part in reversed(range(PARTS)):
-            base = first + part * 3 * step
-            piece = total[base : base + count, :]
-            value = piece if value is None else value + piece
-        return value
+    assemble(pieces, index, total, owned_high, ghost_high, width)
 
     def clear(p, carry):
         outbound[p] = jnp.zeros(outbound.shape[1:], jnp.float32)
@@ -279,9 +301,9 @@
     fields = outbound.shape[0] // (dom_count * sub_count)
     ghost = [None] * 3
     for c in range(3):
-        owned[c] = summed(c * owned_high, owned_high, owned_high)
+        owned[c] = summed(total, c * owned_high, owned_high, owned_high)
         ghost[c] = summed(
-            lines_count * owned_high + c * ghost_high, ghost_high, 3 * sub_count
+            total, 3 * PARTS * owned_high + c * ghost_high, ghost_high, 3 * sub_count
         )
     for o in range(3):
         place = dom + o - 1
@@ -367,9 +389,7 @@
     rows = weighted.shape[1]
     table[:, 0:rows, :] = weighted[...]
     fill_ghosts(table, rows, arrived, dom_count, sub_count, halves)
-    for k in range(10):
-        for b in range(SUBS):
-            index[k, b : b + 1, :] = connect[k : k + 1, b * LANES : (b + 1) * LANES]
+    load_index(connect, index)
 
     def keep(k, c, value):
         pulled[k, c] = value
@@ -413,19 +433,487 @@
     direction_out[...] = residual_next + squared_after / squared_before * search
 
 
-def on_device(
-    background,
-    obs_weight,
-    connect,
-    live_blocks,
-    elem_scale,
-    reg_weight,
-    iterate,
-    residual,
-    direction,
-    send_nodes,
-    send_count,
-    ref_stiff,
+def own_table(source, table):
+    for c in range(3):
+        for r in range(source.shape[1] // LANES):
+            table[c, r : r + 1, :] = source[c : c + 1, r * LANES : (r + 1) * LANES]
+
+
+def pair_start_kernel(counts, nodes, background, obs, pack, index, spots, table):
+    sub = lax.axis_index("sub")
+    step = jnp.where(lax.axis_index("field") == 0, 2, 0)
+    own_table(background, table)
+    table[3] = obs[...]
+    row = lax.broadcasted_iota(jnp.int32, (SUBS, LANES), 0)
+    slot = lax.broadcasted_iota(jnp.int32, (SUBS, LANES), 1) + row % 2 * LANES
+
+    def line(o, k, h):
+        zero = nodes[0, o, 0:1, h * LANES : (h + 1) * LANES]
+        one = nodes[0, o, 1:2, h * LANES : (h + 1) * LANES]
+        return jnp.where((sub ^ k) == 0, zero, one)
+
+    def gate(links):
+        limit = jnp.zeros((SUBS, LANES), jnp.int32)
+        for i, (o, k) in enumerate(links):
+            limit = jnp.where(row // 2 == i, counts[0, sub ^ k, o], limit)
+        return slot < limit
+
+    value_links = ((step, 0), (step, 1), (1, 1))
+    weight_links = ((0, 1), (1, 1), (2, 1))
+    for tile, links in ((index, value_links), (spots, weight_links)):
+        tile[0] = jnp.zeros((SUBS, LANES), jnp.int32)
+        for i, (o, k) in enumerate(links):
+            for h in range(2):
+                tile[0, 2 * i + h : 2 * i + h + 1, :] = line(o, k, h)
+    value_gate = gate(value_links)
+
+    def keep(tile, c, value):
+        pack[c] = jnp.where(value_gate, value, 0.0)
+
+    lookup(table, table.shape[1], index, keep)
+
+    def keep_weight(tile, c, value):
+        pack[5] = value
+
+    lookup(table.at[3:4], table.shape[1], spots, keep_weight, comps=1)
+    pack[3] = jnp.full((SUBS, LANES), -1.0, jnp.float32)
+    pack[4] = jnp.full((SUBS, LANES), -1.0, jnp.float32)
+    lane = lax.broadcasted_iota(jnp.int32, (1, LANES), 1)
+    for o in range(3):
+        for k in range(2):
+            for h in range(2):
+                at = (o * 2 + k) * 2 + h
+                here = lane + h * LANES < counts[0, sub ^ k, o]
+                pack[3 + at // SUBS, at % SUBS : at % SUBS + 1, :] = jnp.where(
+                    here, line(o, k, h), -1
+                ).astype(jnp.float32)
+
+
+def pair_vector_kernel(
+    live, pack, scale, direction, residual, iterate, reg, near, vectors
+):
+    element_vectors(live, scale, (direction, residual, iterate, reg), vectors)
+    near[...] = pack[...]
+
+
+def pair_join_kernel(near, sibling, out):
+    row = lax.broadcasted_iota(jnp.int32, (SUBS, LANES), 0)
+    for c in range(3):
+        out[c] = jnp.where(row < 2, near[c], sibling[c])
+
+
+def pair_ghosts(dom_count, mine, other, middle, table):
+    dom = lax.axis_index("dom")
+    first = lax.axis_index("field") == 0
+    for c in range(3):
+        below = jnp.where(first, mine[c], other[c])
+        above = jnp.where(first, other[c], mine[c])
+        below = jnp.where(dom > 0, below, 0.0)
+        above = jnp.where(dom < dom_count - 1, above, 0.0)
+        table[c, 0:4, :] = below[0:4, :]
+        table[c, 4:6, :] = jnp.zeros((2, LANES), jnp.float32)
+        table[c, 6:8, :] = middle[c, 4:6, :]
+        table[c, 8:12, :] = above[0:4, :]
+
+
+def pair_own_kernel(link_slots, background, connect, index, partial, table):
+    sub = lax.axis_index("sub")
+    own_table(background, table)
+    load_index(connect, index)
+    owned_nodes = background.shape[1]
+    for k in range(10):
+        entry = index[k]
+        index[k] = jnp.where(entry >= owned_nodes, entry ^ (sub * link_slots), entry)
+
+    def keep(k, c, value):
+        partial[c * 10 + k] = value
+
+    lookup(table, table.shape[1], index, keep)
+
+
+def pair_forward_kernel(
+    dom_count,
+    stiff,
+    partial,
+    index,
+    mine,
+    other,
+    middle,
+    vectors,
+    coupled,
+    kept,
+    sent,
+    ghosts,
+    state,
+    pieces,
+    total,
+):
+    owned_high = kept.shape[1] // 2 - SUBS // 2
+    pair_ghosts(dom_count, mine, other, middle, ghosts)
+
+    def begin(k, c):
+        return partial[c * 10 + k]
+
+    def keep(k, c, value):
+        state[c * 10 + k] = value
+
+    lookup(ghosts, 12, index, keep, begin, 2 * owned_high)
+    forward_terms(stiff, state, coupled, vectors, pieces)
+    width = 2 * LANES
+    assemble(pieces, index, total, owned_high, SUBS, width)
+    first = lax.axis_index("field") == 0
+    base = 2 * owned_high
+    for c in range(3):
+        own = summed(total, c * owned_high, owned_high, owned_high)
+        ghost = summed(total, 3 * PARTS * owned_high + c * SUBS, SUBS, SUBS)
+        for h in range(2):
+            half = own[:, h * LANES : (h + 1) * LANES]
+            kept[c, h * owned_high : (h + 1) * owned_high, :] = half
+            sent[c, h * owned_high : (h + 1) * owned_high, :] = half
+            lines = ghost[:, h * LANES : (h + 1) * LANES]
+            for k in range(2):
+                below, above = lines[k : k + 1, :], lines[4 + k : 5 + k, :]
+                at = base + 2 * k + h
+                kept[c, at : at + 1, :] = jnp.where(first, above, below)
+                sent[c, at : at + 1, :] = jnp.where(first, below, above)
+            for out in (kept, sent):
+                out[c, base + 4 + h : base + 5 + h, :] = lines[3:4, :]
+                out[c, base + 6 + h : base + 7 + h, :] = jnp.zeros((1, LANES), jnp.float32)
+
+
+def node_tile(links, tile):
+    values = tile.astype(jnp.int32)
+    return jnp.maximum(values, 0), values >= 0
+
+
+def pair_sum_kernel(kept, came, pack, own, part, index, table):
+    rows = own.shape[1]
+    half = rows // 2
+    for c in range(3):
+        both = kept[c] + came[c]
+        own[c] = both[:rows]
+        for h in range(2):
+            table[c, pl.ds(h, half, stride=2), :] = both[h * half : (h + 1) * half]
+        part[3 + c] = both[rows:]
+    index[0] = jnp.zeros((SUBS, LANES), jnp.int32)
+    for o in range(3):
+        for h in range(2):
+            at = (o * 2 + 1) * 2 + h
+            line = pack[3 + at // SUBS, at % SUBS : at % SUBS + 1, :].astype(jnp.int32)
+            index[0, 2 * o + h : 2 * o + h + 1, :] = jnp.maximum(line, 0)
+
+    def keep(tile, c, value):
+        part[c] = value
+
+    lookup(table, rows, index, keep)
+
+
+def landing(nodes, lines, owned_high, width):
+    pairs = []
+    for (o, k), source in lines:
+        for h in range(2):
+            at = (o * 2 + k) * 2 + h
+            entry = nodes[at // SUBS, at % SUBS : at % SUBS + 1, :].astype(jnp.int32)
+            values = [source(c, h) for c in range(3)]
+            split = [split_parts(v) for v in values]
+            pairs.append(
+                one_hot_pair(
+                    [split[c][part] for part in range(PARTS) for c in range(3)],
+                    entry,
+                    owned_high,
+                    0,
+                    width,
+                )
+            )
+    return contract(*[jnp.concatenate(x, axis=1) for x in zip(*pairs)])
+
+
+def pair_owner_kernel(
+    dom_count,
+    own,
+    part,
+    mine,
+    other,
+    came,
+    pack,
+    sibling,
+    obs,
+    weighted,
+    out,
+    total,
+    index,
+    table,
+):
+    rows = own.shape[1]
+    owned_high = rows // 2
+    width = 2 * LANES
+    dom = lax.axis_index("dom")
+    first = lax.axis_index("field") == 0
+
+    def pick(here, there, inside):
+        def line(k):
+            def get(c, h):
+                at = 2 * k + h
+                a, b = here(c)[at : at + 1, :], there(c)[at : at + 1, :]
+                return jnp.where(inside, jnp.where(first, a, b), 0.0)
+
+            return get
+
+        return line
+
+    mine_at, other_at = (lambda c: mine[c]), (lambda c: other[c])
+    his_mine, his_other = (lambda c: came[6 + c]), (lambda c: came[9 + c])
+    low, high = dom > 0, dom < dom_count - 1
+    below = pick(mine_at, other_at, low)
+    above = pick(other_at, mine_at, high)
+    his_below = pick(his_mine, his_other, low)
+    his_above = pick(his_other, his_mine, high)
+    own_lines = (
+        ((0, 0), below(0)),
+        ((0, 1), his_below(1)),
+        ((1, 1), lambda c, h: came[3 + c, 4 + h : 5 + h, :]),
+        ((2, 0), above(0)),
+        ((2, 1), his_above(1)),
+    )
+    his_lines = (
+        ((0, 0), his_below(0)),
+        ((0, 1), below(1)),
+        ((1, 1), lambda c, h: part[3 + c, 4 + h : 5 + h, :]),
+        ((2, 0), his_above(0)),
+        ((2, 1), above(1)),
+    )
+    total[0] = landing(pack.at[3:5], own_lines, owned_high, width)
+    total[1] = landing(sibling.at[3:5], his_lines, owned_high, width)
+    for c in range(3):
+        landed = summed(total.at[0], c * owned_high, owned_high, owned_high)
+        his = summed(total.at[1], c * owned_high, owned_high, owned_high)
+        for h in range(2):
+            at = pl.ds(h, owned_high, stride=2)
+            value = own[c, h * owned_high : (h + 1) * owned_high, :]
+            value = obs[at, :] * (value + landed[:, h * LANES : (h + 1) * LANES])
+            weighted[c, at, :] = value
+            table[c, at, :] = value
+            table[c, pl.ds(rows + h, owned_high, stride=2), :] = his[
+                :, h * LANES : (h + 1) * LANES
+            ]
+
+    def node(tiles, o, k, h):
+        at = (o * 2 + k) * 2 + h
+        return tiles[3 + at // SUBS, at % SUBS : at % SUBS + 1, :].astype(jnp.int32)
+
+    index[0] = jnp.full((SUBS, LANES), -1, jnp.int32)
+    index[1] = jnp.zeros((SUBS, LANES), jnp.int32)
+    shift = rows * LANES
+    for h in range(2):
+        line = jnp.where(first, node(pack, 2, 0, h), node(pack, 0, 0, h))
+        index[0, h : h + 1, :] = line
+        for at, line in (
+            (2, jnp.where(first, node(sibling, 2, 1, h), node(sibling, 0, 1, h))),
+            (4, node(sibling, 1, 1, h)),
+        ):
+            index[0, at + h : at + h + 1, :] = jnp.where(line < 0, line, line + shift)
+    is_open = index[0] >= 0
+    index[0] = jnp.maximum(index[0], 0)
+    row = lax.broadcasted_iota(jnp.int32, (SUBS, LANES), 0)
+
+    def lined_up(tile):
+        lines = []
+        for h in range(2):
+            lines.append(jnp.where(first, tile[4 + h : 5 + h, :], tile[h : h + 1, :]))
+        lines += [tile[2:3, :], tile[3:4, :]]
+        blank = jnp.zeros((2, LANES), jnp.float32)
+        return jnp.concatenate([blank] + lines + [blank], axis=0)
+
+    weight = lined_up(sibling[5])
+
+    def keep(tile, c, value):
+        value = jnp.where(row < 2, value, weight * (lined_up(came[c]) + value))
+        out[c] = jnp.where(is_open, value, 0.0)
+
+    lookup(table, 2 * rows, index.at[0:1], keep)
+
+
+def pair_near_kernel(weighted, index, coupled, near, pulled):
+    def keep(k, c, value):
+        pulled[c * 10 + k] = value
+
+    lookup(weighted, weighted.shape[1], index, keep)
+    image = None
+    for i in range(30):
+        term = coupled[i] * pulled[i]
+        image = term if image is None else image + term
+    near[...] = image
+
+
+def write_sums(search, remain, image, sums):
+    for i, product in enumerate(
+        (remain * remain, search * image, remain * image, image * image)
+    ):
+        line = jnp.sum(product, axis=0, keepdims=True)
+        for p in range(sums.shape[0]):
+            sums[p, i : i + 1, :] = line
+
+
+def pair_adjoint_kernel(
+    dom_count,
+    rows,
+    near,
+    mine,
+    other,
+    middle,
+    index,
+    coupled,
+    vectors,
+    hess,
+    sums,
+    ghosts,
+    pulled,
+):
+    pair_ghosts(dom_count, mine, other, middle, ghosts)
+
+    def keep(k, c, value):
+        pulled[c * 10 + k] = value
+
+    lookup(ghosts, 12, index, keep, first=rows)
+    image = near[...]
+    for i in range(30):
+        image = image + coupled[i] * pulled[i]
+    image = image + vectors[3]
+    hess[...] = image
+    write_sums(vectors[0], vectors[1], image, sums)
+
+
+def pair_step(background, obs, connect, live_blocks, scale, others, nodes, counts, stiff):
+    f32, i32 = jnp.float32, jnp.int32
+    shape = jax.ShapeDtypeStruct
+    dom_count = lax.axis_size("dom")
+    owned_nodes = background.shape[1]
+    link_slots = nodes.shape[3]
+    rows = owned_nodes // LANES
+    owned_high = owned_nodes // link_slots
+    tile = (SUBS, LANES)
+    swap = [(0, 1), (1, 0)]
+    last = dom_count - 1
+    ring = [(2 * d, 2 * d + 2) for d in range(last)]
+    ring += [(2 * d + 3, 2 * d + 1) for d in range(last)]
+    ring += [(2 * last, 2 * last + 1), (1, 0)]
+    left_rows = 3 * PARTS * owned_high + up_to(3 * PARTS * SUBS, 16)
+
+    def across(x):
+        return lax.ppermute(x, "field", swap)
+
+    def beside(x):
+        return lax.ppermute(x, "sub", swap)
+
+    def along(x):
+        return lax.ppermute(x, ("dom", "field"), ring)
+
+    def call(kernel, outs, scratch, smem, args, params=PARAMS):
+        return pl.pallas_call(
+            kernel,
+            compiler_params=params,
+            out_shape=outs,
+            in_specs=[SMEM] * smem + [VMEM] * (len(args) - smem),
+            out_specs=jax.tree.map(lambda x: VMEM, outs),
+            scratch_shapes=scratch,
+            cost_estimate=pl.CostEstimate(
+                flops=2**20, bytes_accessed=2**16, transcendentals=0
+            ),
+        )(*args)
+
+    pack = call(
+        pair_start_kernel,
+        shape((6,) + tile, f32),
+        [
+            pltpu.VMEM((1,) + tile, i32),
+            pltpu.VMEM((1,) + tile, i32),
+            pltpu.VMEM((4, rows, LANES), f32),
+        ],
+        1,
+        (counts, nodes, background, obs),
+        None,
+    )
+    sibling = beside(pack)
+    pack, vectors = call(
+        pair_vector_kernel,
+        (shape((6,) + tile, f32), shape((5,) + tile, f32)),
+        [],
+        1,
+        (live_blocks, pack, scale) + others,
+    )
+    mine = along(
+        call(pair_join_kernel, shape((3,) + tile, f32), [], 0, (pack, sibling))
+    )
+    index, partial = call(
+        functools.partial(pair_own_kernel, link_slots),
+        (shape((10,) + tile, i32), shape((30,) + tile, f32)),
+        [pltpu.VMEM((3, rows, LANES), f32)],
+        0,
+        (background, connect),
+    )
+    mine, partial = lax.optimization_barrier((mine, partial))
+    other = across(mine)
+    coupled, kept, sent = call(
+        functools.partial(pair_forward_kernel, dom_count),
+        (
+            shape((30,) + tile, f32),
+            shape((3, rows + SUBS, LANES), f32),
+            shape((3, rows + SUBS, LANES), f32),
+        ),
+        [
+            pltpu.VMEM((3, 16, LANES), f32),
+            pltpu.VMEM((30,) + tile, f32),
+            pltpu.VMEM((3 * PARTS, 10) + tile, f32),
+            pltpu.VMEM((left_rows, link_slots), f32),
+        ],
+        1,
+        (stiff, partial, index, mine, other, sibling, vectors),
+    )
+    came = across(sent)
+    mine = along(kept[:, rows:] + came[:, rows:])
+    own, part = call(
+        pair_sum_kernel,
+        (shape((3, rows, LANES), f32), shape((6,) + tile, f32)),
+        [pltpu.VMEM((1,) + tile, i32), pltpu.VMEM((3, rows, LANES), f32)],
+        0,
+        (kept, came, pack),
+    )
+    mine, part = lax.optimization_barrier((mine, part))
+    other = across(mine)
+    came = beside(jnp.concatenate([part, mine, other], axis=0))
+    weighted, outbound = call(
+        functools.partial(pair_owner_kernel, dom_count),
+        (shape((3, rows, LANES), f32), shape((3,) + tile, f32)),
+        [
+            pltpu.VMEM((2, 3 * PARTS * owned_high, link_slots), f32),
+            pltpu.VMEM((2,) + tile, i32),
+            pltpu.VMEM((3, 2 * rows, LANES), f32),
+        ],
+        0,
+        (own, part, mine, other, came, pack, sibling, obs),
+    )
+    mine = along(outbound)
+    near = call(
+        pair_near_kernel,
+        shape(tile, f32),
+        [pltpu.VMEM((30,) + tile, f32)],
+        0,
+        (weighted, index, coupled),
+    )
+    mine, near = lax.optimization_barrier((mine, near))
+    other = across(mine)
+    hess, sums = call(
+        functools.partial(pair_adjoint_kernel, dom_count, rows),
+        (shape(tile, f32), shape((4 * dom_count, SUMS, LANES), f32)),
+        [pltpu.VMEM((3, 16, LANES), f32), pltpu.VMEM((30,) + tile, f32)],
+        0,
+        (near, mine, other, outbound, index, coupled, vectors),
+    )
+    return hess, sums, vectors
+
+
+def general_step(
+    background, obs, connect, live_blocks, scale, others, send_nodes, counts, ref_stiff
 ):
     f32, i32 = jnp.float32, jnp.int32
     shape = jax.ShapeDtypeStruct
@@ -446,12 +934,6 @@
     link_tiles = up_to(ghost_rows, SUBS) // SUBS
     left_rows = 3 * PARTS * owned_high + up_to(3 * PARTS * up_to(3 * sub_count, SUBS), 16)
     dims = (dom_count, sub_count, halves)
-    tiled = lambda x: x.reshape(-1, LANES)
-    scale, reg, guess, remain, search = map(
-        tiled, (elem_scale, reg_weight, iterate, residual, direction)
-    )
-    obs = tiled(obs_weight)
-    counts = jnp.swapaxes(send_count, 1, 2)
     links = ("dom", "sub")
     cores = ("dom", "sub", "field")
 
@@ -473,7 +955,7 @@
         compiler_params=PARAMS,
         out_shape=(
             shape((30, SUBS, LANES), f32),
-            shape((4, SUBS, LANES), f32),
+            shape((5, SUBS, LANES), f32),
             shape((3, owned_high, width), f32),
             shape((devices, chunk, LANES), f32),
         ),
@@ -493,10 +975,7 @@
         arrived,
         connect,
         scale,
-        search,
-        remain,
-        guess,
-        reg,
+        *others,
     )
     swapped = lax.ppermute(
         owned, "field", [(i, (i + 1) % field_count) for i in range(field_count)]
@@ -531,6 +1010,45 @@
             pltpu.VMEM((10, 3, SUBS, LANES), f32),
         ],
     )(weighted, arrived, connect, coupled, vectors)
+    return hess, sums, vectors
+
+
+def on_device(
+    background,
+    obs_weight,
+    connect,
+    live_blocks,
+    elem_scale,
+    reg_weight,
+    iterate,
+    residual,
+    direction,
+    send_nodes,
+    send_count,
+    ref_stiff,
+):
+    f32 = jnp.float32
+    shape = jax.ShapeDtypeStruct
+    tiled = lambda x: x.reshape(-1, LANES)
+    scale, reg, guess, remain, search = map(
+        tiled, (elem_scale, reg_weight, iterate, residual, direction)
+    )
+    obs = tiled(obs_weight)
+    counts = jnp.swapaxes(send_count, 1, 2)
+    two = lax.axis_size("sub") == 2 and lax.axis_size("field") == 2
+    paired = two and send_nodes.shape[3] == 2 * LANES
+    hess, sums, vectors = (pair_step if paired else general_step)(
+        background,
+        obs,
+        connect,
+        live_blocks,
+        scale,
+        (search, remain, guess, reg),
+        send_nodes,
+        counts,
+        ref_stiff,
+    )
+    cores = ("dom", "sub", "field")
     sums = lax.all_to_all(sums, cores, 0, 0, tiled=True)
 
     results = pl.pallas_call(

time: 56.5 us -> 45.9 us (0.81)
  blocking collectives: 18.3 us -> 13 us
  waiting for transfers between devices: 12.5 us -> 8.97 us
  Pallas kernels: 11.7 us -> 10.1 us
    all_to_all x2 -> x0, waiting for transfers between devices: 11.6 us -> none  [the longest x1 6.03 us: on_device(): arrived = lax.all_to_all(outbound, links, 0, 0, tiled=True)]
    all_to_all x2 -> x0, starting transfers between devices: 11 us -> none  [the longest x1 7.42 us: on_device(): arrived = lax.all_to_all(outbound, links, 0, 0, tiled=True)]
    ppermute x1 -> x9, starting transfers between devices: 0.35 us -> 11.4 us  [the longest x3 6.55 us: along(): return lax.ppermute(x, ('dom', 'field'), ring)]
    all_to_all x1 -> x0, blocking collectives: 9.06 us -> none  [on_device(): arrived = lax.all_to_all(outbound, links, 0, 0, tiled=True)]
    ppermute x1 -> x9, waiting for transfers between devices: 0.94 us -> 8.97 us  [the longest x4 4.59 us: across(): return lax.ppermute(x, 'field', swap)]
    all_to_all x1, blocking collectives: 9.2 us -> 13 us  [on_device(): sums = lax.all_to_all(sums, cores, 0, 0, tiled=True)]
    pallas_call x4 -> x9, Pallas kernels: 11 us -> 9.41 us  [call(): pl.pallas_call(kernel, compiler_params=params, out_shape=outs, in_specs=[...]
  transfers between devices with their start and end apart: 3 -> 9, of which waited for: 3 -> 7; matrix products, arithmetic and copies ran while one was open for 0% -> 0% of each run, Pallas kernels for 0% -> 7%
where the time goes in v3:
time: 45.9 us; the launch traced here: 45.7 us
  blocking collectives  13 us (28%)
  starting transfers between devices  11.4 us (25%)
  Pallas kernels  10.1 us (22%)
  waiting for transfers between devices  8.97 us (20%)
  between operations  1.46 us (3%)
  local copies, waits for them, and re-layouts  0.77 us (2%)
    all_to_all x1, blocking collectives, on_device(): sums = lax.all_to_all(sums, cores, 0, 0, tiled=True)  13 us
    pallas_call x9, Pallas kernels, call(): pl.pallas_call(kernel, compiler_params=params, out_shape=outs, in_specs=[...  9.41 us
    ppermute x3, starting transfers between devices, along(): return lax.ppermute(x, ('dom', 'field'), ring)  6.55 us
    ppermute x4, waiting for transfers between devices, across(): return lax.ppermute(x, 'field', swap)  4.59 us
    ppermute x2, starting transfers between devices, beside(): return lax.ppermute(x, 'sub', swap)  4.47 us
    ppermute x2, waiting for transfers between devices, beside(): return lax.ppermute(x, 'sub', swap)  3.15 us
    ppermute x3, waiting for transfers between devices, along(): return lax.ppermute(x, ('dom', 'field'), ring)  1.23 us
  transfers between devices with their start and end apart: 9, of which 7 were waited for; matrix products, arithmetic and copies ran while one was open for 0% of the time, Pallas kernels for 7%

profile of v3, /device:TPU:0, one launch (start us, length us, event | category | flops | bytes accessed | tf_op | source)
XLA Modules:
  0.0 45.7 jit_solution(14300773049686104220)
XLA Ops:
  0.6 0.0 copy-start.5
  0.6 0.0 copy-start.6
  0.7 0.0 copy-start.7
  0.7 0.0 copy-start.8
  0.7 0.0 copy-start.9
  0.7 0.0 copy-start.2
  0.7 1.7 %shard_map.139.pack = f32[6,8,128]{2,1,0:T(8,128)} custom-call(s32[1,2,3]{2,1,0:T(2,128)} %bitcast.17, s32[1,3,2,256]{3,2,1,0:T(2,128)} %nodes.1, f32[3,4096]{1,0:T(4,128)} %background.3, f32[32,128]{1,0:T(8,128)} %bitcast.10), custom_call_target="tpu_custom_call" | custom-call | flops 1048576 | bytes 65536 | tf_op jit(solution)/shard_map/pallas_call | solution.py:812
  2.4 0.0 copy-start
  2.4 3.0 %collective-permute-start = (f32[6,8,128]{2,1,0:T(8,128)}, f32[6,8,128]{2,1,0:T(8,128)S(1)}, u32[]{:S(2)}, u32[]{:S(2)}) collective-permute-start(f32[6,8,128]{2,1,0:T(8,128)} %shard_map.139.pack), channel_id=1, source_target_pairs={{0,2},{2,0},{1,3},{3,1},{4,6},{6,4},{5,7},{7,5},{8,10},{10,8},{9,1... | collective-permute-start | bytes 73736 | tf_op jit(solution)/shard_map/ppermute | solution.py:806
  6.0 0.0 copy-done.5
  6.1 0.0 copy-done.6
  6.1 0.0 copy-done.7
  6.1 0.0 copy-done.8
  6.1 0.0 copy-done.9
  6.1 0.0 copy-start.1
  6.1 0.7 %copy-done.1 = f32[6,8,128]{2,1,0:T(8,128)S(1)} copy-done((f32[6,8,128]{2,1,0:T(8,128)S(1)}, f32[6,8,128]{2,1,0:T(8,128)}, u32[]{:S(2)}) %copy-start.1) | copy-done | bytes 24600
  6.8 0.6 %collective-permute-done.sibling.middle = f32[6,8,128]{2,1,0:T(8,128)S(1)} collective-permute-done((f32[6,8,128]{2,1,0:T(8,128)}, f32[6,8,128]{2,1,0:T(8,128)S(1)}, u32[]{:S(2)}, u32[]{:S(2)}) %collective-permute-start) | collective-permute-done | bytes 24608 | tf_op jit(solution)/shard_map/ppermute | solution.py:806
  7.4 2.1 %collective-permute-start.1 = (f32[3,8,128]{2,1,0:T(8,128)S(1)}, f32[3,8,128]{2,1,0:T(8,128)S(1)}, u32[]{:S(2)}, u32[]{:S(2)}) collective-permute-start(f32[3,8,128]{2,1,0:T(8,128)S(1)} %shard_map.141), channel_id=1, source_target_pairs={{0,4},{4,8},{8,12},{5,1},{9,5},{13,9},{12,13},{1,0},{2,6},{6,10},{... | collective-permute-start | bytes 36872 | tf_op jit(solution)/shard_map/ppermute | solution.py:809
  9.5 0.0 copy-done.2
  9.5 0.0 copy-done
  9.5 0.0 copy-start.4
  9.5 1.5 %shard_map.142 = (s32[10,8,128]{2,1,0:T(8,128)S(1)}, f32[30,8,128]{2,1,0:T(8,128)S(1)}) custom-call(f32[3,4096]{1,0:T(4,128)S(1)} %copy-done, s32[10,1024]{1,0:T(8,128)S(1)} %copy-done.2), custom_call_target="tpu_custom_call" | custom-call | flops 1048576 | bytes 65536 | tf_op jit(solution)/shard_map/pallas_call | solution.py:812
  11.0 0.0 collective-permute-done.1.mine
  11.0 0.1 collective-permute-start.2
  11.1 1.2 %collective-permute-done.2.other = f32[3,8,128]{2,1,0:T(8,128)S(1)} collective-permute-done((f32[3,8,128]{2,1,0:T(8,128)S(1)}, f32[3,8,128]{2,1,0:T(8,128)S(1)}, u32[]{:S(2)}, u32[]{:S(2)}) %collective-permute-start.2) | collective-permute-done | bytes 12320 | tf_op jit(solution)/shard_map/ppermute | solution.py:803
  12.2 0.0 copy-done.4
  12.2 3.1 %shard_map.143 = (f32[30,8,128]{2,1,0:T(8,128)S(1)}, f32[3,40,128]{2,1,0:T(8,128)S(1)}, f32[3,40,128]{2,1,0:T(8,128)S(1)}) custom-call(f32[30,30]{1,0:T(8,128)S(1)} %copy-done.4, f32[30,8,128]{2,1,0:T(8,128)S(1)} %get-tuple-element.27.partial, s32[10,8,128]{2,1,0:T(8,128)S(1)} %get-tuple-element.28.index, f32[3,8,128]{2,1,0:T(8,128)S(1)} %collective-permute-done.1.mine, ...), custom_call_target="tpu_custom_call" | custom-call | flops 1048576 | bytes 65536 | tf_op jit(solution)/shard_map/pallas_call | solution.py:812
  15.4 0.2 collective-permute-start.3
  15.6 1.1 %collective-permute-done.3.came = f32[3,40,128]{2,1,0:T(8,128)S(1)} collective-permute-done((f32[3,40,128]{2,1,0:T(8,128)S(1)}, f32[3,40,128]{2,1,0:T(8,128)S(1)}, u32[]{:S(2)}, u32[]{:S(2)}) %collective-permute-start.3) | collective-permute-done | bytes 61472 | tf_op jit(solution)/shard_map/ppermute | solution.py:803
  16.7 2.1 %collective-permute-start.4 = (f32[3,8,128]{2,1,0:T(8,128)S(1)}, f32[3,8,128]{2,1,0:T(8,128)S(1)}, u32[]{:S(2)}, u32[]{:S(2)}) collective-permute-start(f32[3,8,128]{2,1,0:T(8,128)S(1)} %slice_add_fusion), channel_id=1, source_target_pairs={{0,4},{4,8},{8,12},{5,1},{9,5},{13,9},{12,13},{1,0},{2,6},{6,10},{... | collective-permute-start | bytes 36872 | tf_op jit(solution)/shard_map/ppermute | solution.py:809
  18.9 0.2 shard_map.144
  19.0 1.2 %collective-permute-done.4.mine = f32[3,8,128]{2,1,0:T(8,128)S(1)} collective-permute-done((f32[3,8,128]{2,1,0:T(8,128)S(1)}, f32[3,8,128]{2,1,0:T(8,128)S(1)}, u32[]{:S(2)}, u32[]{:S(2)}) %collective-permute-start.4) | collective-permute-done | bytes 12320 | tf_op jit(solution)/shard_map/ppermute | solution.py:809
  20.3 0.0 copy-start.3
  20.3 0.0 collective-permute-start.5
  20.3 1.2 %collective-permute-done.5.other = f32[3,8,128]{2,1,0:T(8,128)S(1)} collective-permute-done((f32[3,8,128]{2,1,0:T(8,128)S(1)}, f32[3,8,128]{2,1,0:T(8,128)S(1)}, u32[]{:S(2)}, u32[]{:S(2)}) %collective-permute-start.5) | collective-permute-done | bytes 12320 | tf_op jit(solution)/shard_map/ppermute | solution.py:803
  21.4 1.5 %collective-permute-start.6 = (f32[12,8,128]{2,1,0:T(8,128)S(1)}, f32[12,8,128]{2,1,0:T(8,128)S(1)}, u32[]{:S(2)}, u32[]{:S(2)}) collective-permute-start(f32[12,8,128]{2,1,0:T(8,128)S(1)} %pad_maximum_fusion), channel_id=1, source_target_pairs={{0,2},{2,0},{1,3},{3,1},{4,6},{6,4},{5,7},{7,5},{8,10},{10,8},{9,1... | collective-permute-start | bytes 147464 | tf_op jit(solution)/shard_map/ppermute | solution.py:806
  22.9 2.6 %collective-permute-done.6.came = f32[12,8,128]{2,1,0:T(8,128)S(1)} collective-permute-done((f32[12,8,128]{2,1,0:T(8,128)S(1)}, f32[12,8,128]{2,1,0:T(8,128)S(1)}, u32[]{:S(2)}, u32[]{:S(2)}) %collective-permute-start.6) | collective-permute-done | bytes 49184 | tf_op jit(solution)/shard_map/ppermute | solution.py:806
  25.5 0.0 copy-done.3
  25.5 0.9 %shard_map.145 = (f32[3,32,128]{2,1,0:T(8,128)S(1)}, f32[3,8,128]{2,1,0:T(8,128)S(1)}) custom-call(f32[3,32,128]{2,1,0:T(8,128)S(1)} %get-tuple-element.33.own, f32[6,8,128]{2,1,0:T(8,128)S(1)} %get-tuple-element.35.part, f32[3,8,128]{2,1,0:T(8,128)S(1)} %collective-permute-done.4.mine, f32[3,8,128]{2,1,0:T(8,128)S(1)} %collective-permute-done.5.other, ...), custom_call_target="tpu_custom_call" | custom-call | flops 1048576 | bytes 65536 | tf_op jit(solution)/shard_map/pallas_call | solution.py:812
  26.4 2.3 %collective-permute-start.7 = (f32[3,8,128]{2,1,0:T(8,128)S(1)}, f32[3,8,128]{2,1,0:T(8,128)S(1)}, u32[]{:S(2)}, u32[]{:S(2)}) collective-permute-start(f32[3,8,128]{2,1,0:T(8,128)S(1)} %get-tuple-element.37.middle), channel_id=1, source_target_pairs={{0,4},{4,8},{8,12},{5,1},{9,5},{13,9},{12,13},{1,0},{2,6},{6,10},{... | collective-permute-start | bytes 36872 | tf_op jit(solution)/shard_map/ppermute | solution.py:809
  28.7 1.4 %shard_map.146.near = f32[8,128]{1,0:T(8,128)S(1)} custom-call(f32[3,32,128]{2,1,0:T(8,128)S(1)} %get-tuple-element.38.weighted, s32[10,8,128]{2,1,0:T(8,128)S(1)} %get-tuple-element.28.index, f32[30,8,128]{2,1,0:T(8,128)S(1)} %get-tuple-element.39.coupled), custom_call_target="tpu_custom_call" | custom-call | flops 1048576 | bytes 65536 | tf_op jit(solution)/shard_map/pallas_call | solution.py:812
  30.1 0.0 collective-permute-done.7.mine
  30.1 0.1 collective-permute-start.8
  30.2 1.2 %collective-permute-done.8.other = f32[3,8,128]{2,1,0:T(8,128)S(1)} collective-permute-done((f32[3,8,128]{2,1,0:T(8,128)S(1)}, f32[3,8,128]{2,1,0:T(8,128)S(1)}, u32[]{:S(2)}, u32[]{:S(2)}) %collective-permute-start.8) | collective-permute-done | bytes 12320 | tf_op jit(solution)/shard_map/ppermute | solution.py:803
  31.4 0.6 %shard_map.147 = (f32[8,128]{1,0:T(8,128)S(1)}, f32[16,4,128]{2,1,0:T(4,128)S(1)}) custom-call(f32[8,128]{1,0:T(8,128)S(1)} %shard_map.146.near, f32[3,8,128]{2,1,0:T(8,128)S(1)} %collective-permute-done.7.mine, f32[3,8,128]{2,1,0:T(8,128)S(1)} %collective-permute-done.8.other, f32[3,8,128]{2,1,0:T(8,128)S(1)} %get-tuple-element.37.middle, ...), custom_call_target="tpu_custom_call" | custom-call | flops 1048576 | bytes 65536 | tf_op jit(solution)/shard_map/pallas_call | solution.py:812
  32.0 13.0 %all_to_all.5.sums = f32[16,4,128]{2,1,0:T(4,128)S(1)} all-to-all(f32[16,4,128]{2,1,0:T(4,128)S(1)} %get-tuple-element.42), channel_id=1, replica_groups=mesh['groups'=2,'dom'=4,'sub'=2,'field'=2] {'dom','sub','field'}, dimensions={0} | all-to-all | bytes 65536 | tf_op jit(solution)/shard_map/all_to_all | solution.py:1052
  45.0 0.7 %shard_map.148 = (f32[8,128]{1,0:T(8,128)}, f32[8,128]{1,0:T(8,128)}, f32[8,128]{1,0:T(8,128)}) custom-call(f32[16,4,128]{2,1,0:T(4,128)S(1)} %all_to_all.5.sums, f32[8,128]{1,0:T(8,128)S(1)} %get-tuple-element.43.hess, f32[5,8,128]{2,1,0:T(8,128)S(1)} %get-tuple-element.30.vectors), custom_call_target="tpu_custom_call" | custom-call | tf_op jit(solution)/shard_map/pallas_call | solution.py:1054
  (4 shorter events, 0.0 us)
Async XLA Ops:
  0.6 5.4 %copy-start.5 = (f32[1024]{0:T(1024)S(1)}, f32[1024]{0:T(1024)}, u32[]{:S(2)}) copy-start(f32[1024]{0:T(1024)} %param.16) | copy-start | bytes 12292
  0.6 5.4 %copy-start.6 = (f32[1024]{0:T(1024)S(1)}, f32[1024]{0:T(1024)}, u32[]{:S(2)}) copy-start(f32[1024]{0:T(1024)} %param.20) | copy-start | bytes 12292
  0.7 5.4 %copy-start.7 = (f32[1024]{0:T(1024)S(1)}, f32[1024]{0:T(1024)}, u32[]{:S(2)}) copy-start(f32[1024]{0:T(1024)} %param.19) | copy-start | bytes 12292
  0.7 5.4 %copy-start.8 = (f32[1024]{0:T(1024)S(1)}, f32[1024]{0:T(1024)}, u32[]{:S(2)}) copy-start(f32[1024]{0:T(1024)} %param.18) | copy-start | bytes 12292
  0.7 5.4 %copy-start.9 = (f32[1024]{0:T(1024)S(1)}, f32[1024]{0:T(1024)}, u32[]{:S(2)}) copy-start(f32[1024]{0:T(1024)} %param.17) | copy-start | bytes 12292
  0.7 8.8 %copy-start.2 = (s32[10,1024]{1,0:T(8,128)S(1)}, s32[10,1024]{1,0:T(8,128)}, u32[]{:S(2)}) copy-start(s32[10,1024]{1,0:T(8,128)} %connect.1) | copy-start | bytes 122884
  2.4 7.1 %copy-start = (f32[3,4096]{1,0:T(4,128)S(1)}, f32[3,4096]{1,0:T(4,128)}, u32[]{:S(2)}) copy-start(f32[3,4096]{1,0:T(4,128)} %background.3) | copy-start | bytes 147460
  2.4 5.0 %collective-permute-start = (f32[6,8,128]{2,1,0:T(8,128)}, f32[6,8,128]{2,1,0:T(8,128)S(1)}, u32[]{:S(2)}, u32[]{:S(2)}) collective-permute-start(f32[6,8,128]{2,1,0:T(8,128)} %shard_map.139.pack), channel_id=1, source_target_pairs={{0,2},{2,0},{1,3},{3,1},{4,6},{6,4},{5,7},{7,5},{8,10},{10,8},{9,1... | collective-permute-start | bytes 73736 | tf_op jit(solution)/shard_map/ppermute | solution.py:806
  6.1 0.7 %copy-start.1 = (f32[6,8,128]{2,1,0:T(8,128)S(1)}, f32[6,8,128]{2,1,0:T(8,128)}, u32[]{:S(2)}) copy-start(f32[6,8,128]{2,1,0:T(8,128)} %shard_map.139.pack) | copy-start | bytes 73732
  7.4 3.6 %collective-permute-start.1 = (f32[3,8,128]{2,1,0:T(8,128)S(1)}, f32[3,8,128]{2,1,0:T(8,128)S(1)}, u32[]{:S(2)}, u32[]{:S(2)}) collective-permute-start(f32[3,8,128]{2,1,0:T(8,128)S(1)} %shard_map.141), channel_id=1, source_target_pairs={{0,4},{4,8},{8,12},{5,1},{9,5},{13,9},{12,13},{1,0},{2,6},{6,10},{... | collective-permute-start | bytes 36872 | tf_op jit(solution)/shard_map/ppermute | solution.py:809
  9.5 2.7 %copy-start.4 = (f32[30,30]{1,0:T(8,128)S(1)}, f32[30,30]{1,0:T(8,128)}, u32[]{:S(2)}) copy-start(f32[30,30]{1,0:T(8,128)} %stiff.1) | copy-start | bytes 10804
  11.0 1.2 %collective-permute-start.2 = (f32[3,8,128]{2,1,0:T(8,128)S(1)}, f32[3,8,128]{2,1,0:T(8,128)S(1)}, u32[]{:S(2)}, u32[]{:S(2)}) collective-permute-start(f32[3,8,128]{2,1,0:T(8,128)S(1)} %collective-permute-done.1.mine), channel_id=1, source_target_pairs={{0,1},{1,0},{2,3},{3,2},{4,5},{5,4},{6,7},{7,6},{8,9},{9,8},{10,11... | collective-permute-start | bytes 36872 | tf_op jit(solution)/shard_map/ppermute | solution.py:803
  15.4 1.3 %collective-permute-start.3 = (f32[3,40,128]{2,1,0:T(8,128)S(1)}, f32[3,40,128]{2,1,0:T(8,128)S(1)}, u32[]{:S(2)}, u32[]{:S(2)}) collective-permute-start(f32[3,40,128]{2,1,0:T(8,128)S(1)} %get-tuple-element.32), channel_id=1, source_target_pairs={{0,1},{1,0},{2,3},{3,2},{4,5},{5,4},{6,7},{7,6},{8,9},{9,8},{10,11... | collective-permute-start | bytes 184328 | tf_op jit(solution)/shard_map/ppermute | solution.py:803
  16.7 3.5 %collective-permute-start.4 = (f32[3,8,128]{2,1,0:T(8,128)S(1)}, f32[3,8,128]{2,1,0:T(8,128)S(1)}, u32[]{:S(2)}, u32[]{:S(2)}) collective-permute-start(f32[3,8,128]{2,1,0:T(8,128)S(1)} %slice_add_fusion), channel_id=1, source_target_pairs={{0,4},{4,8},{8,12},{5,1},{9,5},{13,9},{12,13},{1,0},{2,6},{6,10},{... | collective-permute-start | bytes 36872 | tf_op jit(solution)/shard_map/ppermute | solution.py:809
  20.3 5.3 %copy-start.3 = (f32[4096]{0:T(1024)S(1)}, f32[4096]{0:T(1024)}, u32[]{:S(2)}) copy-start(f32[4096]{0:T(1024)} %param.13) | copy-start | bytes 49156
  20.3 1.2 %collective-permute-start.5 = (f32[3,8,128]{2,1,0:T(8,128)S(1)}, f32[3,8,128]{2,1,0:T(8,128)S(1)}, u32[]{:S(2)}, u32[]{:S(2)}) collective-permute-start(f32[3,8,128]{2,1,0:T(8,128)S(1)} %collective-permute-done.4.mine), channel_id=1, source_target_pairs={{0,1},{1,0},{2,3},{3,2},{4,5},{5,4},{6,7},{7,6},{8,9},{9,8},{10,11... | collective-permute-start | bytes 36872 | tf_op jit(solution)/shard_map/ppermute | solution.py:803
  21.4 4.1 %collective-permute-start.6 = (f32[12,8,128]{2,1,0:T(8,128)S(1)}, f32[12,8,128]{2,1,0:T(8,128)S(1)}, u32[]{:S(2)}, u32[]{:S(2)}) collective-permute-start(f32[12,8,128]{2,1,0:T(8,128)S(1)} %pad_maximum_fusion), channel_id=1, source_target_pairs={{0,2},{2,0},{1,3},{3,1},{4,6},{6,4},{5,7},{7,5},{8,10},{10,8},{9,1... | collective-permute-start | bytes 147464 | tf_op jit(solution)/shard_map/ppermute | solution.py:806
  26.4 3.7 %collective-permute-start.7 = (f32[3,8,128]{2,1,0:T(8,128)S(1)}, f32[3,8,128]{2,1,0:T(8,128)S(1)}, u32[]{:S(2)}, u32[]{:S(2)}) collective-permute-start(f32[3,8,128]{2,1,0:T(8,128)S(1)} %get-tuple-element.37.middle), channel_id=1, source_target_pairs={{0,4},{4,8},{8,12},{5,1},{9,5},{13,9},{12,13},{1,0},{2,6},{6,10},{... | collective-permute-start | bytes 36872 | tf_op jit(solution)/shard_map/ppermute | solution.py:809
  30.1 1.2 %collective-permute-start.8 = (f32[3,8,128]{2,1,0:T(8,128)S(1)}, f32[3,8,128]{2,1,0:T(8,128)S(1)}, u32[]{:S(2)}, u32[]{:S(2)}) collective-permute-start(f32[3,8,128]{2,1,0:T(8,128)S(1)} %collective-permute-done.7.mine), channel_id=1, source_target_pairs={{0,1},{1,0},{2,3},{3,2},{4,5},{5,4},{6,7},{7,6},{8,9},{9,8},{10,11... | collective-permute-start | bytes 36872 | tf_op jit(solution)/shard_map/ppermute | solution.py:803

commit v4 on v3

--- a/solution.py
+++ b/solution.py
@@ -10,7 +10,7 @@
 BLK = 128
 LANES = 128
 SUBS = 8
-PARTS = 3
+PARTS = 2
 UNROLL = 10
 SUMS = 4
 LANE_BITS = 7
@@ -51,9 +51,9 @@
         lax.fori_loop(0, index.shape[0], step, 0, unroll=min(2 if rows > 16 else 5, index.shape[0]))
 
 
-def split_parts(value):
+def split_parts(value, count=PARTS):
     pieces = []
-    for _ in range(PARTS - 1):
+    for _ in range(count - 1):
         piece = value.astype(jnp.bfloat16).astype(jnp.float32)
         pieces.append(piece)
         value = value - piece
@@ -182,13 +182,17 @@
     forward_terms(stiff, state, coupled, vectors, pieces)
 
 
-def element_vectors(live, scale, others, vectors):
-    direction, residual, iterate, reg = others
+def live_mask(blocks):
     element = (
         lax.broadcasted_iota(jnp.int32, (SUBS, LANES), 0) * LANES
         + lax.broadcasted_iota(jnp.int32, (SUBS, LANES), 1)
     )
-    mask = (element < BLK * live[0]).astype(jnp.float32)
+    return (element < BLK * blocks).astype(jnp.float32)
+
+
+def element_vectors(live, scale, others, vectors):
+    direction, residual, iterate, reg = others
+    mask = live_mask(live[0])
     search = mask * direction[...]
     vectors[0] = search
     vectors[1] = mask * residual[...]
@@ -439,67 +443,41 @@
             table[c, r : r + 1, :] = source[c : c + 1, r * LANES : (r + 1) * LANES]
 
 
-def pair_start_kernel(counts, nodes, background, obs, pack, index, spots, table):
-    sub = lax.axis_index("sub")
+def link_line(nodes, o, k, h):
+    zero = nodes[0, o, 0:1, h * LANES : (h + 1) * LANES]
+    one = nodes[0, o, 1:2, h * LANES : (h + 1) * LANES]
+    return jnp.where((lax.axis_index("sub") ^ k) == 0, zero, one)
+
+
+def link_limit(counts, o, k):
+    return counts[0, lax.axis_index("sub") ^ k, o]
+
+
+def link_tile(nodes, tile, links):
+    tile[0] = jnp.zeros((SUBS, LANES), jnp.int32)
+    for i, (o, k) in enumerate(links):
+        for h in range(2):
+            tile[0, 2 * i + h : 2 * i + h + 1, :] = link_line(nodes, o, k, h)
+
+
+def pair_start_kernel(counts, nodes, background, out, index, table):
     step = jnp.where(lax.axis_index("field") == 0, 2, 0)
+    links = ((step, 0), (step, 1), (1, 1))
     own_table(background, table)
-    table[3] = obs[...]
+    link_tile(nodes, index, links)
     row = lax.broadcasted_iota(jnp.int32, (SUBS, LANES), 0)
     slot = lax.broadcasted_iota(jnp.int32, (SUBS, LANES), 1) + row % 2 * LANES
-
-    def line(o, k, h):
-        zero = nodes[0, o, 0:1, h * LANES : (h + 1) * LANES]
-        one = nodes[0, o, 1:2, h * LANES : (h + 1) * LANES]
-        return jnp.where((sub ^ k) == 0, zero, one)
-
-    def gate(links):
-        limit = jnp.zeros((SUBS, LANES), jnp.int32)
-        for i, (o, k) in enumerate(links):
-            limit = jnp.where(row // 2 == i, counts[0, sub ^ k, o], limit)
-        return slot < limit
-
-    value_links = ((step, 0), (step, 1), (1, 1))
-    weight_links = ((0, 1), (1, 1), (2, 1))
-    for tile, links in ((index, value_links), (spots, weight_links)):
-        tile[0] = jnp.zeros((SUBS, LANES), jnp.int32)
-        for i, (o, k) in enumerate(links):
-            for h in range(2):
-                tile[0, 2 * i + h : 2 * i + h + 1, :] = line(o, k, h)
-    value_gate = gate(value_links)
+    limit = jnp.zeros((SUBS, LANES), jnp.int32)
+    for i, (o, k) in enumerate(links):
+        limit = jnp.where(row // 2 == i, link_limit(counts, o, k), limit)
 
     def keep(tile, c, value):
-        pack[c] = jnp.where(value_gate, value, 0.0)
+        out[c] = jnp.where(slot < limit, value, 0.0)
 
     lookup(table, table.shape[1], index, keep)
 
-    def keep_weight(tile, c, value):
-        pack[5] = value
-
-    lookup(table.at[3:4], table.shape[1], spots, keep_weight, comps=1)
-    pack[3] = jnp.full((SUBS, LANES), -1.0, jnp.float32)
-    pack[4] = jnp.full((SUBS, LANES), -1.0, jnp.float32)
-    lane = lax.broadcasted_iota(jnp.int32, (1, LANES), 1)
-    for o in range(3):
-        for k in range(2):
-            for h in range(2):
-                at = (o * 2 + k) * 2 + h
-                here = lane + h * LANES < counts[0, sub ^ k, o]
-                pack[3 + at // SUBS, at % SUBS : at % SUBS + 1, :] = jnp.where(
-                    here, line(o, k, h), -1
-                ).astype(jnp.float32)
-
-
-def pair_vector_kernel(
-    live, pack, scale, direction, residual, iterate, reg, near, vectors
-):
-    element_vectors(live, scale, (direction, residual, iterate, reg), vectors)
-    near[...] = pack[...]
-
-
-def pair_join_kernel(near, sibling, out):
-    row = lax.broadcasted_iota(jnp.int32, (SUBS, LANES), 0)
-    for c in range(3):
-        out[c] = jnp.where(row < 2, near[c], sibling[c])
+
+BLOCKS = ((0, 0), (0, 1), (1, 0), (0, 2), (1, 1), (2, 0))
 
 
 def pair_ghosts(dom_count, mine, other, middle, table):
@@ -516,7 +494,35 @@
         table[c, 8:12, :] = above[0:4, :]
 
 
-def pair_own_kernel(link_slots, background, connect, index, partial, table):
+def pair_join_kernel(straight, slanted, out):
+    for c in range(3):
+        out[c, 0:4, :] = straight[c, 0:4, :]
+        out[c, 4:8, :] = slanted[c, 0:4, :]
+
+
+def pair_own_kernel(
+    link_slots,
+    background,
+    connect,
+    stiff,
+    live,
+    scale,
+    direction,
+    index,
+    partial,
+    wide,
+    marks,
+    table,
+):
+    mask = live_mask(live[...])
+    marks[0] = mask * direction[...]
+    marks[1] = mask
+    marks[2] = mask * scale[...]
+    wide[...] = jnp.zeros_like(wide)
+    size = stiff.shape[0]
+    split = split_parts(stiff[...], 3)
+    for i, (piece, _) in enumerate(BLOCKS):
+        wide[0:size, i * 32 : i * 32 + size] = split[piece]
     sub = lax.axis_index("sub")
     own_table(background, table)
     load_index(connect, index)
@@ -533,13 +539,13 @@
 
 def pair_forward_kernel(
     dom_count,
-    stiff,
+    wide,
     partial,
     index,
     mine,
     other,
     middle,
-    vectors,
+    marks,
     coupled,
     kept,
     sent,
@@ -555,10 +561,36 @@
         return partial[c * 10 + k]
 
     def keep(k, c, value):
-        state[c * 10 + k] = value
+        at = pl.multiple_of((c * 10 + k) * SUBS, SUBS)
+        state[0, pl.ds(at, SUBS), :] = value
 
     lookup(ghosts, 12, index, keep, begin, 2 * owned_high)
-    forward_terms(stiff, state, coupled, vectors, pieces)
+    spare = state.shape[1] - 30 * SUBS
+    state[0, 30 * SUBS :, :] = jnp.zeros((spare, LANES), jnp.float32)
+    weights = wide[...].astype(jnp.bfloat16)
+    for b in range(0, SUBS, 2):
+        lines = jnp.concatenate(
+            [state[0, pl.ds(b + i, 32, stride=SUBS), :] for i in range(2)], axis=1
+        )
+        split = [x.astype(jnp.bfloat16) for x in split_parts(lines, 3)]
+        product = lax.dot_general(
+            weights,
+            jnp.concatenate([split[his] for _, his in BLOCKS], axis=0),
+            (((1,), (0,)), ((), ())),
+            preferred_element_type=jnp.float32,
+        )
+        for i in range(2):
+            state[1, pl.ds(b + i, 32, stride=SUBS), :] = product[
+                :, i * LANES : (i + 1) * LANES
+            ]
+    search, factor = marks[0], marks[2]
+    for c in range(3):
+        for k in range(10):
+            at = (c * 10 + k) * SUBS
+            result = factor * state[1, at : at + SUBS, :]
+            coupled[c * 10 + k] = result
+            for part, piece in enumerate(split_parts(search * result)):
+                pieces[part * 3 + c, k] = piece
     width = 2 * LANES
     assemble(pieces, index, total, owned_high, SUBS, width)
     first = lax.axis_index("field") == 0
@@ -581,31 +613,43 @@
                 out[c, base + 6 + h : base + 7 + h, :] = jnp.zeros((1, LANES), jnp.float32)
 
 
-def node_tile(links, tile):
-    values = tile.astype(jnp.int32)
-    return jnp.maximum(values, 0), values >= 0
-
-
-def pair_sum_kernel(kept, came, pack, own, part, index, table):
+def pair_sum_kernel(
+    counts, nodes, obs, kept, came, own, link, index, table, weights
+):
+    part, fixed = link.at[0:3], link.at[3:6]
     rows = own.shape[1]
     half = rows // 2
     for c in range(3):
-        both = kept[c] + came[c]
-        own[c] = both[:rows]
+        both = kept[c, 0:rows, :] + came[c, 0:rows, :]
+        own[c] = both
         for h in range(2):
             table[c, pl.ds(h, half, stride=2), :] = both[h * half : (h + 1) * half]
-        part[3 + c] = both[rows:]
-    index[0] = jnp.zeros((SUBS, LANES), jnp.int32)
-    for o in range(3):
-        for h in range(2):
-            at = (o * 2 + 1) * 2 + h
-            line = pack[3 + at // SUBS, at % SUBS : at % SUBS + 1, :].astype(jnp.int32)
-            index[0, 2 * o + h : 2 * o + h + 1, :] = jnp.maximum(line, 0)
+    link_tile(nodes, index, ((0, 1), (1, 1), (2, 1)))
+    weights[0] = obs[...]
 
     def keep(tile, c, value):
         part[c] = value
 
     lookup(table, rows, index, keep)
+    for c in range(3):
+        part[c, 6:8, :] = (
+            kept[c, rows + 4 : rows + 6, :] + came[c, rows + 4 : rows + 6, :]
+        )
+
+    def keep_weight(tile, c, value):
+        fixed[2] = value
+
+    lookup(weights, rows, index, keep_weight, comps=1)
+    fixed[1] = jnp.full((SUBS, LANES), -1.0, jnp.float32)
+    lane = lax.broadcasted_iota(jnp.int32, (1, LANES), 1)
+    for o in range(3):
+        for k in range(2):
+            for h in range(2):
+                at = (o * 2 + k) * 2 + h
+                here = lane + h * LANES < link_limit(counts, o, k)
+                fixed[at // SUBS, at % SUBS : at % SUBS + 1, :] = jnp.where(
+                    here, link_line(nodes, o, k, h), -1
+                ).astype(jnp.float32)
 
 
 def landing(nodes, lines, owned_high, width):
@@ -631,12 +675,10 @@
 def pair_owner_kernel(
     dom_count,
     own,
-    part,
+    link,
     mine,
     other,
     came,
-    pack,
-    sibling,
     obs,
     weighted,
     out,
@@ -654,36 +696,42 @@
         def line(k):
             def get(c, h):
                 at = 2 * k + h
-                a, b = here(c)[at : at + 1, :], there(c)[at : at + 1, :]
-                return jnp.where(inside, jnp.where(first, a, b), 0.0)
+                return jnp.where(
+                    inside, jnp.where(first, here(c, at), there(c, at)), 0.0
+                )
 
             return get
 
         return line
 
-    mine_at, other_at = (lambda c: mine[c]), (lambda c: other[c])
-    his_mine, his_other = (lambda c: came[6 + c]), (lambda c: came[9 + c])
+    def row_of(tiles, base, shift):
+        return lambda c, at: tiles[base + c, shift + at : shift + at + 1, :]
+
+    part, fixed, his_fixed = link.at[0:3], link.at[3:6], came.at[3:6]
     low, high = dom > 0, dom < dom_count - 1
+    mine_at, other_at = row_of(mine, 0, 0), row_of(other, 0, 0)
+    his_mine, his_other = row_of(mine, 0, 4), row_of(other, 0, 4)
     below = pick(mine_at, other_at, low)
     above = pick(other_at, mine_at, high)
     his_below = pick(his_mine, his_other, low)
     his_above = pick(his_other, his_mine, high)
+    own_middle, his_middle = row_of(part, 0, 6), row_of(came, 0, 6)
     own_lines = (
         ((0, 0), below(0)),
         ((0, 1), his_below(1)),
-        ((1, 1), lambda c, h: came[3 + c, 4 + h : 5 + h, :]),
+        ((1, 1), his_middle),
         ((2, 0), above(0)),
         ((2, 1), his_above(1)),
     )
     his_lines = (
         ((0, 0), his_below(0)),
         ((0, 1), below(1)),
-        ((1, 1), lambda c, h: part[3 + c, 4 + h : 5 + h, :]),
+        ((1, 1), own_middle),
         ((2, 0), his_above(0)),
         ((2, 1), above(1)),
     )
-    total[0] = landing(pack.at[3:5], own_lines, owned_high, width)
-    total[1] = landing(sibling.at[3:5], his_lines, owned_high, width)
+    total[0] = landing(fixed, own_lines, owned_high, width)
+    total[1] = landing(his_fixed, his_lines, owned_high, width)
     for c in range(3):
         landed = summed(total.at[0], c * owned_high, owned_high, owned_high)
         his = summed(total.at[1], c * owned_high, owned_high, owned_high)
@@ -699,17 +747,17 @@
 
     def node(tiles, o, k, h):
         at = (o * 2 + k) * 2 + h
-        return tiles[3 + at // SUBS, at % SUBS : at % SUBS + 1, :].astype(jnp.int32)
+        return tiles[at // SUBS, at % SUBS : at % SUBS + 1, :].astype(jnp.int32)
 
     index[0] = jnp.full((SUBS, LANES), -1, jnp.int32)
     index[1] = jnp.zeros((SUBS, LANES), jnp.int32)
     shift = rows * LANES
     for h in range(2):
-        line = jnp.where(first, node(pack, 2, 0, h), node(pack, 0, 0, h))
+        line = jnp.where(first, node(fixed, 2, 0, h), node(fixed, 0, 0, h))
         index[0, h : h + 1, :] = line
         for at, line in (
-            (2, jnp.where(first, node(sibling, 2, 1, h), node(sibling, 0, 1, h))),
-            (4, node(sibling, 1, 1, h)),
+            (2, jnp.where(first, node(his_fixed, 2, 1, h), node(his_fixed, 0, 1, h))),
+            (4, node(his_fixed, 1, 1, h)),
         ):
             index[0, at + h : at + h + 1, :] = jnp.where(line < 0, line, line + shift)
     is_open = index[0] >= 0
@@ -724,7 +772,7 @@
         blank = jnp.zeros((2, LANES), jnp.float32)
         return jnp.concatenate([blank] + lines + [blank], axis=0)
 
-    weight = lined_up(sibling[5])
+    weight = lined_up(his_fixed[2])
 
     def keep(tile, c, value):
         value = jnp.where(row < 2, value, weight * (lined_up(came[c]) + value))
@@ -763,9 +811,13 @@
     middle,
     index,
     coupled,
-    vectors,
+    marks,
+    residual,
+    iterate,
+    reg,
     hess,
     sums,
+    vectors,
     ghosts,
     pulled,
 ):
@@ -778,9 +830,14 @@
     image = near[...]
     for i in range(30):
         image = image + coupled[i] * pulled[i]
-    image = image + vectors[3]
+    search, mask = marks[0], marks[1]
+    remain = mask * residual[...]
+    image = image + reg[...] * search
     hess[...] = image
-    write_sums(vectors[0], vectors[1], image, sums)
+    vectors[0] = search
+    vectors[1] = remain
+    vectors[2] = mask * iterate[...]
+    write_sums(search, remain, image, sums)
 
 
 def pair_step(background, obs, connect, live_blocks, scale, others, nodes, counts, stiff):
@@ -794,9 +851,20 @@
     tile = (SUBS, LANES)
     swap = [(0, 1), (1, 0)]
     last = dom_count - 1
-    ring = [(2 * d, 2 * d + 2) for d in range(last)]
-    ring += [(2 * d + 3, 2 * d + 1) for d in range(last)]
-    ring += [(2 * last, 2 * last + 1), (1, 0)]
+
+    def core(d, t, f):
+        return (2 * d + t) * 2 + f
+
+    def ring(turn):
+        pairs = []
+        for t in range(2):
+            for d in range(last):
+                pairs.append((core(d, t, 0), core(d + 1, t ^ turn, 0)))
+                pairs.append((core(d + 1, t, 1), core(d, t ^ turn, 1)))
+            pairs.append((core(last, t, 0), core(last, t, 1)))
+            pairs.append((core(0, t, 1), core(0, t, 0)))
+        return pairs
+
     left_rows = 3 * PARTS * owned_high + up_to(3 * PARTS * SUBS, 16)
 
     def across(x):
@@ -805,8 +873,8 @@
     def beside(x):
         return lax.ppermute(x, "sub", swap)
 
-    def along(x):
-        return lax.ppermute(x, ("dom", "field"), ring)
+    def along(x, turn=0):
+        return lax.ppermute(x, ("dom", "sub", "field"), ring(turn))
 
     def call(kernel, outs, scratch, smem, args, params=PARAMS):
         return pl.pallas_call(
@@ -821,37 +889,31 @@
             ),
         )(*args)
 
-    pack = call(
+    packed = call(
         pair_start_kernel,
-        shape((6,) + tile, f32),
-        [
-            pltpu.VMEM((1,) + tile, i32),
-            pltpu.VMEM((1,) + tile, i32),
-            pltpu.VMEM((4, rows, LANES), f32),
-        ],
+        shape((3,) + tile, f32),
+        [pltpu.VMEM((1,) + tile, i32), pltpu.VMEM((3, rows, LANES), f32)],
         1,
-        (counts, nodes, background, obs),
+        (counts, nodes, background),
         None,
     )
-    sibling = beside(pack)
-    pack, vectors = call(
-        pair_vector_kernel,
-        (shape((6,) + tile, f32), shape((5,) + tile, f32)),
-        [],
-        1,
-        (live_blocks, pack, scale) + others,
-    )
-    mine = along(
-        call(pair_join_kernel, shape((3,) + tile, f32), [], 0, (pack, sibling))
-    )
-    index, partial = call(
+    straight, slanted, middle = along(packed), along(packed, 1), beside(packed)
+    direction, residual, iterate, reg = others
+    index, partial, wide, marks = call(
         functools.partial(pair_own_kernel, link_slots),
-        (shape((10,) + tile, i32), shape((30,) + tile, f32)),
+        (
+            shape((10,) + tile, i32),
+            shape((30,) + tile, f32),
+            shape((32, 32 * len(BLOCKS)), f32),
+            shape((3,) + tile, f32),
+        ),
         [pltpu.VMEM((3, rows, LANES), f32)],
         0,
-        (background, connect),
-    )
-    mine, partial = lax.optimization_barrier((mine, partial))
+        (background, connect, stiff, live_blocks.reshape(1, 1), scale, direction),
+    )
+    straight, partial = lax.optimization_barrier((straight, partial))
+    upper = lax.broadcasted_iota(i32, (3,) + tile, 1) < 2
+    mine = jnp.where(upper, straight, slanted)
     other = across(mine)
     coupled, kept, sent = call(
         functools.partial(pair_forward_kernel, dom_count),
@@ -862,25 +924,33 @@
         ),
         [
             pltpu.VMEM((3, 16, LANES), f32),
-            pltpu.VMEM((30,) + tile, f32),
+            pltpu.VMEM((2, 32 * SUBS, LANES), f32),
             pltpu.VMEM((3 * PARTS, 10) + tile, f32),
             pltpu.VMEM((left_rows, link_slots), f32),
         ],
-        1,
-        (stiff, partial, index, mine, other, sibling, vectors),
+        0,
+        (wide, partial, index, mine, other, middle, marks),
     )
     came = across(sent)
-    mine = along(kept[:, rows:] + came[:, rows:])
-    own, part = call(
+    linked = kept[:, rows:] + came[:, rows:]
+    straight, slanted = along(linked), along(linked, 1)
+    own, link = call(
         pair_sum_kernel,
         (shape((3, rows, LANES), f32), shape((6,) + tile, f32)),
-        [pltpu.VMEM((1,) + tile, i32), pltpu.VMEM((3, rows, LANES), f32)],
-        0,
-        (kept, came, pack),
-    )
-    mine, part = lax.optimization_barrier((mine, part))
+        [
+            pltpu.VMEM((1,) + tile, i32),
+            pltpu.VMEM((3, rows, LANES), f32),
+            pltpu.VMEM((1, rows, LANES), f32),
+        ],
+        1,
+        (counts, nodes, obs, kept, came),
+    )
+    straight, link = lax.optimization_barrier((straight, link))
+    came = beside(link)
+    mine = call(
+        pair_join_kernel, shape((3,) + tile, f32), [], 0, (straight, slanted)
+    )
     other = across(mine)
-    came = beside(jnp.concatenate([part, mine, other], axis=0))
     weighted, outbound = call(
         functools.partial(pair_owner_kernel, dom_count),
         (shape((3, rows, LANES), f32), shape((3,) + tile, f32)),
@@ -890,24 +960,28 @@
             pltpu.VMEM((3, 2 * rows, LANES), f32),
         ],
         0,
-        (own, part, mine, other, came, pack, sibling, obs),
+        (own, link, mine, other, came, obs),
     )
     mine = along(outbound)
-    near = call(
+    inner = call(
         pair_near_kernel,
         shape(tile, f32),
         [pltpu.VMEM((30,) + tile, f32)],
         0,
         (weighted, index, coupled),
     )
-    mine, near = lax.optimization_barrier((mine, near))
+    mine, inner = lax.optimization_barrier((mine, inner))
     other = across(mine)
-    hess, sums = call(
+    hess, sums, vectors = call(
         functools.partial(pair_adjoint_kernel, dom_count, rows),
-        (shape(tile, f32), shape((4 * dom_count, SUMS, LANES), f32)),
+        (
+            shape(tile, f32),
+            shape((4 * dom_count, SUMS, LANES), f32),
+            shape((3,) + tile, f32),
+        ),
         [pltpu.VMEM((3, 16, LANES), f32), pltpu.VMEM((30,) + tile, f32)],
         0,
-        (near, mine, other, outbound, index, coupled, vectors),
+        (inner, mine, other, outbound, index, coupled, marks, residual, iterate, reg),
     )
     return hess, sums, vectors
 

time: 45.9 us -> 42.2 us (0.919)
  waiting for transfers between devices: 8.97 us -> 6.69 us
  blocking collectives: 13 us -> 11.2 us
    all_to_all x1, blocking collectives: 13 us -> 11.2 us  [on_device(): sums = lax.all_to_all(sums, cores, 0, 0, tiled=True)]
    ppermute x3 -> x5, waiting for transfers between devices: 1.23 us -> 0.01 us  [along(): return lax.ppermute(x, ('dom', 'sub', 'field'), ring(turn))]
    ppermute x2, waiting for transfers between devices: 3.15 us -> 2.1 us  [beside(): return lax.ppermute(x, 'sub', swap)]
    ppermute x3 -> x5, starting transfers between devices: 6.55 us -> 7.56 us  [along(): return lax.ppermute(x, ('dom', 'sub', 'field'), ring(turn))]
    ppermute x2, starting transfers between devices: 4.47 us -> 3.57 us  [beside(): return lax.ppermute(x, 'sub', swap)]
    pallas_call x9 -> x8, Pallas kernels: 9.41 us -> 9.41 us  [call(): pl.pallas_call(kernel, compiler_params=params, out_shape=outs, in_specs=[...]
  transfers between devices with their start and end apart: 9 -> 11, of which waited for: 7 -> 5; matrix products, arithmetic and copies ran while one was open for 0% -> 0% of each run, Pallas kernels for 7% -> 9%
where the time goes in v4:
time: 42.2 us; the launch traced here: 41.9 us
  starting transfers between devices  11.5 us (27%)
  blocking collectives  11.2 us (27%)
  Pallas kernels  10.1 us (24%)
  waiting for transfers between devices  6.69 us (16%)
  between operations  1.49 us (4%)
  local copies, waits for them, and re-layouts  0.88 us (2%)
    all_to_all x1, blocking collectives, on_device(): sums = lax.all_to_all(sums, cores, 0, 0, tiled=True)  11.2 us
    pallas_call x8, Pallas kernels, call(): pl.pallas_call(kernel, compiler_params=params, out_shape=outs, in_specs=[...  9.41 us
    ppermute x5, starting transfers between devices, along(): return lax.ppermute(x, ('dom', 'sub', 'field'), ring(turn))  7.56 us
    ppermute x4, waiting for transfers between devices, across(): return lax.ppermute(x, 'field', swap)  4.57 us
    ppermute x2, starting transfers between devices, beside(): return lax.ppermute(x, 'sub', swap)  3.57 us
    ppermute x2, waiting for transfers between devices, beside(): return lax.ppermute(x, 'sub', swap)  2.1 us
    unnamed x22, local copies, waits for them, and re-layouts  0.88 us
  transfers between devices with their start and end apart: 11, of which 5 were waited for; matrix products, arithmetic and copies ran while one was open for 0% of the time, Pallas kernels for 9%

profile of v4, /device:TPU:0, one launch (start us, length us, event | category | flops | bytes accessed | tf_op | source)
XLA Modules:
  0.0 41.9 jit_solution(15549489205688938858)
XLA Ops:
  0.6 0.0 copy-start
  0.6 0.0 copy-start.4
  0.6 1.7 %shard_map.140 = f32[3,8,128]{2,1,0:T(8,128)} custom-call(s32[1,2,3]{2,1,0:T(2,128)} %bitcast.17, s32[1,3,2,256]{3,2,1,0:T(2,128)} %nodes.3, f32[3,4096]{1,0:T(4,128)} %background.3), custom_call_target="tpu_custom_call" | custom-call | flops 1048576 | bytes 65536 | tf_op jit(solution)/shard_map/pallas_call | solution.py:880
  2.3 3.0 %collective-permute-start.3 = (f32[3,8,128]{2,1,0:T(8,128)}, f32[3,8,128]{2,1,0:T(8,128)S(1)}, u32[]{:S(2)}, u32[]{:S(2)}) collective-permute-start(f32[3,8,128]{2,1,0:T(8,128)} %shard_map.140), channel_id=1, source_target_pairs={{0,2},{2,0},{1,3},{3,1},{4,6},{6,4},{5,7},{7,5},{8,10},{10,8},{9,1... | collective-permute-start | bytes 36872 | tf_op jit(solution)/shard_map/ppermute | solution.py:874
  5.3 1.5 %collective-permute-start.1 = (f32[3,8,128]{2,1,0:T(8,128)}, f32[3,8,128]{2,1,0:T(8,128)S(1)}, u32[]{:S(2)}, u32[]{:S(2)}) collective-permute-start(f32[3,8,128]{2,1,0:T(8,128)} %shard_map.140), channel_id=1, source_target_pairs={{0,6},{5,3},{4,10},{9,7},{8,14},{13,11},{12,13},{1,0},{2,4},{7,1},... | collective-permute-start | bytes 36872 | tf_op jit(solution)/shard_map/ppermute | solution.py:877
  6.9 1.6 %collective-permute-start = (f32[3,8,128]{2,1,0:T(8,128)}, f32[3,8,128]{2,1,0:T(8,128)S(1)}, u32[]{:S(2)}, u32[]{:S(2)}) collective-permute-start(f32[3,8,128]{2,1,0:T(8,128)} %shard_map.140), channel_id=1, source_target_pairs={{0,4},{5,1},{4,8},{9,5},{8,12},{13,9},{12,13},{1,0},{2,6},{7,3},{6... | collective-permute-start | bytes 36872 | tf_op jit(solution)/shard_map/ppermute | solution.py:877
  9.1 0.0 copy-done
  9.1 0.0 copy-done.4
  9.1 0.0 copy-done.10
  9.1 0.0 copy-done.9
  9.2 0.0 copy-start.2
  9.2 0.8 %copy-done.2 = s32[10,1024]{1,0:T(8,128)S(1)} copy-done((s32[10,1024]{1,0:T(8,128)S(1)}, s32[10,1024]{1,0:T(8,128)}, u32[]{:S(2)}) %copy-start.2) | copy-done | bytes 40984
  10.0 1.5 %shard_map.139 = (s32[10,8,128]{2,1,0:T(8,128)S(1)}, f32[30,8,128]{2,1,0:T(8,128)S(1)}, f32[32,192]{1,0:T(8,128)S(1)}, f32[3,8,128]{2,1,0:T(8,128)S(1)}) custom-call(f32[3,4096]{1,0:T(4,128)S(1)} %copy-done, s32[10,1024]{1,0:T(8,128)S(1)} %copy-done.2, f32[30,30]{1,0:T(8,128)S(1)} %copy-done.4, s32[1,1]{1,0:T(1,128)} %bitcast.11.live, ...), custom_call_target="tpu_custom_call" | custom-call | flops 1048576 | bytes 65536 | tf_op jit(solution)/shard_map/pallas_call | solution.py:880
  11.5 0.0 collective-permute-done
  11.5 0.0 collective-permute-done.1
  11.5 0.1 broadcast_select_fusion.mine
  11.6 0.0 collective-permute-start.2
  11.6 0.0 collective-permute-done.3.middle
  11.6 1.2 %collective-permute-done.2.other = f32[3,8,128]{2,1,0:T(8,128)S(1)} collective-permute-done((f32[3,8,128]{2,1,0:T(8,128)S(1)}, f32[3,8,128]{2,1,0:T(8,128)S(1)}, u32[]{:S(2)}, u32[]{:S(2)}) %collective-permute-start.2) | collective-permute-done | bytes 12320 | tf_op jit(solution)/shard_map/ppermute | solution.py:871
  12.8 2.6 %shard_map.141 = (f32[30,8,128]{2,1,0:T(8,128)S(1)}, f32[3,40,128]{2,1,0:T(8,128)S(1)}, f32[3,40,128]{2,1,0:T(8,128)S(1)}) custom-call(f32[32,192]{1,0:T(8,128)S(1)} %get-tuple-element.26.wide, f32[30,8,128]{2,1,0:T(8,128)S(1)} %get-tuple-element.28.partial, s32[10,8,128]{2,1,0:T(8,128)S(1)} %get-tuple-element.29.index, ...), custom_call_target="tpu_custom_call" | custom-call | flops 1048576 | bytes 65536 | tf_op jit(solution)/shard_map/pallas_call | solution.py:880
  15.4 0.2 collective-permute-start.4
  15.6 1.1 %collective-permute-done.4.came = f32[3,40,128]{2,1,0:T(8,128)S(1)} collective-permute-done((f32[3,40,128]{2,1,0:T(8,128)S(1)}, f32[3,40,128]{2,1,0:T(8,128)S(1)}, u32[]{:S(2)}, u32[]{:S(2)}) %collective-permute-start.4) | collective-permute-done | bytes 61472 | tf_op jit(solution)/shard_map/ppermute | solution.py:871
  16.7 0.0 copy-start.8
  16.7 1.6 %collective-permute-start.5 = (f32[3,8,128]{2,1,0:T(8,128)S(1)}, f32[3,8,128]{2,1,0:T(8,128)S(1)}, u32[]{:S(2)}, u32[]{:S(2)}) collective-permute-start(f32[3,8,128]{2,1,0:T(8,128)S(1)} %slice_add_fusion), channel_id=1, source_target_pairs={{0,4},{5,1},{4,8},{9,5},{8,12},{13,9},{12,13},{1,0},{2,6},{7,3},{6... | collective-permute-start | bytes 36872 | tf_op jit(solution)/shard_map/ppermute | solution.py:877
  18.3 1.8 %collective-permute-start.6 = (f32[3,8,128]{2,1,0:T(8,128)S(1)}, f32[3,8,128]{2,1,0:T(8,128)S(1)}, u32[]{:S(2)}, u32[]{:S(2)}) collective-permute-start(f32[3,8,128]{2,1,0:T(8,128)S(1)} %slice_add_fusion), channel_id=1, source_target_pairs={{0,6},{5,3},{4,10},{9,7},{8,14},{13,11},{12,13},{1,0},{2,4},{7,1},... | collective-permute-start | bytes 36872 | tf_op jit(solution)/shard_map/ppermute | solution.py:877
  20.1 0.0 copy-done.1
  20.1 0.0 copy-done.3
  20.1 0.0 copy-done.8
  20.1 0.8 %shard_map.142 = (f32[3,32,128]{2,1,0:T(8,128)S(1)}, f32[6,8,128]{2,1,0:T(8,128)S(1)}) custom-call(s32[1,2,3]{2,1,0:T(2,128)S(1)} %bitcast.18, s32[1,3,2,256]{3,2,1,0:T(2,128)S(1)} %copy-done.3, f32[32,128]{1,0:T(8,128)S(1)} %bitcast.12, f32[3,40,128]{2,1,0:T(8,128)S(1)} %get-tuple-element.32.kept, f32[3,40,128]{2,1,0:T(8,128)S(1)} %collective-permute-done.4.came), custom_call_target="tpu_custom_call" | custom-call | flops 1048576 | bytes 65536 | tf_op jit(solution)/shard_map/pallas_call | solution.py:880
  20.9 0.0 collective-permute-done.5.straight
  20.9 0.6 %collective-permute-start.8 = (f32[6,8,128]{2,1,0:T(8,128)S(1)}, f32[6,8,128]{2,1,0:T(8,128)S(1)}, u32[]{:S(2)}, u32[]{:S(2)}) collective-permute-start(f32[6,8,128]{2,1,0:T(8,128)S(1)} %get-tuple-element.36.link), channel_id=1, source_target_pairs={{0,2},{2,0},{1,3},{3,1},{4,6},{6,4},{5,7},{7,5},{8,10},{10,8},{9,1... | collective-permute-start | bytes 73736 | tf_op jit(solution)/shard_map/ppermute | solution.py:874
  21.5 0.0 collective-permute-done.6.slanted
  21.5 0.0 collective-permute-start.7
  21.5 1.2 %collective-permute-done.7.other = f32[3,8,128]{2,1,0:T(8,128)S(1)} collective-permute-done((f32[3,8,128]{2,1,0:T(8,128)S(1)}, f32[3,8,128]{2,1,0:T(8,128)S(1)}, u32[]{:S(2)}, u32[]{:S(2)}) %collective-permute-start.7) | collective-permute-done | bytes 12320 | tf_op jit(solution)/shard_map/ppermute | solution.py:871
  22.7 2.1 %collective-permute-done.8.came = f32[6,8,128]{2,1,0:T(8,128)S(1)} collective-permute-done((f32[6,8,128]{2,1,0:T(8,128)S(1)}, f32[6,8,128]{2,1,0:T(8,128)S(1)}, u32[]{:S(2)}, u32[]{:S(2)}) %collective-permute-start.8) | collective-permute-done | bytes 24608 | tf_op jit(solution)/shard_map/ppermute | solution.py:874
  24.8 0.8 %shard_map.144 = (f32[3,32,128]{2,1,0:T(8,128)S(1)}, f32[3,8,128]{2,1,0:T(8,128)S(1)}) custom-call(f32[3,32,128]{2,1,0:T(8,128)S(1)} %get-tuple-element.34.own, f32[6,8,128]{2,1,0:T(8,128)S(1)} %get-tuple-element.36.link, f32[3,8,128]{2,1,0:T(8,128)S(1)} %shard_map.143.mine, f32[3,8,128]{2,1,0:T(8,128)S(1)} %collective-permute-done.7.other, ...), custom_call_target="tpu_custom_call" | custom-call | flops 1048576 | bytes 65536 | tf_op jit(solution)/shard_map/pallas_call | solution.py:880
  25.6 1.1 %collective-permute-start.9 = (f32[3,8,128]{2,1,0:T(8,128)S(1)}, f32[3,8,128]{2,1,0:T(8,128)S(1)}, u32[]{:S(2)}, u32[]{:S(2)}) collective-permute-start(f32[3,8,128]{2,1,0:T(8,128)S(1)} %get-tuple-element.38.middle), channel_id=1, source_target_pairs={{0,4},{5,1},{4,8},{9,5},{8,12},{13,9},{12,13},{1,0},{2,6},{7,3},{6... | collective-permute-start | bytes 36872 | tf_op jit(solution)/shard_map/ppermute | solution.py:877
  26.7 1.4 %shard_map.145.near = f32[8,128]{1,0:T(8,128)S(1)} custom-call(f32[3,32,128]{2,1,0:T(8,128)S(1)} %get-tuple-element.39.weighted, s32[10,8,128]{2,1,0:T(8,128)S(1)} %get-tuple-element.29.index, f32[30,8,128]{2,1,0:T(8,128)S(1)} %get-tuple-element.40.coupled), custom_call_target="tpu_custom_call" | custom-call | flops 1048576 | bytes 65536 | tf_op jit(solution)/shard_map/pallas_call | solution.py:880
  28.1 0.0 copy-start.5
  28.1 0.0 collective-permute-done.9.mine
  28.1 0.1 collective-permute-start.10
  28.2 1.2 %collective-permute-done.10.other = f32[3,8,128]{2,1,0:T(8,128)S(1)} collective-permute-done((f32[3,8,128]{2,1,0:T(8,128)S(1)}, f32[3,8,128]{2,1,0:T(8,128)S(1)}, u32[]{:S(2)}, u32[]{:S(2)}) %collective-permute-start.10) | collective-permute-done | bytes 12320 | tf_op jit(solution)/shard_map/ppermute | solution.py:871
  29.4 0.0 copy-done.6
  29.4 0.0 copy-done.7
  29.4 0.0 copy-done.5
  29.4 0.6 %shard_map.146 = (f32[8,128]{1,0:T(8,128)S(1)}, f32[16,4,128]{2,1,0:T(4,128)S(1)}, f32[3,8,128]{2,1,0:T(8,128)S(1)}) custom-call(f32[8,128]{1,0:T(8,128)S(1)} %shard_map.145.near, f32[3,8,128]{2,1,0:T(8,128)S(1)} %collective-permute-done.9.mine, f32[3,8,128]{2,1,0:T(8,128)S(1)} %collective-permute-done.10.other, f32[3,8,128]{2,1,0:T(8,128)S(1)} %get-tuple-element.38.middle, ...), custom_call_target="tpu_custom_call" | custom-call | flops 1048576 | bytes 65536 | tf_op jit(solution)/shard_map/pallas_call | solution.py:880
  30.0 11.2 %all_to_all.5.sums = f32[16,4,128]{2,1,0:T(4,128)S(1)} all-to-all(f32[16,4,128]{2,1,0:T(4,128)S(1)} %get-tuple-element.43), channel_id=1, replica_groups=mesh['groups'=2,'dom'=4,'sub'=2,'field'=2] {'dom','sub','field'}, dimensions={0} | all-to-all | bytes 65536 | tf_op jit(solution)/shard_map/all_to_all | solution.py:1126
  41.2 0.7 %shard_map.147 = (f32[8,128]{1,0:T(8,128)}, f32[8,128]{1,0:T(8,128)}, f32[8,128]{1,0:T(8,128)}) custom-call(f32[16,4,128]{2,1,0:T(4,128)S(1)} %all_to_all.5.sums, f32[8,128]{1,0:T(8,128)S(1)} %get-tuple-element.44.hess, f32[3,8,128]{2,1,0:T(8,128)S(1)} %get-tuple-element.45.vectors), custom_call_target="tpu_custom_call" | custom-call | tf_op jit(solution)/shard_map/pallas_call | solution.py:1128
  (9 shorter events, 0.0 us)
Async XLA Ops:
  0.6 8.5 %copy-start = (f32[3,4096]{1,0:T(4,128)S(1)}, f32[3,4096]{1,0:T(4,128)}, u32[]{:S(2)}) copy-start(f32[3,4096]{1,0:T(4,128)} %background.3) | copy-start | bytes 147460
  0.6 8.5 %copy-start.4 = (f32[30,30]{1,0:T(8,128)S(1)}, f32[30,30]{1,0:T(8,128)}, u32[]{:S(2)}) copy-start(f32[30,30]{1,0:T(8,128)} %stiff.1) | copy-start | bytes 10804
  2.3 9.2 %collective-permute-start.3 = (f32[3,8,128]{2,1,0:T(8,128)}, f32[3,8,128]{2,1,0:T(8,128)S(1)}, u32[]{:S(2)}, u32[]{:S(2)}) collective-permute-start(f32[3,8,128]{2,1,0:T(8,128)} %shard_map.140), channel_id=1, source_target_pairs={{0,2},{2,0},{1,3},{3,1},{4,6},{6,4},{5,7},{7,5},{8,10},{10,8},{9,1... | collective-permute-start | bytes 36872 | tf_op jit(solution)/shard_map/ppermute | solution.py:874
  5.3 6.2 %collective-permute-start.1 = (f32[3,8,128]{2,1,0:T(8,128)}, f32[3,8,128]{2,1,0:T(8,128)S(1)}, u32[]{:S(2)}, u32[]{:S(2)}) collective-permute-start(f32[3,8,128]{2,1,0:T(8,128)} %shard_map.140), channel_id=1, source_target_pairs={{0,6},{5,3},{4,10},{9,7},{8,14},{13,11},{12,13},{1,0},{2,4},{7,1},... | collective-permute-start | bytes 36872 | tf_op jit(solution)/shard_map/ppermute | solution.py:877
  6.9 4.6 %collective-permute-start = (f32[3,8,128]{2,1,0:T(8,128)}, f32[3,8,128]{2,1,0:T(8,128)S(1)}, u32[]{:S(2)}, u32[]{:S(2)}) collective-permute-start(f32[3,8,128]{2,1,0:T(8,128)} %shard_map.140), channel_id=1, source_target_pairs={{0,4},{5,1},{4,8},{9,5},{8,12},{13,9},{12,13},{1,0},{2,6},{7,3},{6... | collective-permute-start | bytes 36872 | tf_op jit(solution)/shard_map/ppermute | solution.py:877
  8.4 0.7 %copy-start.10 = (f32[1024]{0:T(1024)S(1)}, f32[1024]{0:T(1024)}, u32[]{:S(2)}) copy-start(f32[1024]{0:T(1024)} %param.20) | copy-start | bytes 12292
  8.4 0.7 %copy-start.9 = (f32[1024]{0:T(1024)S(1)}, f32[1024]{0:T(1024)}, u32[]{:S(2)}) copy-start(f32[1024]{0:T(1024)} %param.16) | copy-start | bytes 12292
  9.2 0.8 %copy-start.2 = (s32[10,1024]{1,0:T(8,128)S(1)}, s32[10,1024]{1,0:T(8,128)}, u32[]{:S(2)}) copy-start(s32[10,1024]{1,0:T(8,128)} %connect.1) | copy-start | bytes 122884
  11.6 1.2 %collective-permute-start.2 = (f32[3,8,128]{2,1,0:T(8,128)S(1)}, f32[3,8,128]{2,1,0:T(8,128)S(1)}, u32[]{:S(2)}, u32[]{:S(2)}) collective-permute-start(f32[3,8,128]{2,1,0:T(8,128)S(1)} %broadcast_select_fusion.mine), channel_id=1, source_target_pairs={{0,1},{1,0},{2,3},{3,2},{4,5},{5,4},{6,7},{7,6},{8,9},{9,8},{10,11... | collective-permute-start | bytes 36872 | tf_op jit(solution)/shard_map/ppermute | solution.py:871
  15.4 1.3 %collective-permute-start.4 = (f32[3,40,128]{2,1,0:T(8,128)S(1)}, f32[3,40,128]{2,1,0:T(8,128)S(1)}, u32[]{:S(2)}, u32[]{:S(2)}) collective-permute-start(f32[3,40,128]{2,1,0:T(8,128)S(1)} %get-tuple-element.33), channel_id=1, source_target_pairs={{0,1},{1,0},{2,3},{3,2},{4,5},{5,4},{6,7},{7,6},{8,9},{9,8},{10,11... | collective-permute-start | bytes 184328 | tf_op jit(solution)/shard_map/ppermute | solution.py:871
  16.7 3.4 %copy-start.1 = (f32[4096]{0:T(1024)S(1)}, f32[4096]{0:T(1024)}, u32[]{:S(2)}) copy-start(f32[4096]{0:T(1024)} %param.13) | copy-start | bytes 49156
  16.7 3.4 %copy-start.3 = (s32[1,3,2,256]{3,2,1,0:T(2,128)S(1)}, s32[1,3,2,256]{3,2,1,0:T(2,128)}, u32[]{:S(2)}) copy-start(s32[1,3,2,256]{3,2,1,0:T(2,128)} %nodes.3) | copy-start | bytes 18436
  16.7 3.4 %copy-start.8 = (s32[1,3,2]{1,2,0:T(2,128)S(1)}, s32[1,3,2]{1,2,0:T(2,128)}, u32[]{:S(2)}) copy-start(s32[1,3,2]{1,2,0:T(2,128)} %param.22) | copy-start | bytes 76
  16.7 4.2 %collective-permute-start.5 = (f32[3,8,128]{2,1,0:T(8,128)S(1)}, f32[3,8,128]{2,1,0:T(8,128)S(1)}, u32[]{:S(2)}, u32[]{:S(2)}) collective-permute-start(f32[3,8,128]{2,1,0:T(8,128)S(1)} %slice_add_fusion), channel_id=1, source_target_pairs={{0,4},{5,1},{4,8},{9,5},{8,12},{13,9},{12,13},{1,0},{2,6},{7,3},{6... | collective-permute-start | bytes 36872 | tf_op jit(solution)/shard_map/ppermute | solution.py:877
  18.3 3.2 %collective-permute-start.6 = (f32[3,8,128]{2,1,0:T(8,128)S(1)}, f32[3,8,128]{2,1,0:T(8,128)S(1)}, u32[]{:S(2)}, u32[]{:S(2)}) collective-permute-start(f32[3,8,128]{2,1,0:T(8,128)S(1)} %slice_add_fusion), channel_id=1, source_target_pairs={{0,6},{5,3},{4,10},{9,7},{8,14},{13,11},{12,13},{1,0},{2,4},{7,1},... | collective-permute-start | bytes 36872 | tf_op jit(solution)/shard_map/ppermute | solution.py:877
  20.9 3.9 %collective-permute-start.8 = (f32[6,8,128]{2,1,0:T(8,128)S(1)}, f32[6,8,128]{2,1,0:T(8,128)S(1)}, u32[]{:S(2)}, u32[]{:S(2)}) collective-permute-start(f32[6,8,128]{2,1,0:T(8,128)S(1)} %get-tuple-element.36.link), channel_id=1, source_target_pairs={{0,2},{2,0},{1,3},{3,1},{4,6},{6,4},{5,7},{7,5},{8,10},{10,8},{9,1... | collective-permute-start | bytes 73736 | tf_op jit(solution)/shard_map/ppermute | solution.py:874
  21.5 1.2 %collective-permute-start.7 = (f32[3,8,128]{2,1,0:T(8,128)S(1)}, f32[3,8,128]{2,1,0:T(8,128)S(1)}, u32[]{:S(2)}, u32[]{:S(2)}) collective-permute-start(f32[3,8,128]{2,1,0:T(8,128)S(1)} %shard_map.143.mine), channel_id=1, source_target_pairs={{0,1},{1,0},{2,3},{3,2},{4,5},{5,4},{6,7},{7,6},{8,9},{9,8},{10,11... | collective-permute-start | bytes 36872 | tf_op jit(solution)/shard_map/ppermute | solution.py:871
  25.6 2.5 %collective-permute-start.9 = (f32[3,8,128]{2,1,0:T(8,128)S(1)}, f32[3,8,128]{2,1,0:T(8,128)S(1)}, u32[]{:S(2)}, u32[]{:S(2)}) collective-permute-start(f32[3,8,128]{2,1,0:T(8,128)S(1)} %get-tuple-element.38.middle), channel_id=1, source_target_pairs={{0,4},{5,1},{4,8},{9,5},{8,12},{13,9},{12,13},{1,0},{2,6},{7,3},{6... | collective-permute-start | bytes 36872 | tf_op jit(solution)/shard_map/ppermute | solution.py:877
  26.7 2.7 %copy-start.6 = (f32[1024]{0:T(1024)S(1)}, f32[1024]{0:T(1024)}, u32[]{:S(2)}) copy-start(f32[1024]{0:T(1024)} %param.18) | copy-start | bytes 12292
  26.7 2.7 %copy-start.7 = (f32[1024]{0:T(1024)S(1)}, f32[1024]{0:T(1024)}, u32[]{:S(2)}) copy-start(f32[1024]{0:T(1024)} %param.17) | copy-start | bytes 12292
  28.1 1.3 %copy-start.5 = (f32[1024]{0:T(1024)S(1)}, f32[1024]{0:T(1024)}, u32[]{:S(2)}) copy-start(f32[1024]{0:T(1024)} %param.19) | copy-start | bytes 12292
  28.1 1.2 %collective-permute-start.10 = (f32[3,8,128]{2,1,0:T(8,128)S(1)}, f32[3,8,128]{2,1,0:T(8,128)S(1)}, u32[]{:S(2)}, u32[]{:S(2)}) collective-permute-start(f32[3,8,128]{2,1,0:T(8,128)S(1)} %collective-permute-done.9.mine), channel_id=1, source_target_pairs={{0,1},{1,0},{2,3},{3,2},{4,5},{5,4},{6,7},{7,6},{8,9},{9,8},{10,11... | collective-permute-start | bytes 36872 | tf_op jit(solution)/shard_map/ppermute | solution.py:871

commit v5 on v4

--- a/solution.py
+++ b/solution.py
@@ -17,6 +17,7 @@
 
 VMEM = pl.BlockSpec(memory_space=pltpu.VMEM)
 SMEM = pl.BlockSpec(memory_space=pltpu.SMEM)
+FIRST = None
 PARAMS = pltpu.CompilerParams(vmem_limit_bytes=16 * 2**20)
 
 
@@ -24,13 +25,15 @@
     return -(-count // step) * step
 
 
-def lookup(table, rows, index, store, begin=None, first=0, comps=3):
+def lookup(table, rows, index, store, begin=None, first=0, comps=3, skip=()):
     def one(tile):
         entry = index[tile]
         high = lax.shift_right_logical(entry, LANE_BITS)
         low = entry & (LANES - 1)
         found = [0.0 if begin is None else begin(tile, c) for c in range(comps)]
         for row in range(rows):
+            if row in skip:
+                continue
             here = high == first + row
             for c in range(comps):
                 line = jnp.broadcast_to(table[c, row : row + 1, :], (SUBS, LANES))
@@ -480,6 +483,9 @@
 BLOCKS = ((0, 0), (0, 1), (1, 0), (0, 2), (1, 1), (2, 0))
 
 
+NOBODY = (4, 5)
+
+
 def pair_ghosts(dom_count, mine, other, middle, table):
     dom = lax.axis_index("dom")
     first = lax.axis_index("field") == 0
@@ -489,7 +495,6 @@
         below = jnp.where(dom > 0, below, 0.0)
         above = jnp.where(dom < dom_count - 1, above, 0.0)
         table[c, 0:4, :] = below[0:4, :]
-        table[c, 4:6, :] = jnp.zeros((2, LANES), jnp.float32)
         table[c, 6:8, :] = middle[c, 4:6, :]
         table[c, 8:12, :] = above[0:4, :]
 
@@ -505,19 +510,16 @@
     background,
     connect,
     stiff,
-    live,
     scale,
     direction,
     index,
     partial,
     wide,
-    marks,
+    vectors,
     table,
 ):
-    mask = live_mask(live[...])
-    marks[0] = mask * direction[...]
-    marks[1] = mask
-    marks[2] = mask * scale[...]
+    vectors[0] = direction[...]
+    vectors[1] = scale[...]
     wide[...] = jnp.zeros_like(wide)
     size = stiff.shape[0]
     split = split_parts(stiff[...], 3)
@@ -545,8 +547,10 @@
     mine,
     other,
     middle,
+    live,
+    vectors,
+    coupled,
     marks,
-    coupled,
     kept,
     sent,
     ghosts,
@@ -564,7 +568,7 @@
         at = pl.multiple_of((c * 10 + k) * SUBS, SUBS)
         state[0, pl.ds(at, SUBS), :] = value
 
-    lookup(ghosts, 12, index, keep, begin, 2 * owned_high)
+    lookup(ghosts, 12, index, keep, begin, 2 * owned_high, skip=NOBODY)
     spare = state.shape[1] - 30 * SUBS
     state[0, 30 * SUBS :, :] = jnp.zeros((spare, LANES), jnp.float32)
     weights = wide[...].astype(jnp.bfloat16)
@@ -583,7 +587,10 @@
             state[1, pl.ds(b + i, 32, stride=SUBS), :] = product[
                 :, i * LANES : (i + 1) * LANES
             ]
-    search, factor = marks[0], marks[2]
+    mask = live_mask(live[...])
+    search, factor = mask * vectors[0], mask * vectors[1]
+    marks[0] = search
+    marks[1] = mask
     for c in range(3):
         for k in range(10):
             at = (c * 10 + k) * SUBS
@@ -826,7 +833,7 @@
     def keep(k, c, value):
         pulled[c * 10 + k] = value
 
-    lookup(ghosts, 12, index, keep, first=rows)
+    lookup(ghosts, 12, index, keep, first=rows, skip=NOBODY)
     image = near[...]
     for i in range(30):
         image = image + coupled[i] * pulled[i]
@@ -895,30 +902,31 @@
         [pltpu.VMEM((1,) + tile, i32), pltpu.VMEM((3, rows, LANES), f32)],
         1,
         (counts, nodes, background),
-        None,
-    )
-    straight, slanted, middle = along(packed), along(packed, 1), beside(packed)
+        FIRST,
+    )
+    middle, slanted, straight = beside(packed), along(packed, 1), along(packed)
     direction, residual, iterate, reg = others
-    index, partial, wide, marks = call(
+    index, partial, wide, vectors = call(
         functools.partial(pair_own_kernel, link_slots),
         (
             shape((10,) + tile, i32),
             shape((30,) + tile, f32),
             shape((32, 32 * len(BLOCKS)), f32),
-            shape((3,) + tile, f32),
+            shape((2,) + tile, f32),
         ),
         [pltpu.VMEM((3, rows, LANES), f32)],
         0,
-        (background, connect, stiff, live_blocks.reshape(1, 1), scale, direction),
+        (background, connect, stiff, scale, direction),
     )
     straight, partial = lax.optimization_barrier((straight, partial))
     upper = lax.broadcasted_iota(i32, (3,) + tile, 1) < 2
     mine = jnp.where(upper, straight, slanted)
     other = across(mine)
-    coupled, kept, sent = call(
+    coupled, marks, kept, sent = call(
         functools.partial(pair_forward_kernel, dom_count),
         (
             shape((30,) + tile, f32),
+            shape((2,) + tile, f32),
             shape((3, rows + SUBS, LANES), f32),
             shape((3, rows + SUBS, LANES), f32),
         ),
@@ -929,7 +937,16 @@
             pltpu.VMEM((left_rows, link_slots), f32),
         ],
         0,
-        (wide, partial, index, mine, other, middle, marks),
+        (
+            wide,
+            partial,
+            index,
+            mine,
+            other,
+            middle,
+            live_blocks.reshape(1, 1),
+            vectors,
+        ),
     )
     came = across(sent)
     linked = kept[:, rows:] + came[:, rows:]
@@ -945,8 +962,8 @@
         1,
         (counts, nodes, obs, kept, came),
     )
-    straight, link = lax.optimization_barrier((straight, link))
     came = beside(link)
+    straight, slanted, _ = lax.optimization_barrier((straight, slanted, link))
     mine = call(
         pair_join_kernel, shape((3,) + tile, f32), [], 0, (straight, slanted)
     )

time: 42.2 us -> 40.7 us (0.964)
  waiting for transfers between devices: 6.69 us -> 5.68 us
  blocking collectives: 11.2 us -> 10.7 us
    ppermute x4, waiting for transfers between devices: 4.57 us -> 3.62 us  [across(): return lax.ppermute(x, 'field', swap)]
    all_to_all x1, blocking collectives: 11.2 us -> 10.7 us  [on_device(): sums = lax.all_to_all(sums, cores, 0, 0, tiled=True)]
where the time goes in v5:
time: 40.7 us; the launch traced here: 40.4 us
  starting transfers between devices  11.7 us (29%)
  blocking collectives  10.7 us (26%)
  Pallas kernels  9.95 us (24%)
  waiting for transfers between devices  5.68 us (14%)
  between operations  1.45 us (4%)
  local copies, waits for them, and re-layouts  0.88 us (2%)
    all_to_all x1, blocking collectives, on_device(): sums = lax.all_to_all(sums, cores, 0, 0, tiled=True)  10.7 us
    pallas_call x8, Pallas kernels, call(): pl.pallas_call(kernel, compiler_params=params, out_shape=outs, in_specs=[...  9.24 us
    ppermute x5, starting transfers between devices, along(): return lax.ppermute(x, ('dom', 'sub', 'field'), ring(turn))  7.44 us
    ppermute x4, waiting for transfers between devices, across(): return lax.ppermute(x, 'field', swap)  3.62 us
    ppermute x2, starting transfers between devices, beside(): return lax.ppermute(x, 'sub', swap)  3.57 us
    ppermute x2, waiting for transfers between devices, beside(): return lax.ppermute(x, 'sub', swap)  2.03 us
    unnamed x22, local copies, waits for them, and re-layouts  0.88 us
  transfers between devices with their start and end apart: 11, of which 5 were waited for; matrix products, arithmetic and copies ran while one was open for 0% of the time, Pallas kernels for 9%

profile of v5, /device:TPU:0, one launch (start us, length us, event | category | flops | bytes accessed | tf_op | source)
XLA Modules:
  0.0 40.4 jit_solution(5070833978661696406)
XLA Ops:
  0.6 0.0 copy-start
  0.6 0.0 copy-start.4
  0.7 0.0 copy-start.10
  0.7 1.7 %shard_map.140 = f32[3,8,128]{2,1,0:T(8,128)} custom-call(s32[1,2,3]{2,1,0:T(2,128)} %bitcast.17, s32[1,3,2,256]{3,2,1,0:T(2,128)} %nodes.3, f32[3,4096]{1,0:T(4,128)} %background.3), custom_call_target="tpu_custom_call" | custom-call | flops 1048576 | bytes 65536 | tf_op jit(solution)/shard_map/pallas_call | solution.py:887
  2.4 3.0 %collective-permute-start.3 = (f32[3,8,128]{2,1,0:T(8,128)}, f32[3,8,128]{2,1,0:T(8,128)S(1)}, u32[]{:S(2)}, u32[]{:S(2)}) collective-permute-start(f32[3,8,128]{2,1,0:T(8,128)} %shard_map.140), channel_id=1, source_target_pairs={{0,2},{2,0},{1,3},{3,1},{4,6},{6,4},{5,7},{7,5},{8,10},{10,8},{9,1... | collective-permute-start | bytes 36872 | tf_op jit(solution)/shard_map/ppermute | solution.py:881
  5.3 1.5 %collective-permute-start.1 = (f32[3,8,128]{2,1,0:T(8,128)}, f32[3,8,128]{2,1,0:T(8,128)S(1)}, u32[]{:S(2)}, u32[]{:S(2)}) collective-permute-start(f32[3,8,128]{2,1,0:T(8,128)} %shard_map.140), channel_id=1, source_target_pairs={{0,6},{5,3},{4,10},{9,7},{8,14},{13,11},{12,13},{1,0},{2,4},{7,1},... | collective-permute-start | bytes 36872 | tf_op jit(solution)/shard_map/ppermute | solution.py:884
  6.9 1.6 %collective-permute-start = (f32[3,8,128]{2,1,0:T(8,128)}, f32[3,8,128]{2,1,0:T(8,128)S(1)}, u32[]{:S(2)}, u32[]{:S(2)}) collective-permute-start(f32[3,8,128]{2,1,0:T(8,128)} %shard_map.140), channel_id=1, source_target_pairs={{0,4},{5,1},{4,8},{9,5},{8,12},{13,9},{12,13},{1,0},{2,6},{7,3},{6... | collective-permute-start | bytes 36872 | tf_op jit(solution)/shard_map/ppermute | solution.py:884
  8.4 0.0 copy-done
  8.5 0.0 copy-done.4
  8.5 0.0 copy-done.10
  8.5 0.0 copy-done.9
  8.5 0.0 copy-start.2
  8.5 0.8 %copy-done.2 = s32[10,1024]{1,0:T(8,128)S(1)} copy-done((s32[10,1024]{1,0:T(8,128)S(1)}, s32[10,1024]{1,0:T(8,128)}, u32[]{:S(2)}) %copy-start.2) | copy-done | bytes 40984
  9.3 1.5 %shard_map.139 = (s32[10,8,128]{2,1,0:T(8,128)S(1)}, f32[30,8,128]{2,1,0:T(8,128)S(1)}, f32[32,192]{1,0:T(8,128)S(1)}, f32[2,8,128]{2,1,0:T(8,128)S(1)}) custom-call(f32[3,4096]{1,0:T(4,128)S(1)} %copy-done, s32[10,1024]{1,0:T(8,128)S(1)} %copy-done.2, f32[30,30]{1,0:T(8,128)S(1)} %copy-done.4, f32[8,128]{1,0:T(8,128)S(1)} %bitcast.19, f32[8,128]{1,0:T(8,128)S(1)} %bitcast.20), custom_call_target="tpu_custom_call" | custom-call | flops 1048576 | bytes 65536 | tf_op jit(solution)/shard_map/pallas_call | solution.py:887
  10.8 0.0 collective-permute-done
  10.8 0.0 collective-permute-done.1
  10.8 0.1 broadcast_select_fusion.mine
  10.9 0.0 collective-permute-start.2
  11.5 0.0 collective-permute-done.3.middle
  11.6 0.5 %collective-permute-done.2.other = f32[3,8,128]{2,1,0:T(8,128)S(1)} collective-permute-done((f32[3,8,128]{2,1,0:T(8,128)S(1)}, f32[3,8,128]{2,1,0:T(8,128)S(1)}, u32[]{:S(2)}, u32[]{:S(2)}) %collective-permute-start.2) | collective-permute-done | bytes 12320 | tf_op jit(solution)/shard_map/ppermute | solution.py:878
  12.1 2.5 %shard_map.141 = (f32[30,8,128]{2,1,0:T(8,128)S(1)}, f32[2,8,128]{2,1,0:T(8,128)S(1)}, f32[3,40,128]{2,1,0:T(8,128)S(1)}, f32[3,40,128]{2,1,0:T(8,128)S(1)}) custom-call(f32[32,192]{1,0:T(8,128)S(1)} %get-tuple-element.27.wide, f32[30,8,128]{2,1,0:T(8,128)S(1)} %get-tuple-element.29.partial, s32[10,8,128]{2,1,0:T(8,128)S(1)} %get-tuple-element.30.index, ...), custom_call_target="tpu_custom_call" | custom-call | flops 1048576 | bytes 65536 | tf_op jit(solution)/shard_map/pallas_call | solution.py:887
  14.6 0.2 collective-permute-start.4
  14.8 1.1 %collective-permute-done.4.came = f32[3,40,128]{2,1,0:T(8,128)S(1)} collective-permute-done((f32[3,40,128]{2,1,0:T(8,128)S(1)}, f32[3,40,128]{2,1,0:T(8,128)S(1)}, u32[]{:S(2)}, u32[]{:S(2)}) %collective-permute-start.4) | collective-permute-done | bytes 61472 | tf_op jit(solution)/shard_map/ppermute | solution.py:878
  15.9 0.0 copy-start.8
  15.9 2.6 %collective-permute-start.6 = (f32[3,8,128]{2,1,0:T(8,128)S(1)}, f32[3,8,128]{2,1,0:T(8,128)S(1)}, u32[]{:S(2)}, u32[]{:S(2)}) collective-permute-start(f32[3,8,128]{2,1,0:T(8,128)S(1)} %slice_add_fusion), channel_id=1, source_target_pairs={{0,6},{5,3},{4,10},{9,7},{8,14},{13,11},{12,13},{1,0},{2,4},{7,1},... | collective-permute-start | bytes 36872 | tf_op jit(solution)/shard_map/ppermute | solution.py:884
  18.5 1.5 %collective-permute-start.5 = (f32[3,8,128]{2,1,0:T(8,128)S(1)}, f32[3,8,128]{2,1,0:T(8,128)S(1)}, u32[]{:S(2)}, u32[]{:S(2)}) collective-permute-start(f32[3,8,128]{2,1,0:T(8,128)S(1)} %slice_add_fusion), channel_id=1, source_target_pairs={{0,4},{5,1},{4,8},{9,5},{8,12},{13,9},{12,13},{1,0},{2,6},{7,3},{6... | collective-permute-start | bytes 36872 | tf_op jit(solution)/shard_map/ppermute | solution.py:884
  20.0 0.0 copy-done.1
  20.0 0.0 copy-done.3
  20.0 0.0 copy-done.8
  20.0 0.8 %shard_map.142 = (f32[3,32,128]{2,1,0:T(8,128)S(1)}, f32[6,8,128]{2,1,0:T(8,128)S(1)}) custom-call(s32[1,2,3]{2,1,0:T(2,128)S(1)} %bitcast.18, s32[1,3,2,256]{3,2,1,0:T(2,128)S(1)} %copy-done.3, f32[32,128]{1,0:T(8,128)S(1)} %bitcast.12, f32[3,40,128]{2,1,0:T(8,128)S(1)} %get-tuple-element.33.kept, f32[3,40,128]{2,1,0:T(8,128)S(1)} %collective-permute-done.4.came), custom_call_target="tpu_custom_call" | custom-call | flops 1048576 | bytes 65536 | tf_op jit(solution)/shard_map/pallas_call | solution.py:887
  20.8 0.6 %collective-permute-start.8 = (f32[6,8,128]{2,1,0:T(8,128)S(1)}, f32[6,8,128]{2,1,0:T(8,128)S(1)}, u32[]{:S(2)}, u32[]{:S(2)}) collective-permute-start(f32[6,8,128]{2,1,0:T(8,128)S(1)} %get-tuple-element.36.link), channel_id=1, source_target_pairs={{0,2},{2,0},{1,3},{3,1},{4,6},{6,4},{5,7},{7,5},{8,10},{10,8},{9,1... | collective-permute-start | bytes 73736 | tf_op jit(solution)/shard_map/ppermute | solution.py:881
  21.4 0.0 collective-permute-done.6.slanted
  21.4 0.0 collective-permute-done.5.straight
  21.4 0.1 collective-permute-start.7
  21.5 1.2 %collective-permute-done.7.other = f32[3,8,128]{2,1,0:T(8,128)S(1)} collective-permute-done((f32[3,8,128]{2,1,0:T(8,128)S(1)}, f32[3,8,128]{2,1,0:T(8,128)S(1)}, u32[]{:S(2)}, u32[]{:S(2)}) %collective-permute-start.7) | collective-permute-done | bytes 12320 | tf_op jit(solution)/shard_map/ppermute | solution.py:878
  22.7 2.0 %collective-permute-done.8.came = f32[6,8,128]{2,1,0:T(8,128)S(1)} collective-permute-done((f32[6,8,128]{2,1,0:T(8,128)S(1)}, f32[6,8,128]{2,1,0:T(8,128)S(1)}, u32[]{:S(2)}, u32[]{:S(2)}) %collective-permute-start.8) | collective-permute-done | bytes 24608 | tf_op jit(solution)/shard_map/ppermute | solution.py:881
  24.7 0.8 %shard_map.144 = (f32[3,32,128]{2,1,0:T(8,128)S(1)}, f32[3,8,128]{2,1,0:T(8,128)S(1)}) custom-call(f32[3,32,128]{2,1,0:T(8,128)S(1)} %get-tuple-element.35.own, f32[6,8,128]{2,1,0:T(8,128)S(1)} %get-tuple-element.36.link, f32[3,8,128]{2,1,0:T(8,128)S(1)} %shard_map.143.mine, f32[3,8,128]{2,1,0:T(8,128)S(1)} %collective-permute-done.7.other, ...), custom_call_target="tpu_custom_call" | custom-call | flops 1048576 | bytes 65536 | tf_op jit(solution)/shard_map/pallas_call | solution.py:887
  25.5 0.2 collective-permute-start.9
  25.8 1.4 %shard_map.145.near = f32[8,128]{1,0:T(8,128)S(1)} custom-call(f32[3,32,128]{2,1,0:T(8,128)S(1)} %get-tuple-element.40.weighted, s32[10,8,128]{2,1,0:T(8,128)S(1)} %get-tuple-element.30.index, f32[30,8,128]{2,1,0:T(8,128)S(1)} %get-tuple-element.41.coupled), custom_call_target="tpu_custom_call" | custom-call | flops 1048576 | bytes 65536 | tf_op jit(solution)/shard_map/pallas_call | solution.py:887
  27.2 0.0 copy-start.5
  27.2 0.0 collective-permute-done.9.mine
  27.2 0.4 collective-permute-start.10
  27.6 0.9 %collective-permute-done.10.other = f32[3,8,128]{2,1,0:T(8,128)S(1)} collective-permute-done((f32[3,8,128]{2,1,0:T(8,128)S(1)}, f32[3,8,128]{2,1,0:T(8,128)S(1)}, u32[]{:S(2)}, u32[]{:S(2)}) %collective-permute-start.10) | collective-permute-done | bytes 12320 | tf_op jit(solution)/shard_map/ppermute | solution.py:878
  28.5 0.0 copy-done.6
  28.5 0.0 copy-done.7
  28.5 0.6 %shard_map.146 = (f32[8,128]{1,0:T(8,128)S(1)}, f32[16,4,128]{2,1,0:T(4,128)S(1)}, f32[3,8,128]{2,1,0:T(8,128)S(1)}) custom-call(f32[8,128]{1,0:T(8,128)S(1)} %shard_map.145.near, f32[3,8,128]{2,1,0:T(8,128)S(1)} %collective-permute-done.9.mine, f32[3,8,128]{2,1,0:T(8,128)S(1)} %collective-permute-done.10.other, f32[3,8,128]{2,1,0:T(8,128)S(1)} %get-tuple-element.39.middle, ...), custom_call_target="tpu_custom_call" | custom-call | flops 1048576 | bytes 65536 | tf_op jit(solution)/shard_map/pallas_call | solution.py:887
  29.0 10.7 %all_to_all.5.sums = f32[16,4,128]{2,1,0:T(4,128)S(1)} all-to-all(f32[16,4,128]{2,1,0:T(4,128)S(1)} %get-tuple-element.45), channel_id=1, replica_groups=mesh['groups'=2,'dom'=4,'sub'=2,'field'=2] {'dom','sub','field'}, dimensions={0} | all-to-all | bytes 65536 | tf_op jit(solution)/shard_map/all_to_all | solution.py:1143
  39.7 0.7 %shard_map.147 = (f32[8,128]{1,0:T(8,128)}, f32[8,128]{1,0:T(8,128)}, f32[8,128]{1,0:T(8,128)}) custom-call(f32[16,4,128]{2,1,0:T(4,128)S(1)} %all_to_all.5.sums, f32[8,128]{1,0:T(8,128)S(1)} %get-tuple-element.46.hess, f32[3,8,128]{2,1,0:T(8,128)S(1)} %get-tuple-element.47.vectors), custom_call_target="tpu_custom_call" | custom-call | tf_op jit(solution)/shard_map/pallas_call | solution.py:1145
  (9 shorter events, 0.0 us)
Async XLA Ops:
  0.6 7.8 %copy-start = (f32[3,4096]{1,0:T(4,128)S(1)}, f32[3,4096]{1,0:T(4,128)}, u32[]{:S(2)}) copy-start(f32[3,4096]{1,0:T(4,128)} %background.3) | copy-start | bytes 147460
  0.6 7.8 %copy-start.4 = (f32[30,30]{1,0:T(8,128)S(1)}, f32[30,30]{1,0:T(8,128)}, u32[]{:S(2)}) copy-start(f32[30,30]{1,0:T(8,128)} %stiff.1) | copy-start | bytes 10804
  0.7 7.8 %copy-start.10 = (f32[1024]{0:T(1024)S(1)}, f32[1024]{0:T(1024)}, u32[]{:S(2)}) copy-start(f32[1024]{0:T(1024)} %param.20) | copy-start | bytes 12292
  2.3 6.1 %copy-start.9 = (f32[1024]{0:T(1024)S(1)}, f32[1024]{0:T(1024)}, u32[]{:S(2)}) copy-start(f32[1024]{0:T(1024)} %param.16) | copy-start | bytes 12292
  2.4 9.2 %collective-permute-start.3 = (f32[3,8,128]{2,1,0:T(8,128)}, f32[3,8,128]{2,1,0:T(8,128)S(1)}, u32[]{:S(2)}, u32[]{:S(2)}) collective-permute-start(f32[3,8,128]{2,1,0:T(8,128)} %shard_map.140), channel_id=1, source_target_pairs={{0,2},{2,0},{1,3},{3,1},{4,6},{6,4},{5,7},{7,5},{8,10},{10,8},{9,1... | collective-permute-start | bytes 36872 | tf_op jit(solution)/shard_map/ppermute | solution.py:881
  5.3 5.5 %collective-permute-start.1 = (f32[3,8,128]{2,1,0:T(8,128)}, f32[3,8,128]{2,1,0:T(8,128)S(1)}, u32[]{:S(2)}, u32[]{:S(2)}) collective-permute-start(f32[3,8,128]{2,1,0:T(8,128)} %shard_map.140), channel_id=1, source_target_pairs={{0,6},{5,3},{4,10},{9,7},{8,14},{13,11},{12,13},{1,0},{2,4},{7,1},... | collective-permute-start | bytes 36872 | tf_op jit(solution)/shard_map/ppermute | solution.py:884
  6.9 3.9 %collective-permute-start = (f32[3,8,128]{2,1,0:T(8,128)}, f32[3,8,128]{2,1,0:T(8,128)S(1)}, u32[]{:S(2)}, u32[]{:S(2)}) collective-permute-start(f32[3,8,128]{2,1,0:T(8,128)} %shard_map.140), channel_id=1, source_target_pairs={{0,4},{5,1},{4,8},{9,5},{8,12},{13,9},{12,13},{1,0},{2,6},{7,3},{6... | collective-permute-start | bytes 36872 | tf_op jit(solution)/shard_map/ppermute | solution.py:884
  8.5 0.8 %copy-start.2 = (s32[10,1024]{1,0:T(8,128)S(1)}, s32[10,1024]{1,0:T(8,128)}, u32[]{:S(2)}) copy-start(s32[10,1024]{1,0:T(8,128)} %connect.1) | copy-start | bytes 122884
  10.9 1.2 %collective-permute-start.2 = (f32[3,8,128]{2,1,0:T(8,128)S(1)}, f32[3,8,128]{2,1,0:T(8,128)S(1)}, u32[]{:S(2)}, u32[]{:S(2)}) collective-permute-start(f32[3,8,128]{2,1,0:T(8,128)S(1)} %broadcast_select_fusion.mine), channel_id=1, source_target_pairs={{0,1},{1,0},{2,3},{3,2},{4,5},{5,4},{6,7},{7,6},{8,9},{9,8},{10,11... | collective-permute-start | bytes 36872 | tf_op jit(solution)/shard_map/ppermute | solution.py:878
  14.6 1.3 %collective-permute-start.4 = (f32[3,40,128]{2,1,0:T(8,128)S(1)}, f32[3,40,128]{2,1,0:T(8,128)S(1)}, u32[]{:S(2)}, u32[]{:S(2)}) collective-permute-start(f32[3,40,128]{2,1,0:T(8,128)S(1)} %get-tuple-element.34), channel_id=1, source_target_pairs={{0,1},{1,0},{2,3},{3,2},{4,5},{5,4},{6,7},{7,6},{8,9},{9,8},{10,11... | collective-permute-start | bytes 184328 | tf_op jit(solution)/shard_map/ppermute | solution.py:878
  15.9 4.1 %copy-start.1 = (f32[4096]{0:T(1024)S(1)}, f32[4096]{0:T(1024)}, u32[]{:S(2)}) copy-start(f32[4096]{0:T(1024)} %param.13) | copy-start | bytes 49156
  15.9 4.1 %copy-start.3 = (s32[1,3,2,256]{3,2,1,0:T(2,128)S(1)}, s32[1,3,2,256]{3,2,1,0:T(2,128)}, u32[]{:S(2)}) copy-start(s32[1,3,2,256]{3,2,1,0:T(2,128)} %nodes.3) | copy-start | bytes 18436
  15.9 4.1 %copy-start.8 = (s32[1,3,2]{1,2,0:T(2,128)S(1)}, s32[1,3,2]{1,2,0:T(2,128)}, u32[]{:S(2)}) copy-start(s32[1,3,2]{1,2,0:T(2,128)} %param.22) | copy-start | bytes 76
  15.9 5.5 %collective-permute-start.6 = (f32[3,8,128]{2,1,0:T(8,128)S(1)}, f32[3,8,128]{2,1,0:T(8,128)S(1)}, u32[]{:S(2)}, u32[]{:S(2)}) collective-permute-start(f32[3,8,128]{2,1,0:T(8,128)S(1)} %slice_add_fusion), channel_id=1, source_target_pairs={{0,6},{5,3},{4,10},{9,7},{8,14},{13,11},{12,13},{1,0},{2,4},{7,1},... | collective-permute-start | bytes 36872 | tf_op jit(solution)/shard_map/ppermute | solution.py:884
  18.5 2.9 %collective-permute-start.5 = (f32[3,8,128]{2,1,0:T(8,128)S(1)}, f32[3,8,128]{2,1,0:T(8,128)S(1)}, u32[]{:S(2)}, u32[]{:S(2)}) collective-permute-start(f32[3,8,128]{2,1,0:T(8,128)S(1)} %slice_add_fusion), channel_id=1, source_target_pairs={{0,4},{5,1},{4,8},{9,5},{8,12},{13,9},{12,13},{1,0},{2,6},{7,3},{6... | collective-permute-start | bytes 36872 | tf_op jit(solution)/shard_map/ppermute | solution.py:884
  20.8 3.9 %collective-permute-start.8 = (f32[6,8,128]{2,1,0:T(8,128)S(1)}, f32[6,8,128]{2,1,0:T(8,128)S(1)}, u32[]{:S(2)}, u32[]{:S(2)}) collective-permute-start(f32[6,8,128]{2,1,0:T(8,128)S(1)} %get-tuple-element.36.link), channel_id=1, source_target_pairs={{0,2},{2,0},{1,3},{3,1},{4,6},{6,4},{5,7},{7,5},{8,10},{10,8},{9,1... | collective-permute-start | bytes 73736 | tf_op jit(solution)/shard_map/ppermute | solution.py:881
  21.4 1.2 %collective-permute-start.7 = (f32[3,8,128]{2,1,0:T(8,128)S(1)}, f32[3,8,128]{2,1,0:T(8,128)S(1)}, u32[]{:S(2)}, u32[]{:S(2)}) collective-permute-start(f32[3,8,128]{2,1,0:T(8,128)S(1)} %shard_map.143.mine), channel_id=1, source_target_pairs={{0,1},{1,0},{2,3},{3,2},{4,5},{5,4},{6,7},{7,6},{8,9},{9,8},{10,11... | collective-permute-start | bytes 36872 | tf_op jit(solution)/shard_map/ppermute | solution.py:878
  25.5 1.7 %collective-permute-start.9 = (f32[3,8,128]{2,1,0:T(8,128)S(1)}, f32[3,8,128]{2,1,0:T(8,128)S(1)}, u32[]{:S(2)}, u32[]{:S(2)}) collective-permute-start(f32[3,8,128]{2,1,0:T(8,128)S(1)} %get-tuple-element.39.middle), channel_id=1, source_target_pairs={{0,4},{5,1},{4,8},{9,5},{8,12},{13,9},{12,13},{1,0},{2,6},{7,3},{6... | collective-permute-start | bytes 36872 | tf_op jit(solution)/shard_map/ppermute | solution.py:884
  25.8 2.7 %copy-start.6 = (f32[1024]{0:T(1024)S(1)}, f32[1024]{0:T(1024)}, u32[]{:S(2)}) copy-start(f32[1024]{0:T(1024)} %param.18) | copy-start | bytes 12292
  25.8 2.7 %copy-start.7 = (f32[1024]{0:T(1024)S(1)}, f32[1024]{0:T(1024)}, u32[]{:S(2)}) copy-start(f32[1024]{0:T(1024)} %param.17) | copy-start | bytes 12292
  27.2 1.3 %copy-start.5 = (f32[1024]{0:T(1024)S(1)}, f32[1024]{0:T(1024)}, u32[]{:S(2)}) copy-start(f32[1024]{0:T(1024)} %param.19) | copy-start | bytes 12292
  27.2 1.2 %collective-permute-start.10 = (f32[3,8,128]{2,1,0:T(8,128)S(1)}, f32[3,8,128]{2,1,0:T(8,128)S(1)}, u32[]{:S(2)}, u32[]{:S(2)}) collective-permute-start(f32[3,8,128]{2,1,0:T(8,128)S(1)} %collective-permute-done.9.mine), channel_id=1, source_target_pairs={{0,1},{1,0},{2,3},{3,2},{4,5},{5,4},{6,7},{7,6},{8,9},{9,8},{10,11... | collective-permute-start | bytes 36872 | tf_op jit(solution)/shard_map/ppermute | solution.py:878

commit v6 on v5

--- a/solution.py
+++ b/solution.py
@@ -17,7 +17,6 @@
 
 VMEM = pl.BlockSpec(memory_space=pltpu.VMEM)
 SMEM = pl.BlockSpec(memory_space=pltpu.SMEM)
-FIRST = None
 PARAMS = pltpu.CompilerParams(vmem_limit_bytes=16 * 2**20)
 
 
@@ -499,6 +498,10 @@
         table[c, 8:12, :] = above[0:4, :]
 
 
+def pair_copy_kernel(source, out):
+    out[...] = source[...]
+
+
 def pair_join_kernel(straight, slanted, out):
     for c in range(3):
         out[c, 0:4, :] = straight[c, 0:4, :]
@@ -620,28 +623,11 @@
                 out[c, base + 6 + h : base + 7 + h, :] = jnp.zeros((1, LANES), jnp.float32)
 
 
-def pair_sum_kernel(
-    counts, nodes, obs, kept, came, own, link, index, table, weights
-):
-    part, fixed = link.at[0:3], link.at[3:6]
-    rows = own.shape[1]
-    half = rows // 2
-    for c in range(3):
-        both = kept[c, 0:rows, :] + came[c, 0:rows, :]
-        own[c] = both
-        for h in range(2):
-            table[c, pl.ds(h, half, stride=2), :] = both[h * half : (h + 1) * half]
+def pair_fixed_kernel(counts, nodes, obs, fixed, index, weights):
+    rows = obs.shape[0]
+    weights[0] = obs[...]
     link_tile(nodes, index, ((0, 1), (1, 1), (2, 1)))
-    weights[0] = obs[...]
-
-    def keep(tile, c, value):
-        part[c] = value
-
-    lookup(table, rows, index, keep)
-    for c in range(3):
-        part[c, 6:8, :] = (
-            kept[c, rows + 4 : rows + 6, :] + came[c, rows + 4 : rows + 6, :]
-        )
+    fixed[3] = index[0].astype(jnp.float32)
 
     def keep_weight(tile, c, value):
         fixed[2] = value
@@ -657,6 +643,27 @@
                 fixed[at // SUBS, at % SUBS : at % SUBS + 1, :] = jnp.where(
                     here, link_line(nodes, o, k, h), -1
                 ).astype(jnp.float32)
+
+
+def pair_sum_kernel(fixed, kept, came, own, link, index, table):
+    rows = own.shape[1]
+    half = rows // 2
+    for c in range(3):
+        both = kept[c, 0:rows, :] + came[c, 0:rows, :]
+        own[c] = both
+        for h in range(2):
+            table[c, pl.ds(h, half, stride=2), :] = both[h * half : (h + 1) * half]
+    index[0] = fixed[3].astype(jnp.int32)
+
+    def keep(tile, c, value):
+        link[c] = value
+
+    lookup(table, rows, index, keep)
+    for c in range(3):
+        link[c, 6:8, :] = (
+            kept[c, rows + 4 : rows + 6, :] + came[c, rows + 4 : rows + 6, :]
+        )
+        link[3 + c] = fixed[c]
 
 
 def landing(nodes, lines, owned_high, width):
@@ -902,9 +909,10 @@
         [pltpu.VMEM((1,) + tile, i32), pltpu.VMEM((3, rows, LANES), f32)],
         1,
         (counts, nodes, background),
-        FIRST,
-    )
-    middle, slanted, straight = beside(packed), along(packed, 1), along(packed)
+        None,
+    )
+    straight, slanted = along(packed), along(packed, 1)
+    middle = beside(call(pair_copy_kernel, shape((3,) + tile, f32), [], 0, (packed,)))
     direction, residual, iterate, reg = others
     index, partial, wide, vectors = call(
         functools.partial(pair_own_kernel, link_slots),
@@ -949,18 +957,23 @@
         ),
     )
     came = across(sent)
+    nodes, _ = lax.optimization_barrier((nodes, sent))
+    fixed = call(
+        pair_fixed_kernel,
+        shape((4,) + tile, f32),
+        [pltpu.VMEM((1,) + tile, i32), pltpu.VMEM((1, rows, LANES), f32)],
+        1,
+        (counts, nodes, obs),
+    )
+    came, fixed = lax.optimization_barrier((came, fixed))
     linked = kept[:, rows:] + came[:, rows:]
     straight, slanted = along(linked), along(linked, 1)
     own, link = call(
         pair_sum_kernel,
         (shape((3, rows, LANES), f32), shape((6,) + tile, f32)),
-        [
-            pltpu.VMEM((1,) + tile, i32),
-            pltpu.VMEM((3, rows, LANES), f32),
-            pltpu.VMEM((1, rows, LANES), f32),
-        ],
-        1,
-        (counts, nodes, obs, kept, came),
+        [pltpu.VMEM((1,) + tile, i32), pltpu.VMEM((3, rows, LANES), f32)],
+        0,
+        (fixed, kept, came),
     )
     came = beside(link)
     straight, slanted, _ = lax.optimization_barrier((straight, slanted, link))

time: 40.7 us -> 40.3 us (level)
  local copies, waits for them, and re-layouts: 0.88 us -> 2.2 us
  starting transfers between devices: 11.7 us -> 10.6 us
  waiting for transfers between devices: 5.68 us -> 4.74 us
    ppermute x2, starting transfers between devices: 3.57 us -> 1.36 us  [beside(): return lax.ppermute(x, 'sub', swap)]
    ppermute x5, starting transfers between devices: 7.44 us -> 8.96 us  [along(): return lax.ppermute(x, ('dom', 'sub', 'field'), ring(turn))]
    unnamed x22 -> x24, local copies, waits for them, and re-layouts: 0.88 us -> 2.2 us
    ppermute x4, waiting for transfers between devices: 3.62 us -> 2.85 us  [across(): return lax.ppermute(x, 'field', swap)]
    ppermute x2, waiting for transfers between devices: 2.03 us -> 1.4 us  [beside(): return lax.ppermute(x, 'sub', swap)]
    ppermute x5, waiting for transfers between devices: 0.02 us -> 0.49 us  [along(): return lax.ppermute(x, ('dom', 'sub', 'field'), ring(turn))]
    pallas_call x8 -> x10, Pallas kernels: 9.24 us -> 9.31 us  [call(): pl.pallas_call(kernel, compiler_params=params, out_shape=outs, in_specs=[...]
  transfers between devices with their start and end apart: 11 -> 11, of which waited for: 5 -> 6; matrix products, arithmetic and copies ran while one was open for 0% -> 0% of each run, Pallas kernels for 9% -> 9%
where the time goes in v6:
time: 40.3 us; the launch traced here: 39.9 us
  blocking collectives  10.8 us (27%)
  starting transfers between devices  10.6 us (26%)
  Pallas kernels  10 us (25%)
  waiting for transfers between devices  4.74 us (12%)
  local copies, waits for them, and re-layouts  2.2 us (5%)
  between operations  1.44 us (4%)
    all_to_all x1, blocking collectives, on_device(): sums = lax.all_to_all(sums, cores, 0, 0, tiled=True)  10.8 us
    pallas_call x10, Pallas kernels, call(): pl.pallas_call(kernel, compiler_params=params, out_shape=outs, in_specs=[...  9.31 us
    ppermute x5, starting transfers between devices, along(): return lax.ppermute(x, ('dom', 'sub', 'field'), ring(turn))  8.96 us
    ppermute x4, waiting for transfers between devices, across(): return lax.ppermute(x, 'field', swap)  2.85 us
    unnamed x24, local copies, waits for them, and re-layouts  2.2 us
    ppermute x2, waiting for transfers between devices, beside(): return lax.ppermute(x, 'sub', swap)  1.4 us
    ppermute x2, starting transfers between devices, beside(): return lax.ppermute(x, 'sub', swap)  1.36 us
  transfers between devices with their start and end apart: 11, of which 6 were waited for; matrix products, arithmetic and copies ran while one was open for 0% of the time, Pallas kernels for 9%

profile of v6, /device:TPU:0, one launch (start us, length us, event | category | flops | bytes accessed | tf_op | source)
XLA Modules:
  0.0 39.9 jit_solution(16329469593539027992)
XLA Ops:
  0.6 0.0 copy-start
  0.6 0.0 copy-start.5
  0.6 1.7 %shard_map.140.source = f32[3,8,128]{2,1,0:T(8,128)} custom-call(s32[1,2,3]{2,1,0:T(2,128)} %bitcast.17, s32[1,3,2,256]{3,2,1,0:T(2,128)} %nodes.2, f32[3,4096]{1,0:T(4,128)} %background.3), custom_call_target="tpu_custom_call" | custom-call | flops 1048576 | bytes 65536 | tf_op jit(solution)/shard_map/pallas_call | solution.py:894
  2.3 4.0 %collective-permute-start.1 = (f32[3,8,128]{2,1,0:T(8,128)}, f32[3,8,128]{2,1,0:T(8,128)S(1)}, u32[]{:S(2)}, u32[]{:S(2)}) collective-permute-start(f32[3,8,128]{2,1,0:T(8,128)} %shard_map.140.source), channel_id=1, source_target_pairs={{0,6},{5,3},{4,10},{9,7},{8,14},{13,11},{12,13},{1,0},{2,4},{7,1},... | collective-permute-start | bytes 36872 | tf_op jit(solution)/shard_map/ppermute | solution.py:891
  6.3 1.6 %collective-permute-start = (f32[3,8,128]{2,1,0:T(8,128)}, f32[3,8,128]{2,1,0:T(8,128)S(1)}, u32[]{:S(2)}, u32[]{:S(2)}) collective-permute-start(f32[3,8,128]{2,1,0:T(8,128)} %shard_map.140.source), channel_id=1, source_target_pairs={{0,4},{5,1},{4,8},{9,5},{8,12},{13,9},{12,13},{1,0},{2,6},{7,3},{6... | collective-permute-start | bytes 36872 | tf_op jit(solution)/shard_map/ppermute | solution.py:891
  7.9 0.7 %copy-done.3 = f32[3,8,128]{2,1,0:T(8,128)S(1)} copy-done((f32[3,8,128]{2,1,0:T(8,128)S(1)}, f32[3,8,128]{2,1,0:T(8,128)}, u32[]{:S(2)}) %copy-start.3) | copy-done | bytes 12312
  8.6 0.5 %collective-permute-start.3 = (f32[3,8,128]{2,1,0:T(8,128)S(1)}, f32[3,8,128]{2,1,0:T(8,128)S(1)}, u32[]{:S(2)}, u32[]{:S(2)}) collective-permute-start(f32[3,8,128]{2,1,0:T(8,128)S(1)} %shard_map.141), channel_id=1, source_target_pairs={{0,2},{2,0},{1,3},{3,1},{4,6},{6,4},{5,7},{7,5},{8,10},{10,8},{9,1... | collective-permute-start | bytes 36872 | tf_op jit(solution)/shard_map/ppermute | solution.py:888
  9.2 0.0 copy-done
  9.2 0.0 copy-done.5
  9.2 0.1 copy-done.11
  9.3 0.0 copy-done.10
  9.3 0.8 %copy-done.2 = s32[10,1024]{1,0:T(8,128)S(1)} copy-done((s32[10,1024]{1,0:T(8,128)S(1)}, s32[10,1024]{1,0:T(8,128)}, u32[]{:S(2)}) %copy-start.2) | copy-done | bytes 40984
  10.2 1.5 %shard_map.139 = (s32[10,8,128]{2,1,0:T(8,128)S(1)}, f32[30,8,128]{2,1,0:T(8,128)S(1)}, f32[32,192]{1,0:T(8,128)S(1)}, f32[2,8,128]{2,1,0:T(8,128)S(1)}) custom-call(f32[3,4096]{1,0:T(4,128)S(1)} %copy-done, s32[10,1024]{1,0:T(8,128)S(1)} %copy-done.2, f32[30,30]{1,0:T(8,128)S(1)} %copy-done.5, f32[8,128]{1,0:T(8,128)S(1)} %bitcast.19, f32[8,128]{1,0:T(8,128)S(1)} %bitcast.20), custom_call_target="tpu_custom_call" | custom-call | flops 1048576 | bytes 65536 | tf_op jit(solution)/shard_map/pallas_call | solution.py:894
  11.7 0.0 collective-permute-done
  11.7 0.0 collective-permute-done.1
  11.7 0.1 broadcast_select_fusion.mine
  11.7 0.0 collective-permute-start.2
  12.4 0.0 collective-permute-done.3.middle
  12.4 0.5 %collective-permute-done.2.other = f32[3,8,128]{2,1,0:T(8,128)S(1)} collective-permute-done((f32[3,8,128]{2,1,0:T(8,128)S(1)}, f32[3,8,128]{2,1,0:T(8,128)S(1)}, u32[]{:S(2)}, u32[]{:S(2)}) %collective-permute-start.2) | collective-permute-done | bytes 12320 | tf_op jit(solution)/shard_map/ppermute | solution.py:885
  12.9 2.5 %shard_map.142 = (f32[30,8,128]{2,1,0:T(8,128)S(1)}, f32[2,8,128]{2,1,0:T(8,128)S(1)}, f32[3,40,128]{2,1,0:T(8,128)S(1)}, f32[3,40,128]{2,1,0:T(8,128)S(1)}) custom-call(f32[32,192]{1,0:T(8,128)S(1)} %get-tuple-element.30.wide, f32[30,8,128]{2,1,0:T(8,128)S(1)} %get-tuple-element.32.partial, s32[10,8,128]{2,1,0:T(8,128)S(1)} %get-tuple-element.33.index, ...), custom_call_target="tpu_custom_call" | custom-call | flops 1048576 | bytes 65536 | tf_op jit(solution)/shard_map/pallas_call | solution.py:894
  15.5 0.0 copy-start.9
  15.5 0.2 collective-permute-start.4
  15.7 0.0 copy-done.1
  15.7 0.0 copy-done.4
  15.7 0.4 %copy-done.9 = s32[1,3,2]{1,2,0:T(2,128)S(1)} copy-done((s32[1,3,2]{1,2,0:T(2,128)S(1)}, s32[1,3,2]{1,2,0:T(2,128)}, u32[]{:S(2)}) %copy-start.9) | copy-done | bytes 48
  16.1 0.7 %shard_map.143.fixed = f32[4,8,128]{2,1,0:T(8,128)S(1)} custom-call(s32[1,2,3]{2,1,0:T(2,128)S(1)} %bitcast.18, s32[1,3,2,256]{3,2,1,0:T(2,128)S(1)} %copy-done.4, f32[32,128]{1,0:T(8,128)S(1)} %bitcast.12), custom_call_target="tpu_custom_call" | custom-call | flops 1048576 | bytes 65536 | tf_op jit(solution)/shard_map/pallas_call | solution.py:894
  16.8 0.0 collective-permute-done.4.came
  16.8 2.4 %collective-permute-start.6 = (f32[3,8,128]{2,1,0:T(8,128)S(1)}, f32[3,8,128]{2,1,0:T(8,128)S(1)}, u32[]{:S(2)}, u32[]{:S(2)}) collective-permute-start(f32[3,8,128]{2,1,0:T(8,128)S(1)} %slice_add_fusion), channel_id=1, source_target_pairs={{0,6},{5,3},{4,10},{9,7},{8,14},{13,11},{12,13},{1,0},{2,4},{7,1},... | collective-permute-start | bytes 36872 | tf_op jit(solution)/shard_map/ppermute | solution.py:891
  19.3 0.0 collective-permute-start.5
  19.3 0.2 shard_map.144
  19.5 0.8 %collective-permute-start.8 = (f32[6,8,128]{2,1,0:T(8,128)S(1)}, f32[6,8,128]{2,1,0:T(8,128)S(1)}, u32[]{:S(2)}, u32[]{:S(2)}) collective-permute-start(f32[6,8,128]{2,1,0:T(8,128)S(1)} %get-tuple-element.42.link), channel_id=1, source_target_pairs={{0,2},{2,0},{1,3},{3,1},{4,6},{6,4},{5,7},{7,5},{8,10},{10,8},{9,1... | collective-permute-start | bytes 73736 | tf_op jit(solution)/shard_map/ppermute | solution.py:888
  20.3 0.4 collective-permute-done.6.slanted
  20.7 0.1 collective-permute-done.5.straight
  20.8 0.0 collective-permute-start.7
  20.8 1.2 %collective-permute-done.7.other = f32[3,8,128]{2,1,0:T(8,128)S(1)} collective-permute-done((f32[3,8,128]{2,1,0:T(8,128)S(1)}, f32[3,8,128]{2,1,0:T(8,128)S(1)}, u32[]{:S(2)}, u32[]{:S(2)}) %collective-permute-start.7) | collective-permute-done | bytes 12320 | tf_op jit(solution)/shard_map/ppermute | solution.py:885
  22.0 1.4 %collective-permute-done.8.came = f32[6,8,128]{2,1,0:T(8,128)S(1)} collective-permute-done((f32[6,8,128]{2,1,0:T(8,128)S(1)}, f32[6,8,128]{2,1,0:T(8,128)S(1)}, u32[]{:S(2)}, u32[]{:S(2)}) %collective-permute-start.8) | collective-permute-done | bytes 24608 | tf_op jit(solution)/shard_map/ppermute | solution.py:888
  23.4 0.8 %shard_map.146 = (f32[3,32,128]{2,1,0:T(8,128)S(1)}, f32[3,8,128]{2,1,0:T(8,128)S(1)}) custom-call(f32[3,32,128]{2,1,0:T(8,128)S(1)} %get-tuple-element.41.own, f32[6,8,128]{2,1,0:T(8,128)S(1)} %get-tuple-element.42.link, f32[3,8,128]{2,1,0:T(8,128)S(1)} %shard_map.145.mine, f32[3,8,128]{2,1,0:T(8,128)S(1)} %collective-permute-done.7.other, ...), custom_call_target="tpu_custom_call" | custom-call | flops 1048576 | bytes 65536 | tf_op jit(solution)/shard_map/pallas_call | solution.py:894
  24.2 0.9 %collective-permute-start.9 = (f32[3,8,128]{2,1,0:T(8,128)S(1)}, f32[3,8,128]{2,1,0:T(8,128)S(1)}, u32[]{:S(2)}, u32[]{:S(2)}) collective-permute-start(f32[3,8,128]{2,1,0:T(8,128)S(1)} %get-tuple-element.45.middle), channel_id=1, source_target_pairs={{0,4},{5,1},{4,8},{9,5},{8,12},{13,9},{12,13},{1,0},{2,6},{7,3},{6... | collective-permute-start | bytes 36872 | tf_op jit(solution)/shard_map/ppermute | solution.py:891
  25.1 1.4 %shard_map.147.near = f32[8,128]{1,0:T(8,128)S(1)} custom-call(f32[3,32,128]{2,1,0:T(8,128)S(1)} %get-tuple-element.46.weighted, s32[10,8,128]{2,1,0:T(8,128)S(1)} %get-tuple-element.33.index, f32[30,8,128]{2,1,0:T(8,128)S(1)} %get-tuple-element.47.coupled), custom_call_target="tpu_custom_call" | custom-call | flops 1048576 | bytes 65536 | tf_op jit(solution)/shard_map/pallas_call | solution.py:894
  26.6 0.0 copy-start.6
  26.6 0.0 collective-permute-done.9.mine
  26.6 0.1 collective-permute-start.10
  26.7 1.2 %collective-permute-done.10.other = f32[3,8,128]{2,1,0:T(8,128)S(1)} collective-permute-done((f32[3,8,128]{2,1,0:T(8,128)S(1)}, f32[3,8,128]{2,1,0:T(8,128)S(1)}, u32[]{:S(2)}, u32[]{:S(2)}) %collective-permute-start.10) | collective-permute-done | bytes 12320 | tf_op jit(solution)/shard_map/ppermute | solution.py:885
  27.8 0.0 copy-done.7
  27.8 0.0 copy-done.6
  27.8 0.6 %shard_map.148 = (f32[8,128]{1,0:T(8,128)S(1)}, f32[16,4,128]{2,1,0:T(4,128)S(1)}, f32[3,8,128]{2,1,0:T(8,128)S(1)}) custom-call(f32[8,128]{1,0:T(8,128)S(1)} %shard_map.147.near, f32[3,8,128]{2,1,0:T(8,128)S(1)} %collective-permute-done.9.mine, f32[3,8,128]{2,1,0:T(8,128)S(1)} %collective-permute-done.10.other, f32[3,8,128]{2,1,0:T(8,128)S(1)} %get-tuple-element.45.middle, ...), custom_call_target="tpu_custom_call" | custom-call | flops 1048576 | bytes 65536 | tf_op jit(solution)/shard_map/pallas_call | solution.py:894
  28.4 10.8 %all_to_all.5.sums = f32[16,4,128]{2,1,0:T(4,128)S(1)} all-to-all(f32[16,4,128]{2,1,0:T(4,128)S(1)} %get-tuple-element.51), channel_id=1, replica_groups=mesh['groups'=2,'dom'=4,'sub'=2,'field'=2] {'dom','sub','field'}, dimensions={0} | all-to-all | bytes 65536 | tf_op jit(solution)/shard_map/all_to_all | solution.py:1156
  39.2 0.7 %shard_map.149 = (f32[8,128]{1,0:T(8,128)}, f32[8,128]{1,0:T(8,128)}, f32[8,128]{1,0:T(8,128)}) custom-call(f32[16,4,128]{2,1,0:T(4,128)S(1)} %all_to_all.5.sums, f32[8,128]{1,0:T(8,128)S(1)} %get-tuple-element.52.hess, f32[3,8,128]{2,1,0:T(8,128)S(1)} %get-tuple-element.53.vectors), custom_call_target="tpu_custom_call" | custom-call | tf_op jit(solution)/shard_map/pallas_call | solution.py:1158
  (13 shorter events, 0.0 us)
Async XLA Ops:
  0.6 8.6 %copy-start = (f32[3,4096]{1,0:T(4,128)S(1)}, f32[3,4096]{1,0:T(4,128)}, u32[]{:S(2)}) copy-start(f32[3,4096]{1,0:T(4,128)} %background.3) | copy-start | bytes 147460
  0.6 8.6 %copy-start.5 = (f32[30,30]{1,0:T(8,128)S(1)}, f32[30,30]{1,0:T(8,128)}, u32[]{:S(2)}) copy-start(f32[30,30]{1,0:T(8,128)} %stiff.1) | copy-start | bytes 10804
  2.3 9.3 %collective-permute-start.1 = (f32[3,8,128]{2,1,0:T(8,128)}, f32[3,8,128]{2,1,0:T(8,128)S(1)}, u32[]{:S(2)}, u32[]{:S(2)}) collective-permute-start(f32[3,8,128]{2,1,0:T(8,128)} %shard_map.140.source), channel_id=1, source_target_pairs={{0,6},{5,3},{4,10},{9,7},{8,14},{13,11},{12,13},{1,0},{2,4},{7,1},... | collective-permute-start | bytes 36872 | tf_op jit(solution)/shard_map/ppermute | solution.py:891
  6.3 5.3 %collective-permute-start = (f32[3,8,128]{2,1,0:T(8,128)}, f32[3,8,128]{2,1,0:T(8,128)S(1)}, u32[]{:S(2)}, u32[]{:S(2)}) collective-permute-start(f32[3,8,128]{2,1,0:T(8,128)} %shard_map.140.source), channel_id=1, source_target_pairs={{0,4},{5,1},{4,8},{9,5},{8,12},{13,9},{12,13},{1,0},{2,6},{7,3},{6... | collective-permute-start | bytes 36872 | tf_op jit(solution)/shard_map/ppermute | solution.py:891
  7.9 0.7 %copy-start.3 = (f32[3,8,128]{2,1,0:T(8,128)S(1)}, f32[3,8,128]{2,1,0:T(8,128)}, u32[]{:S(2)}) copy-start(f32[3,8,128]{2,1,0:T(8,128)} %shard_map.140.source) | copy-start | bytes 36868
  8.6 0.7 %copy-start.11 = (f32[1024]{0:T(1024)S(1)}, f32[1024]{0:T(1024)}, u32[]{:S(2)}) copy-start(f32[1024]{0:T(1024)} %param.20) | copy-start | bytes 12292
  8.6 0.7 %copy-start.10 = (f32[1024]{0:T(1024)S(1)}, f32[1024]{0:T(1024)}, u32[]{:S(2)}) copy-start(f32[1024]{0:T(1024)} %param.16) | copy-start | bytes 12292
  8.6 3.8 %collective-permute-start.3 = (f32[3,8,128]{2,1,0:T(8,128)S(1)}, f32[3,8,128]{2,1,0:T(8,128)S(1)}, u32[]{:S(2)}, u32[]{:S(2)}) collective-permute-start(f32[3,8,128]{2,1,0:T(8,128)S(1)} %shard_map.141), channel_id=1, source_target_pairs={{0,2},{2,0},{1,3},{3,1},{4,6},{6,4},{5,7},{7,5},{8,10},{10,8},{9,1... | collective-permute-start | bytes 36872 | tf_op jit(solution)/shard_map/ppermute | solution.py:888
  9.3 0.8 %copy-start.2 = (s32[10,1024]{1,0:T(8,128)S(1)}, s32[10,1024]{1,0:T(8,128)}, u32[]{:S(2)}) copy-start(s32[10,1024]{1,0:T(8,128)} %connect.1) | copy-start | bytes 122884
  11.7 1.2 %collective-permute-start.2 = (f32[3,8,128]{2,1,0:T(8,128)S(1)}, f32[3,8,128]{2,1,0:T(8,128)S(1)}, u32[]{:S(2)}, u32[]{:S(2)}) collective-permute-start(f32[3,8,128]{2,1,0:T(8,128)S(1)} %broadcast_select_fusion.mine), channel_id=1, source_target_pairs={{0,1},{1,0},{2,3},{3,2},{4,5},{5,4},{6,7},{7,6},{8,9},{9,8},{10,11... | collective-permute-start | bytes 36872 | tf_op jit(solution)/shard_map/ppermute | solution.py:885
  12.9 2.8 %copy-start.1 = (f32[4096]{0:T(1024)S(1)}, f32[4096]{0:T(1024)}, u32[]{:S(2)}) copy-start(f32[4096]{0:T(1024)} %param.13) | copy-start | bytes 49156
  12.9 2.8 %copy-start.4 = (s32[1,3,2,256]{3,2,1,0:T(2,128)S(1)}, s32[1,3,2,256]{3,2,1,0:T(2,128)}, u32[]{:S(2)}) copy-start(s32[1,3,2,256]{3,2,1,0:T(2,128)} %nodes.2) | copy-start | bytes 18436
  15.5 0.7 %copy-start.9 = (s32[1,3,2]{1,2,0:T(2,128)S(1)}, s32[1,3,2]{1,2,0:T(2,128)}, u32[]{:S(2)}) copy-start(s32[1,3,2]{1,2,0:T(2,128)} %param.22) | copy-start | bytes 76
  15.5 1.3 %collective-permute-start.4 = (f32[3,40,128]{2,1,0:T(8,128)S(1)}, f32[3,40,128]{2,1,0:T(8,128)S(1)}, u32[]{:S(2)}, u32[]{:S(2)}) collective-permute-start(f32[3,40,128]{2,1,0:T(8,128)S(1)} %get-tuple-element.36), channel_id=1, source_target_pairs={{0,1},{1,0},{2,3},{3,2},{4,5},{5,4},{6,7},{7,6},{8,9},{9,8},{10,11... | collective-permute-start | bytes 184328 | tf_op jit(solution)/shard_map/ppermute | solution.py:885
  16.8 3.8 %collective-permute-start.6 = (f32[3,8,128]{2,1,0:T(8,128)S(1)}, f32[3,8,128]{2,1,0:T(8,128)S(1)}, u32[]{:S(2)}, u32[]{:S(2)}) collective-permute-start(f32[3,8,128]{2,1,0:T(8,128)S(1)} %slice_add_fusion), channel_id=1, source_target_pairs={{0,6},{5,3},{4,10},{9,7},{8,14},{13,11},{12,13},{1,0},{2,4},{7,1},... | collective-permute-start | bytes 36872 | tf_op jit(solution)/shard_map/ppermute | solution.py:891
  19.3 1.5 %collective-permute-start.5 = (f32[3,8,128]{2,1,0:T(8,128)S(1)}, f32[3,8,128]{2,1,0:T(8,128)S(1)}, u32[]{:S(2)}, u32[]{:S(2)}) collective-permute-start(f32[3,8,128]{2,1,0:T(8,128)S(1)} %slice_add_fusion), channel_id=1, source_target_pairs={{0,4},{5,1},{4,8},{9,5},{8,12},{13,9},{12,13},{1,0},{2,6},{7,3},{6... | collective-permute-start | bytes 36872 | tf_op jit(solution)/shard_map/ppermute | solution.py:891
  19.5 3.9 %collective-permute-start.8 = (f32[6,8,128]{2,1,0:T(8,128)S(1)}, f32[6,8,128]{2,1,0:T(8,128)S(1)}, u32[]{:S(2)}, u32[]{:S(2)}) collective-permute-start(f32[6,8,128]{2,1,0:T(8,128)S(1)} %get-tuple-element.42.link), channel_id=1, source_target_pairs={{0,2},{2,0},{1,3},{3,1},{4,6},{6,4},{5,7},{7,5},{8,10},{10,8},{9,1... | collective-permute-start | bytes 73736 | tf_op jit(solution)/shard_map/ppermute | solution.py:888
  20.8 1.2 %collective-permute-start.7 = (f32[3,8,128]{2,1,0:T(8,128)S(1)}, f32[3,8,128]{2,1,0:T(8,128)S(1)}, u32[]{:S(2)}, u32[]{:S(2)}) collective-permute-start(f32[3,8,128]{2,1,0:T(8,128)S(1)} %shard_map.145.mine), channel_id=1, source_target_pairs={{0,1},{1,0},{2,3},{3,2},{4,5},{5,4},{6,7},{7,6},{8,9},{9,8},{10,11... | collective-permute-start | bytes 36872 | tf_op jit(solution)/shard_map/ppermute | solution.py:885
  24.2 2.4 %collective-permute-start.9 = (f32[3,8,128]{2,1,0:T(8,128)S(1)}, f32[3,8,128]{2,1,0:T(8,128)S(1)}, u32[]{:S(2)}, u32[]{:S(2)}) collective-permute-start(f32[3,8,128]{2,1,0:T(8,128)S(1)} %get-tuple-element.45.middle), channel_id=1, source_target_pairs={{0,4},{5,1},{4,8},{9,5},{8,12},{13,9},{12,13},{1,0},{2,6},{7,3},{6... | collective-permute-start | bytes 36872 | tf_op jit(solution)/shard_map/ppermute | solution.py:891
  25.1 2.7 %copy-start.7 = (f32[1024]{0:T(1024)S(1)}, f32[1024]{0:T(1024)}, u32[]{:S(2)}) copy-start(f32[1024]{0:T(1024)} %param.18) | copy-start | bytes 12292
  25.1 2.7 %copy-start.8 = (f32[1024]{0:T(1024)S(1)}, f32[1024]{0:T(1024)}, u32[]{:S(2)}) copy-start(f32[1024]{0:T(1024)} %param.17) | copy-start | bytes 12292
  26.6 1.3 %copy-start.6 = (f32[1024]{0:T(1024)S(1)}, f32[1024]{0:T(1024)}, u32[]{:S(2)}) copy-start(f32[1024]{0:T(1024)} %param.19) | copy-start | bytes 12292
  26.6 1.2 %collective-permute-start.10 = (f32[3,8,128]{2,1,0:T(8,128)S(1)}, f32[3,8,128]{2,1,0:T(8,128)S(1)}, u32[]{:S(2)}, u32[]{:S(2)}) collective-permute-start(f32[3,8,128]{2,1,0:T(8,128)S(1)} %collective-permute-done.9.mine), channel_id=1, source_target_pairs={{0,1},{1,0},{2,3},{3,2},{4,5},{5,4},{6,7},{7,6},{8,9},{9,8},{10,11... | collective-permute-start | bytes 36872 | tf_op jit(solution)/shard_map/ppermute | solution.py:885

commit v7 on v6

--- a/solution.py
+++ b/solution.py
@@ -899,7 +899,7 @@
             out_specs=jax.tree.map(lambda x: VMEM, outs),
             scratch_shapes=scratch,
             cost_estimate=pl.CostEstimate(
-                flops=2**20, bytes_accessed=2**16, transcendentals=0
+                flops=2**34, bytes_accessed=2**16, transcendentals=0
             ),
         )(*args)
 

time: 40.3 us -> 39.7 us (0.985)
  local copies, waits for them, and re-layouts: 2.2 us -> 1.36 us
  starting transfers between devices: 10.6 us -> 11.3 us
  waiting for transfers between devices: 4.74 us -> 4.32 us
    unnamed x24, local copies, waits for them, and re-layouts: 2.2 us -> 1.36 us
    ppermute x2, starting transfers between devices: 1.36 us -> 2.09 us  [beside(): return lax.ppermute(x, 'sub', swap)]
    ppermute x2, waiting for transfers between devices: 1.4 us -> 1.97 us  [beside(): return lax.ppermute(x, 'sub', swap)]
    ppermute x4, waiting for transfers between devices: 2.85 us -> 2.33 us  [across(): return lax.ppermute(x, 'field', swap)]
    ppermute x5, waiting for transfers between devices: 0.49 us -> 0.01 us  [along(): return lax.ppermute(x, ('dom', 'sub', 'field'), ring(turn))]
  transfers between devices with their start and end apart: 11 -> 11, of which waited for: 6 -> 4; matrix products, arithmetic and copies ran while one was open for 0% -> 0% of each run, Pallas kernels for 9% -> 9%
where the time goes in v7:
time: 39.7 us; the launch traced here: 39.4 us
  starting transfers between devices  11.3 us (28%)
  blocking collectives  10.9 us (27%)
  Pallas kernels  10 us (25%)
  waiting for transfers between devices  4.32 us (11%)
  between operations  1.48 us (4%)
  local copies, waits for them, and re-layouts  1.36 us (3%)
    all_to_all x1, blocking collectives, on_device(): sums = lax.all_to_all(sums, cores, 0, 0, tiled=True)  10.9 us
    pallas_call x10, Pallas kernels, call(): pl.pallas_call(kernel, compiler_params=params, out_shape=outs, in_specs=[...  9.29 us
    ppermute x5, starting transfers between devices, along(): return lax.ppermute(x, ('dom', 'sub', 'field'), ring(turn))  8.98 us
    ppermute x4, waiting for transfers between devices, across(): return lax.ppermute(x, 'field', swap)  2.33 us
    ppermute x2, starting transfers between devices, beside(): return lax.ppermute(x, 'sub', swap)  2.09 us
    ppermute x2, waiting for transfers between devices, beside(): return lax.ppermute(x, 'sub', swap)  1.97 us
    unnamed x24, local copies, waits for them, and re-layouts  1.36 us
  transfers between devices with their start and end apart: 11, of which 4 were waited for; matrix products, arithmetic and copies ran while one was open for 0% of the time, Pallas kernels for 9%

profile of v7, /device:TPU:0, one launch (start us, length us, event | category | flops | bytes accessed | tf_op | source)
XLA Modules:
  0.0 39.4 jit_solution(13485195048401309476)
XLA Ops:
  0.6 0.0 copy-start.6
  0.6 0.0 copy-start.7
  0.7 1.7 %shard_map.140.source = f32[3,8,128]{2,1,0:T(8,128)} custom-call(s32[1,2,3]{2,1,0:T(2,128)} %bitcast.19, s32[1,3,2,256]{3,2,1,0:T(2,128)} %nodes.2, f32[3,4096]{1,0:T(4,128)} %background.3), custom_call_target="tpu_custom_call" | custom-call | flops 17179869184 | bytes 65536 | tf_op jit(solution)/shard_map/pallas_call | solution.py:894
  2.3 4.0 %collective-permute-start.1 = (f32[3,8,128]{2,1,0:T(8,128)}, f32[3,8,128]{2,1,0:T(8,128)S(1)}, u32[]{:S(2)}, u32[]{:S(2)}) collective-permute-start(f32[3,8,128]{2,1,0:T(8,128)} %shard_map.140.source), channel_id=1, source_target_pairs={{0,6},{5,3},{4,10},{9,7},{8,14},{13,11},{12,13},{1,0},{2,4},{7,1},... | collective-permute-start | bytes 36872 | tf_op jit(solution)/shard_map/ppermute | solution.py:891
  6.4 1.6 %collective-permute-start = (f32[3,8,128]{2,1,0:T(8,128)}, f32[3,8,128]{2,1,0:T(8,128)S(1)}, u32[]{:S(2)}, u32[]{:S(2)}) collective-permute-start(f32[3,8,128]{2,1,0:T(8,128)} %shard_map.140.source), channel_id=1, source_target_pairs={{0,4},{5,1},{4,8},{9,5},{8,12},{13,9},{12,13},{1,0},{2,6},{7,3},{6... | collective-permute-start | bytes 36872 | tf_op jit(solution)/shard_map/ppermute | solution.py:891
  7.9 0.7 %copy-done.4 = f32[3,8,128]{2,1,0:T(8,128)S(1)} copy-done((f32[3,8,128]{2,1,0:T(8,128)S(1)}, f32[3,8,128]{2,1,0:T(8,128)}, u32[]{:S(2)}) %copy-start.4) | copy-done | bytes 12312
  8.7 0.5 %collective-permute-start.3 = (f32[3,8,128]{2,1,0:T(8,128)S(1)}, f32[3,8,128]{2,1,0:T(8,128)S(1)}, u32[]{:S(2)}, u32[]{:S(2)}) collective-permute-start(f32[3,8,128]{2,1,0:T(8,128)S(1)} %shard_map.141), channel_id=1, source_target_pairs={{0,2},{2,0},{1,3},{3,1},{4,6},{6,4},{5,7},{7,5},{8,10},{10,8},{9,1... | collective-permute-start | bytes 36872 | tf_op jit(solution)/shard_map/ppermute | solution.py:888
  9.2 0.0 copy-done.6
  9.2 0.0 copy-done.7
  9.2 0.0 copy-done
  9.2 0.0 copy-done.1
  9.2 0.0 copy-done.2
  9.2 1.5 %shard_map.139 = (s32[10,8,128]{2,1,0:T(8,128)S(1)}, f32[30,8,128]{2,1,0:T(8,128)S(1)}, f32[32,192]{1,0:T(8,128)S(1)}, f32[2,8,128]{2,1,0:T(8,128)S(1)}) custom-call(f32[3,4096]{1,0:T(4,128)S(1)} %copy-done, s32[10,1024]{1,0:T(8,128)S(1)} %copy-done.1, f32[30,30]{1,0:T(8,128)S(1)} %copy-done.2, f32[8,128]{1,0:T(8,128)S(1)} %bitcast.14, f32[8,128]{1,0:T(8,128)S(1)} %bitcast.15), custom_call_target="tpu_custom_call" | custom-call | flops 17179869184 | bytes 65536 | tf_op jit(solution)/shard_map/pallas_call | solution.py:894
  10.7 0.0 collective-permute-done
  10.7 0.0 collective-permute-done.1
  10.7 0.1 broadcast_select_fusion.mine
  10.8 0.0 collective-permute-start.2
  11.5 0.9 %collective-permute-done.3.middle = f32[3,8,128]{2,1,0:T(8,128)S(1)} collective-permute-done((f32[3,8,128]{2,1,0:T(8,128)S(1)}, f32[3,8,128]{2,1,0:T(8,128)S(1)}, u32[]{:S(2)}, u32[]{:S(2)}) %collective-permute-start.3) | collective-permute-done | bytes 12320 | tf_op jit(solution)/shard_map/ppermute | solution.py:888
  12.4 0.0 collective-permute-done.2.other
  12.4 2.5 %shard_map.142 = (f32[30,8,128]{2,1,0:T(8,128)S(1)}, f32[2,8,128]{2,1,0:T(8,128)S(1)}, f32[3,40,128]{2,1,0:T(8,128)S(1)}, f32[3,40,128]{2,1,0:T(8,128)S(1)}) custom-call(f32[32,192]{1,0:T(8,128)S(1)} %get-tuple-element.30.wide, f32[30,8,128]{2,1,0:T(8,128)S(1)} %get-tuple-element.32.partial, s32[10,8,128]{2,1,0:T(8,128)S(1)} %get-tuple-element.33.index, ...), custom_call_target="tpu_custom_call" | custom-call | flops 17179869184 | bytes 65536 | tf_op jit(solution)/shard_map/pallas_call | solution.py:894
  14.9 0.0 copy-start.11
  14.9 0.1 collective-permute-start.4
  15.0 0.0 copy-done.3
  15.0 0.0 copy-done.5
  15.0 0.6 %copy-done.11 = s32[1,3,2]{1,2,0:T(2,128)S(1)} copy-done((s32[1,3,2]{1,2,0:T(2,128)S(1)}, s32[1,3,2]{1,2,0:T(2,128)}, u32[]{:S(2)}) %copy-start.11) | copy-done | bytes 48
  15.6 0.7 %shard_map.143.fixed = f32[4,8,128]{2,1,0:T(8,128)S(1)} custom-call(s32[1,2,3]{2,1,0:T(2,128)S(1)} %bitcast.20, s32[1,3,2,256]{3,2,1,0:T(2,128)S(1)} %copy-done.5, f32[32,128]{1,0:T(8,128)S(1)} %bitcast.12), custom_call_target="tpu_custom_call" | custom-call | flops 17179869184 | bytes 65536 | tf_op jit(solution)/shard_map/pallas_call | solution.py:894
  16.3 0.0 collective-permute-done.4.came
  16.3 2.2 %collective-permute-start.6 = (f32[3,8,128]{2,1,0:T(8,128)S(1)}, f32[3,8,128]{2,1,0:T(8,128)S(1)}, u32[]{:S(2)}, u32[]{:S(2)}) collective-permute-start(f32[3,8,128]{2,1,0:T(8,128)S(1)} %slice_add_fusion), channel_id=1, source_target_pairs={{0,6},{5,3},{4,10},{9,7},{8,14},{13,11},{12,13},{1,0},{2,4},{7,1},... | collective-permute-start | bytes 36872 | tf_op jit(solution)/shard_map/ppermute | solution.py:891
  18.5 0.1 collective-permute-start.5
  18.6 0.2 shard_map.144
  18.8 1.6 %collective-permute-start.8 = (f32[6,8,128]{2,1,0:T(8,128)S(1)}, f32[6,8,128]{2,1,0:T(8,128)S(1)}, u32[]{:S(2)}, u32[]{:S(2)}) collective-permute-start(f32[6,8,128]{2,1,0:T(8,128)S(1)} %get-tuple-element.42.link), channel_id=1, source_target_pairs={{0,2},{2,0},{1,3},{3,1},{4,6},{6,4},{5,7},{7,5},{8,10},{10,8},{9,1... | collective-permute-start | bytes 73736 | tf_op jit(solution)/shard_map/ppermute | solution.py:888
  20.3 0.0 collective-permute-done.6.slanted
  20.3 0.0 collective-permute-done.5.straight
  20.4 0.1 collective-permute-start.7
  20.4 1.2 %collective-permute-done.7.other = f32[3,8,128]{2,1,0:T(8,128)S(1)} collective-permute-done((f32[3,8,128]{2,1,0:T(8,128)S(1)}, f32[3,8,128]{2,1,0:T(8,128)S(1)}, u32[]{:S(2)}, u32[]{:S(2)}) %collective-permute-start.7) | collective-permute-done | bytes 12320 | tf_op jit(solution)/shard_map/ppermute | solution.py:885
  21.6 1.1 %collective-permute-done.8.came = f32[6,8,128]{2,1,0:T(8,128)S(1)} collective-permute-done((f32[6,8,128]{2,1,0:T(8,128)S(1)}, f32[6,8,128]{2,1,0:T(8,128)S(1)}, u32[]{:S(2)}, u32[]{:S(2)}) %collective-permute-start.8) | collective-permute-done | bytes 24608 | tf_op jit(solution)/shard_map/ppermute | solution.py:888
  22.7 0.8 %shard_map.146 = (f32[3,32,128]{2,1,0:T(8,128)S(1)}, f32[3,8,128]{2,1,0:T(8,128)S(1)}) custom-call(f32[3,32,128]{2,1,0:T(8,128)S(1)} %get-tuple-element.41.own, f32[6,8,128]{2,1,0:T(8,128)S(1)} %get-tuple-element.42.link, f32[3,8,128]{2,1,0:T(8,128)S(1)} %shard_map.145.mine, f32[3,8,128]{2,1,0:T(8,128)S(1)} %collective-permute-done.7.other, ...), custom_call_target="tpu_custom_call" | custom-call | flops 17179869184 | bytes 65536 | tf_op jit(solution)/shard_map/pallas_call | solution.py:894
  23.5 1.0 %collective-permute-start.9 = (f32[3,8,128]{2,1,0:T(8,128)S(1)}, f32[3,8,128]{2,1,0:T(8,128)S(1)}, u32[]{:S(2)}, u32[]{:S(2)}) collective-permute-start(f32[3,8,128]{2,1,0:T(8,128)S(1)} %get-tuple-element.45.middle), channel_id=1, source_target_pairs={{0,4},{5,1},{4,8},{9,5},{8,12},{13,9},{12,13},{1,0},{2,6},{7,3},{6... | collective-permute-start | bytes 36872 | tf_op jit(solution)/shard_map/ppermute | solution.py:891
  24.6 1.4 %shard_map.147.near = f32[8,128]{1,0:T(8,128)S(1)} custom-call(f32[3,32,128]{2,1,0:T(8,128)S(1)} %get-tuple-element.46.weighted, s32[10,8,128]{2,1,0:T(8,128)S(1)} %get-tuple-element.33.index, f32[30,8,128]{2,1,0:T(8,128)S(1)} %get-tuple-element.47.coupled), custom_call_target="tpu_custom_call" | custom-call | flops 17179869184 | bytes 65536 | tf_op jit(solution)/shard_map/pallas_call | solution.py:894
  26.0 0.0 copy-start.8
  26.0 0.0 collective-permute-done.9.mine
  26.0 0.1 collective-permute-start.10
  26.1 1.2 %collective-permute-done.10.other = f32[3,8,128]{2,1,0:T(8,128)S(1)} collective-permute-done((f32[3,8,128]{2,1,0:T(8,128)S(1)}, f32[3,8,128]{2,1,0:T(8,128)S(1)}, u32[]{:S(2)}, u32[]{:S(2)}) %collective-permute-start.10) | collective-permute-done | bytes 12320 | tf_op jit(solution)/shard_map/ppermute | solution.py:885
  27.2 0.0 copy-done.9
  27.2 0.0 copy-done.10
  27.3 0.6 %shard_map.148 = (f32[8,128]{1,0:T(8,128)S(1)}, f32[16,4,128]{2,1,0:T(4,128)S(1)}, f32[3,8,128]{2,1,0:T(8,128)S(1)}) custom-call(f32[8,128]{1,0:T(8,128)S(1)} %shard_map.147.near, f32[3,8,128]{2,1,0:T(8,128)S(1)} %collective-permute-done.9.mine, f32[3,8,128]{2,1,0:T(8,128)S(1)} %collective-permute-done.10.other, f32[3,8,128]{2,1,0:T(8,128)S(1)} %get-tuple-element.45.middle, ...), custom_call_target="tpu_custom_call" | custom-call | flops 17179869184 | bytes 65536 | tf_op jit(solution)/shard_map/pallas_call | solution.py:894
  27.8 10.9 %all_to_all.5.sums = f32[16,4,128]{2,1,0:T(4,128)S(1)} all-to-all(f32[16,4,128]{2,1,0:T(4,128)S(1)} %get-tuple-element.51), channel_id=1, replica_groups=mesh['groups'=2,'dom'=4,'sub'=2,'field'=2] {'dom','sub','field'}, dimensions={0} | all-to-all | bytes 65536 | tf_op jit(solution)/shard_map/all_to_all | solution.py:1156
  38.7 0.7 %shard_map.149 = (f32[8,128]{1,0:T(8,128)}, f32[8,128]{1,0:T(8,128)}, f32[8,128]{1,0:T(8,128)}) custom-call(f32[16,4,128]{2,1,0:T(4,128)S(1)} %all_to_all.5.sums, f32[8,128]{1,0:T(8,128)S(1)} %get-tuple-element.52.hess, f32[3,8,128]{2,1,0:T(8,128)S(1)} %get-tuple-element.53.vectors), custom_call_target="tpu_custom_call" | custom-call | tf_op jit(solution)/shard_map/pallas_call | solution.py:1158
  (13 shorter events, 0.0 us)
Async XLA Ops:
  0.6 8.6 %copy-start.6 = (f32[1024]{0:T(1024)S(1)}, f32[1024]{0:T(1024)}, u32[]{:S(2)}) copy-start(f32[1024]{0:T(1024)} %param.16) | copy-start | bytes 12292
  0.6 8.6 %copy-start.7 = (f32[1024]{0:T(1024)S(1)}, f32[1024]{0:T(1024)}, u32[]{:S(2)}) copy-start(f32[1024]{0:T(1024)} %param.20) | copy-start | bytes 12292
  2.3 6.9 %copy-start = (f32[3,4096]{1,0:T(4,128)S(1)}, f32[3,4096]{1,0:T(4,128)}, u32[]{:S(2)}) copy-start(f32[3,4096]{1,0:T(4,128)} %background.3) | copy-start | bytes 147460
  2.3 6.9 %copy-start.1 = (s32[10,1024]{1,0:T(8,128)S(1)}, s32[10,1024]{1,0:T(8,128)}, u32[]{:S(2)}) copy-start(s32[10,1024]{1,0:T(8,128)} %connect.1) | copy-start | bytes 122884
  2.3 6.9 %copy-start.2 = (f32[30,30]{1,0:T(8,128)S(1)}, f32[30,30]{1,0:T(8,128)}, u32[]{:S(2)}) copy-start(f32[30,30]{1,0:T(8,128)} %stiff.1) | copy-start | bytes 10804
  2.3 8.4 %collective-permute-start.1 = (f32[3,8,128]{2,1,0:T(8,128)}, f32[3,8,128]{2,1,0:T(8,128)S(1)}, u32[]{:S(2)}, u32[]{:S(2)}) collective-permute-start(f32[3,8,128]{2,1,0:T(8,128)} %shard_map.140.source), channel_id=1, source_target_pairs={{0,6},{5,3},{4,10},{9,7},{8,14},{13,11},{12,13},{1,0},{2,4},{7,1},... | collective-permute-start | bytes 36872 | tf_op jit(solution)/shard_map/ppermute | solution.py:891
  6.4 4.4 %collective-permute-start = (f32[3,8,128]{2,1,0:T(8,128)}, f32[3,8,128]{2,1,0:T(8,128)S(1)}, u32[]{:S(2)}, u32[]{:S(2)}) collective-permute-start(f32[3,8,128]{2,1,0:T(8,128)} %shard_map.140.source), channel_id=1, source_target_pairs={{0,4},{5,1},{4,8},{9,5},{8,12},{13,9},{12,13},{1,0},{2,6},{7,3},{6... | collective-permute-start | bytes 36872 | tf_op jit(solution)/shard_map/ppermute | solution.py:891
  7.9 0.7 %copy-start.4 = (f32[3,8,128]{2,1,0:T(8,128)S(1)}, f32[3,8,128]{2,1,0:T(8,128)}, u32[]{:S(2)}) copy-start(f32[3,8,128]{2,1,0:T(8,128)} %shard_map.140.source) | copy-start | bytes 36868
  8.7 3.7 %collective-permute-start.3 = (f32[3,8,128]{2,1,0:T(8,128)S(1)}, f32[3,8,128]{2,1,0:T(8,128)S(1)}, u32[]{:S(2)}, u32[]{:S(2)}) collective-permute-start(f32[3,8,128]{2,1,0:T(8,128)S(1)} %shard_map.141), channel_id=1, source_target_pairs={{0,2},{2,0},{1,3},{3,1},{4,6},{6,4},{5,7},{7,5},{8,10},{10,8},{9,1... | collective-permute-start | bytes 36872 | tf_op jit(solution)/shard_map/ppermute | solution.py:888
  10.8 1.6 %collective-permute-start.2 = (f32[3,8,128]{2,1,0:T(8,128)S(1)}, f32[3,8,128]{2,1,0:T(8,128)S(1)}, u32[]{:S(2)}, u32[]{:S(2)}) collective-permute-start(f32[3,8,128]{2,1,0:T(8,128)S(1)} %broadcast_select_fusion.mine), channel_id=1, source_target_pairs={{0,1},{1,0},{2,3},{3,2},{4,5},{5,4},{6,7},{7,6},{8,9},{9,8},{10,11... | collective-permute-start | bytes 36872 | tf_op jit(solution)/shard_map/ppermute | solution.py:885
  12.4 2.6 %copy-start.3 = (f32[4096]{0:T(1024)S(1)}, f32[4096]{0:T(1024)}, u32[]{:S(2)}) copy-start(f32[4096]{0:T(1024)} %param.13) | copy-start | bytes 49156
  12.4 2.6 %copy-start.5 = (s32[1,3,2,256]{3,2,1,0:T(2,128)S(1)}, s32[1,3,2,256]{3,2,1,0:T(2,128)}, u32[]{:S(2)}) copy-start(s32[1,3,2,256]{3,2,1,0:T(2,128)} %nodes.2) | copy-start | bytes 18436
  14.9 0.7 %copy-start.11 = (s32[1,3,2]{1,2,0:T(2,128)S(1)}, s32[1,3,2]{1,2,0:T(2,128)}, u32[]{:S(2)}) copy-start(s32[1,3,2]{1,2,0:T(2,128)} %param.22) | copy-start | bytes 76
  14.9 1.3 %collective-permute-start.4 = (f32[3,40,128]{2,1,0:T(8,128)S(1)}, f32[3,40,128]{2,1,0:T(8,128)S(1)}, u32[]{:S(2)}, u32[]{:S(2)}) collective-permute-start(f32[3,40,128]{2,1,0:T(8,128)S(1)} %get-tuple-element.36), channel_id=1, source_target_pairs={{0,1},{1,0},{2,3},{3,2},{4,5},{5,4},{6,7},{7,6},{8,9},{9,8},{10,11... | collective-permute-start | bytes 184328 | tf_op jit(solution)/shard_map/ppermute | solution.py:885
  16.3 4.1 %collective-permute-start.6 = (f32[3,8,128]{2,1,0:T(8,128)S(1)}, f32[3,8,128]{2,1,0:T(8,128)S(1)}, u32[]{:S(2)}, u32[]{:S(2)}) collective-permute-start(f32[3,8,128]{2,1,0:T(8,128)S(1)} %slice_add_fusion), channel_id=1, source_target_pairs={{0,6},{5,3},{4,10},{9,7},{8,14},{13,11},{12,13},{1,0},{2,4},{7,1},... | collective-permute-start | bytes 36872 | tf_op jit(solution)/shard_map/ppermute | solution.py:891
  18.5 1.9 %collective-permute-start.5 = (f32[3,8,128]{2,1,0:T(8,128)S(1)}, f32[3,8,128]{2,1,0:T(8,128)S(1)}, u32[]{:S(2)}, u32[]{:S(2)}) collective-permute-start(f32[3,8,128]{2,1,0:T(8,128)S(1)} %slice_add_fusion), channel_id=1, source_target_pairs={{0,4},{5,1},{4,8},{9,5},{8,12},{13,9},{12,13},{1,0},{2,6},{7,3},{6... | collective-permute-start | bytes 36872 | tf_op jit(solution)/shard_map/ppermute | solution.py:891
  18.8 3.9 %collective-permute-start.8 = (f32[6,8,128]{2,1,0:T(8,128)S(1)}, f32[6,8,128]{2,1,0:T(8,128)S(1)}, u32[]{:S(2)}, u32[]{:S(2)}) collective-permute-start(f32[6,8,128]{2,1,0:T(8,128)S(1)} %get-tuple-element.42.link), channel_id=1, source_target_pairs={{0,2},{2,0},{1,3},{3,1},{4,6},{6,4},{5,7},{7,5},{8,10},{10,8},{9,1... | collective-permute-start | bytes 73736 | tf_op jit(solution)/shard_map/ppermute | solution.py:888
  20.4 1.2 %collective-permute-start.7 = (f32[3,8,128]{2,1,0:T(8,128)S(1)}, f32[3,8,128]{2,1,0:T(8,128)S(1)}, u32[]{:S(2)}, u32[]{:S(2)}) collective-permute-start(f32[3,8,128]{2,1,0:T(8,128)S(1)} %shard_map.145.mine), channel_id=1, source_target_pairs={{0,1},{1,0},{2,3},{3,2},{4,5},{5,4},{6,7},{7,6},{8,9},{9,8},{10,11... | collective-permute-start | bytes 36872 | tf_op jit(solution)/shard_map/ppermute | solution.py:885
  23.5 2.5 %collective-permute-start.9 = (f32[3,8,128]{2,1,0:T(8,128)S(1)}, f32[3,8,128]{2,1,0:T(8,128)S(1)}, u32[]{:S(2)}, u32[]{:S(2)}) collective-permute-start(f32[3,8,128]{2,1,0:T(8,128)S(1)} %get-tuple-element.45.middle), channel_id=1, source_target_pairs={{0,4},{5,1},{4,8},{9,5},{8,12},{13,9},{12,13},{1,0},{2,6},{7,3},{6... | collective-permute-start | bytes 36872 | tf_op jit(solution)/shard_map/ppermute | solution.py:891
  24.6 2.7 %copy-start.9 = (f32[1024]{0:T(1024)S(1)}, f32[1024]{0:T(1024)}, u32[]{:S(2)}) copy-start(f32[1024]{0:T(1024)} %param.18) | copy-start | bytes 12292
  24.6 2.7 %copy-start.10 = (f32[1024]{0:T(1024)S(1)}, f32[1024]{0:T(1024)}, u32[]{:S(2)}) copy-start(f32[1024]{0:T(1024)} %param.17) | copy-start | bytes 12292
  26.0 1.3 %copy-start.8 = (f32[1024]{0:T(1024)S(1)}, f32[1024]{0:T(1024)}, u32[]{:S(2)}) copy-start(f32[1024]{0:T(1024)} %param.19) | copy-start | bytes 12292
  26.0 1.2 %collective-permute-start.10 = (f32[3,8,128]{2,1,0:T(8,128)S(1)}, f32[3,8,128]{2,1,0:T(8,128)S(1)}, u32[]{:S(2)}, u32[]{:S(2)}) collective-permute-start(f32[3,8,128]{2,1,0:T(8,128)S(1)} %collective-permute-done.9.mine), channel_id=1, source_target_pairs={{0,1},{1,0},{2,3},{3,2},{4,5},{5,4},{6,7},{7,6},{8,9},{9,8},{10,11... | collective-permute-start | bytes 36872 | tf_op jit(solution)/shard_map/ppermute | solution.py:885

commit v8 on v7

--- a/solution.py
+++ b/solution.py
@@ -795,11 +795,18 @@
     lookup(table, 2 * rows, index.at[0:1], keep)
 
 
-def pair_near_kernel(weighted, index, coupled, near, pulled):
+def pair_near_kernel(weighted, middle, index, coupled, near, pulled, ghosts):
     def keep(k, c, value):
         pulled[c * 10 + k] = value
 
-    lookup(weighted, weighted.shape[1], index, keep)
+    def begin(k, c):
+        return pulled[c * 10 + k]
+
+    rows = weighted.shape[1]
+    lookup(weighted, rows, index, keep)
+    for c in range(3):
+        ghosts[c, 6:8, :] = middle[c, 4:6, :]
+    lookup(ghosts, 8, index, keep, begin, rows, skip=range(6))
     image = None
     for i in range(30):
         term = coupled[i] * pulled[i]
@@ -840,7 +847,7 @@
     def keep(k, c, value):
         pulled[c * 10 + k] = value
 
-    lookup(ghosts, 12, index, keep, first=rows, skip=NOBODY)
+    lookup(ghosts, 12, index, keep, first=rows, skip=NOBODY + (6, 7))
     image = near[...]
     for i in range(30):
         image = image + coupled[i] * pulled[i]
@@ -996,9 +1003,9 @@
     inner = call(
         pair_near_kernel,
         shape(tile, f32),
-        [pltpu.VMEM((30,) + tile, f32)],
+        [pltpu.VMEM((30,) + tile, f32), pltpu.VMEM((3, 16, LANES), f32)],
         0,
-        (weighted, index, coupled),
+        (weighted, outbound, index, coupled),
     )
     mine, inner = lax.optimization_barrier((mine, inner))
     other = across(mine)

time: 39.7 us -> 39.6 us (level)
  transfers between devices with their start and end apart: 11 -> 11, of which waited for: 4 -> 4; matrix products, arithmetic and copies ran while one was open for 0% -> 0% of each run, Pallas kernels for 9% -> 10%
where the time goes in v8:
time: 39.6 us; the launch traced here: 39.3 us
  starting transfers between devices  11.3 us (29%)
  blocking collectives  10.6 us (27%)
  Pallas kernels  10.2 us (26%)
  waiting for transfers between devices  4.32 us (11%)
  between operations  1.48 us (4%)
  local copies, waits for them, and re-layouts  1.36 us (3%)
    all_to_all x1, blocking collectives, on_device(): sums = lax.all_to_all(sums, cores, 0, 0, tiled=True)  10.6 us
    pallas_call x10, Pallas kernels, call(): pl.pallas_call(kernel, compiler_params=params, out_shape=outs, in_specs=[...  9.48 us
    ppermute x5, starting transfers between devices, along(): return lax.ppermute(x, ('dom', 'sub', 'field'), ring(turn))  8.98 us
    ppermute x4, waiting for transfers between devices, across(): return lax.ppermute(x, 'field', swap)  2.33 us
    ppermute x2, starting transfers between devices, beside(): return lax.ppermute(x, 'sub', swap)  2.09 us
    ppermute x2, waiting for transfers between devices, beside(): return lax.ppermute(x, 'sub', swap)  1.97 us
    unnamed x24, local copies, waits for them, and re-layouts  1.36 us
  transfers between devices with their start and end apart: 11, of which 4 were waited for; matrix products, arithmetic and copies ran while one was open for 0% of the time, Pallas kernels for 10%

profile of v8, /device:TPU:0, one launch (start us, length us, event | category | flops | bytes accessed | tf_op | source)
XLA Modules:
  0.0 39.3 jit_solution(17522969503896724562)
XLA Ops:
  0.6 0.0 copy-start.6
  0.6 0.0 copy-start.7
  0.7 1.7 %shard_map.140.source = f32[3,8,128]{2,1,0:T(8,128)} custom-call(s32[1,2,3]{2,1,0:T(2,128)} %bitcast.19, s32[1,3,2,256]{3,2,1,0:T(2,128)} %nodes.2, f32[3,4096]{1,0:T(4,128)} %background.3), custom_call_target="tpu_custom_call" | custom-call | flops 17179869184 | bytes 65536 | tf_op jit(solution)/shard_map/pallas_call | solution.py:901
  2.3 4.0 %collective-permute-start.1 = (f32[3,8,128]{2,1,0:T(8,128)}, f32[3,8,128]{2,1,0:T(8,128)S(1)}, u32[]{:S(2)}, u32[]{:S(2)}) collective-permute-start(f32[3,8,128]{2,1,0:T(8,128)} %shard_map.140.source), channel_id=1, source_target_pairs={{0,6},{5,3},{4,10},{9,7},{8,14},{13,11},{12,13},{1,0},{2,4},{7,1},... | collective-permute-start | bytes 36872 | tf_op jit(solution)/shard_map/ppermute | solution.py:898
  6.4 1.6 %collective-permute-start = (f32[3,8,128]{2,1,0:T(8,128)}, f32[3,8,128]{2,1,0:T(8,128)S(1)}, u32[]{:S(2)}, u32[]{:S(2)}) collective-permute-start(f32[3,8,128]{2,1,0:T(8,128)} %shard_map.140.source), channel_id=1, source_target_pairs={{0,4},{5,1},{4,8},{9,5},{8,12},{13,9},{12,13},{1,0},{2,6},{7,3},{6... | collective-permute-start | bytes 36872 | tf_op jit(solution)/shard_map/ppermute | solution.py:898
  7.9 0.7 %copy-done.4 = f32[3,8,128]{2,1,0:T(8,128)S(1)} copy-done((f32[3,8,128]{2,1,0:T(8,128)S(1)}, f32[3,8,128]{2,1,0:T(8,128)}, u32[]{:S(2)}) %copy-start.4) | copy-done | bytes 12312
  8.7 0.5 %collective-permute-start.3 = (f32[3,8,128]{2,1,0:T(8,128)S(1)}, f32[3,8,128]{2,1,0:T(8,128)S(1)}, u32[]{:S(2)}, u32[]{:S(2)}) collective-permute-start(f32[3,8,128]{2,1,0:T(8,128)S(1)} %shard_map.141), channel_id=1, source_target_pairs={{0,2},{2,0},{1,3},{3,1},{4,6},{6,4},{5,7},{7,5},{8,10},{10,8},{9,1... | collective-permute-start | bytes 36872 | tf_op jit(solution)/shard_map/ppermute | solution.py:895
  9.2 0.0 copy-done.6
  9.2 0.0 copy-done.7
  9.2 0.0 copy-done
  9.2 0.0 copy-done.1
  9.2 0.0 copy-done.2
  9.2 1.5 %shard_map.139 = (s32[10,8,128]{2,1,0:T(8,128)S(1)}, f32[30,8,128]{2,1,0:T(8,128)S(1)}, f32[32,192]{1,0:T(8,128)S(1)}, f32[2,8,128]{2,1,0:T(8,128)S(1)}) custom-call(f32[3,4096]{1,0:T(4,128)S(1)} %copy-done, s32[10,1024]{1,0:T(8,128)S(1)} %copy-done.1, f32[30,30]{1,0:T(8,128)S(1)} %copy-done.2, f32[8,128]{1,0:T(8,128)S(1)} %bitcast.14, f32[8,128]{1,0:T(8,128)S(1)} %bitcast.15), custom_call_target="tpu_custom_call" | custom-call | flops 17179869184 | bytes 65536 | tf_op jit(solution)/shard_map/pallas_call | solution.py:901
  10.7 0.0 collective-permute-done
  10.7 0.0 collective-permute-done.1
  10.7 0.1 broadcast_select_fusion.mine
  10.8 0.0 collective-permute-start.2
  11.5 0.9 %collective-permute-done.3.middle = f32[3,8,128]{2,1,0:T(8,128)S(1)} collective-permute-done((f32[3,8,128]{2,1,0:T(8,128)S(1)}, f32[3,8,128]{2,1,0:T(8,128)S(1)}, u32[]{:S(2)}, u32[]{:S(2)}) %collective-permute-start.3) | collective-permute-done | bytes 12320 | tf_op jit(solution)/shard_map/ppermute | solution.py:895
  12.4 0.0 collective-permute-done.2.other
  12.4 2.5 %shard_map.142 = (f32[30,8,128]{2,1,0:T(8,128)S(1)}, f32[2,8,128]{2,1,0:T(8,128)S(1)}, f32[3,40,128]{2,1,0:T(8,128)S(1)}, f32[3,40,128]{2,1,0:T(8,128)S(1)}) custom-call(f32[32,192]{1,0:T(8,128)S(1)} %get-tuple-element.30.wide, f32[30,8,128]{2,1,0:T(8,128)S(1)} %get-tuple-element.32.partial, s32[10,8,128]{2,1,0:T(8,128)S(1)} %get-tuple-element.33.index, ...), custom_call_target="tpu_custom_call" | custom-call | flops 17179869184 | bytes 65536 | tf_op jit(solution)/shard_map/pallas_call | solution.py:901
  14.9 0.0 copy-start.11
  14.9 0.1 collective-permute-start.4
  15.0 0.0 copy-done.3
  15.0 0.0 copy-done.5
  15.0 0.6 %copy-done.11 = s32[1,3,2]{1,2,0:T(2,128)S(1)} copy-done((s32[1,3,2]{1,2,0:T(2,128)S(1)}, s32[1,3,2]{1,2,0:T(2,128)}, u32[]{:S(2)}) %copy-start.11) | copy-done | bytes 48
  15.6 0.7 %shard_map.143.fixed = f32[4,8,128]{2,1,0:T(8,128)S(1)} custom-call(s32[1,2,3]{2,1,0:T(2,128)S(1)} %bitcast.20, s32[1,3,2,256]{3,2,1,0:T(2,128)S(1)} %copy-done.5, f32[32,128]{1,0:T(8,128)S(1)} %bitcast.12), custom_call_target="tpu_custom_call" | custom-call | flops 17179869184 | bytes 65536 | tf_op jit(solution)/shard_map/pallas_call | solution.py:901
  16.3 0.0 collective-permute-done.4.came
  16.3 2.2 %collective-permute-start.6 = (f32[3,8,128]{2,1,0:T(8,128)S(1)}, f32[3,8,128]{2,1,0:T(8,128)S(1)}, u32[]{:S(2)}, u32[]{:S(2)}) collective-permute-start(f32[3,8,128]{2,1,0:T(8,128)S(1)} %slice_add_fusion), channel_id=1, source_target_pairs={{0,6},{5,3},{4,10},{9,7},{8,14},{13,11},{12,13},{1,0},{2,4},{7,1},... | collective-permute-start | bytes 36872 | tf_op jit(solution)/shard_map/ppermute | solution.py:898
  18.5 0.1 collective-permute-start.5
  18.6 0.2 shard_map.144
  18.8 1.6 %collective-permute-start.8 = (f32[6,8,128]{2,1,0:T(8,128)S(1)}, f32[6,8,128]{2,1,0:T(8,128)S(1)}, u32[]{:S(2)}, u32[]{:S(2)}) collective-permute-start(f32[6,8,128]{2,1,0:T(8,128)S(1)} %get-tuple-element.42.link), channel_id=1, source_target_pairs={{0,2},{2,0},{1,3},{3,1},{4,6},{6,4},{5,7},{7,5},{8,10},{10,8},{9,1... | collective-permute-start | bytes 73736 | tf_op jit(solution)/shard_map/ppermute | solution.py:895
  20.3 0.0 collective-permute-done.6.slanted
  20.3 0.0 collective-permute-done.5.straight
  20.4 0.1 collective-permute-start.7
  20.4 1.2 %collective-permute-done.7.other = f32[3,8,128]{2,1,0:T(8,128)S(1)} collective-permute-done((f32[3,8,128]{2,1,0:T(8,128)S(1)}, f32[3,8,128]{2,1,0:T(8,128)S(1)}, u32[]{:S(2)}, u32[]{:S(2)}) %collective-permute-start.7) | collective-permute-done | bytes 12320 | tf_op jit(solution)/shard_map/ppermute | solution.py:892
  21.6 1.1 %collective-permute-done.8.came = f32[6,8,128]{2,1,0:T(8,128)S(1)} collective-permute-done((f32[6,8,128]{2,1,0:T(8,128)S(1)}, f32[6,8,128]{2,1,0:T(8,128)S(1)}, u32[]{:S(2)}, u32[]{:S(2)}) %collective-permute-start.8) | collective-permute-done | bytes 24608 | tf_op jit(solution)/shard_map/ppermute | solution.py:895
  22.7 0.8 %shard_map.146 = (f32[3,32,128]{2,1,0:T(8,128)S(1)}, f32[3,8,128]{2,1,0:T(8,128)S(1)}) custom-call(f32[3,32,128]{2,1,0:T(8,128)S(1)} %get-tuple-element.41.own, f32[6,8,128]{2,1,0:T(8,128)S(1)} %get-tuple-element.42.link, f32[3,8,128]{2,1,0:T(8,128)S(1)} %shard_map.145.mine, f32[3,8,128]{2,1,0:T(8,128)S(1)} %collective-permute-done.7.other, ...), custom_call_target="tpu_custom_call" | custom-call | flops 17179869184 | bytes 65536 | tf_op jit(solution)/shard_map/pallas_call | solution.py:901
  23.5 1.0 %collective-permute-start.9 = (f32[3,8,128]{2,1,0:T(8,128)S(1)}, f32[3,8,128]{2,1,0:T(8,128)S(1)}, u32[]{:S(2)}, u32[]{:S(2)}) collective-permute-start(f32[3,8,128]{2,1,0:T(8,128)S(1)} %get-tuple-element.45.middle), channel_id=1, source_target_pairs={{0,4},{5,1},{4,8},{9,5},{8,12},{13,9},{12,13},{1,0},{2,6},{7,3},{6... | collective-permute-start | bytes 36872 | tf_op jit(solution)/shard_map/ppermute | solution.py:898
  24.6 1.7 %shard_map.147.near = f32[8,128]{1,0:T(8,128)S(1)} custom-call(f32[3,32,128]{2,1,0:T(8,128)S(1)} %get-tuple-element.46.weighted, f32[3,8,128]{2,1,0:T(8,128)S(1)} %get-tuple-element.45.middle, s32[10,8,128]{2,1,0:T(8,128)S(1)} %get-tuple-element.33.index, f32[30,8,128]{2,1,0:T(8,128)S(1)} %get-tuple-element.47.coupled), custom_call_target="tpu_custom_call" | custom-call | flops 17179869184 | bytes 65536 | tf_op jit(solution)/shard_map/pallas_call | solution.py:901
  26.2 0.0 copy-start.8
  26.2 0.0 collective-permute-done.9.mine
  26.3 0.1 collective-permute-start.10
  26.3 1.2 %collective-permute-done.10.other = f32[3,8,128]{2,1,0:T(8,128)S(1)} collective-permute-done((f32[3,8,128]{2,1,0:T(8,128)S(1)}, f32[3,8,128]{2,1,0:T(8,128)S(1)}, u32[]{:S(2)}, u32[]{:S(2)}) %collective-permute-start.10) | collective-permute-done | bytes 12320 | tf_op jit(solution)/shard_map/ppermute | solution.py:892
  27.5 0.0 copy-done.9
  27.5 0.0 copy-done.10
  27.5 0.5 %shard_map.148 = (f32[8,128]{1,0:T(8,128)S(1)}, f32[16,4,128]{2,1,0:T(4,128)S(1)}, f32[3,8,128]{2,1,0:T(8,128)S(1)}) custom-call(f32[8,128]{1,0:T(8,128)S(1)} %shard_map.147.near, f32[3,8,128]{2,1,0:T(8,128)S(1)} %collective-permute-done.9.mine, f32[3,8,128]{2,1,0:T(8,128)S(1)} %collective-permute-done.10.other, f32[3,8,128]{2,1,0:T(8,128)S(1)} %get-tuple-element.45.middle, ...), custom_call_target="tpu_custom_call" | custom-call | flops 17179869184 | bytes 65536 | tf_op jit(solution)/shard_map/pallas_call | solution.py:901
  28.0 10.6 %all_to_all.5.sums = f32[16,4,128]{2,1,0:T(4,128)S(1)} all-to-all(f32[16,4,128]{2,1,0:T(4,128)S(1)} %get-tuple-element.51), channel_id=1, replica_groups=mesh['groups'=2,'dom'=4,'sub'=2,'field'=2] {'dom','sub','field'}, dimensions={0} | all-to-all | bytes 65536 | tf_op jit(solution)/shard_map/all_to_all | solution.py:1163
  38.6 0.7 %shard_map.149 = (f32[8,128]{1,0:T(8,128)}, f32[8,128]{1,0:T(8,128)}, f32[8,128]{1,0:T(8,128)}) custom-call(f32[16,4,128]{2,1,0:T(4,128)S(1)} %all_to_all.5.sums, f32[8,128]{1,0:T(8,128)S(1)} %get-tuple-element.52.hess, f32[3,8,128]{2,1,0:T(8,128)S(1)} %get-tuple-element.53.vectors), custom_call_target="tpu_custom_call" | custom-call | tf_op jit(solution)/shard_map/pallas_call | solution.py:1165
  (13 shorter events, 0.0 us)
Async XLA Ops:
  0.6 8.6 %copy-start.6 = (f32[1024]{0:T(1024)S(1)}, f32[1024]{0:T(1024)}, u32[]{:S(2)}) copy-start(f32[1024]{0:T(1024)} %param.16) | copy-start | bytes 12292
  0.6 8.6 %copy-start.7 = (f32[1024]{0:T(1024)S(1)}, f32[1024]{0:T(1024)}, u32[]{:S(2)}) copy-start(f32[1024]{0:T(1024)} %param.20) | copy-start | bytes 12292
  2.3 6.9 %copy-start = (f32[3,4096]{1,0:T(4,128)S(1)}, f32[3,4096]{1,0:T(4,128)}, u32[]{:S(2)}) copy-start(f32[3,4096]{1,0:T(4,128)} %background.3) | copy-start | bytes 147460
  2.3 6.9 %copy-start.1 = (s32[10,1024]{1,0:T(8,128)S(1)}, s32[10,1024]{1,0:T(8,128)}, u32[]{:S(2)}) copy-start(s32[10,1024]{1,0:T(8,128)} %connect.1) | copy-start | bytes 122884
  2.3 6.9 %copy-start.2 = (f32[30,30]{1,0:T(8,128)S(1)}, f32[30,30]{1,0:T(8,128)}, u32[]{:S(2)}) copy-start(f32[30,30]{1,0:T(8,128)} %stiff.1) | copy-start | bytes 10804
  2.3 8.4 %collective-permute-start.1 = (f32[3,8,128]{2,1,0:T(8,128)}, f32[3,8,128]{2,1,0:T(8,128)S(1)}, u32[]{:S(2)}, u32[]{:S(2)}) collective-permute-start(f32[3,8,128]{2,1,0:T(8,128)} %shard_map.140.source), channel_id=1, source_target_pairs={{0,6},{5,3},{4,10},{9,7},{8,14},{13,11},{12,13},{1,0},{2,4},{7,1},... | collective-permute-start | bytes 36872 | tf_op jit(solution)/shard_map/ppermute | solution.py:898
  6.4 4.4 %collective-permute-start = (f32[3,8,128]{2,1,0:T(8,128)}, f32[3,8,128]{2,1,0:T(8,128)S(1)}, u32[]{:S(2)}, u32[]{:S(2)}) collective-permute-start(f32[3,8,128]{2,1,0:T(8,128)} %shard_map.140.source), channel_id=1, source_target_pairs={{0,4},{5,1},{4,8},{9,5},{8,12},{13,9},{12,13},{1,0},{2,6},{7,3},{6... | collective-permute-start | bytes 36872 | tf_op jit(solution)/shard_map/ppermute | solution.py:898
  7.9 0.7 %copy-start.4 = (f32[3,8,128]{2,1,0:T(8,128)S(1)}, f32[3,8,128]{2,1,0:T(8,128)}, u32[]{:S(2)}) copy-start(f32[3,8,128]{2,1,0:T(8,128)} %shard_map.140.source) | copy-start | bytes 36868
  8.7 3.7 %collective-permute-start.3 = (f32[3,8,128]{2,1,0:T(8,128)S(1)}, f32[3,8,128]{2,1,0:T(8,128)S(1)}, u32[]{:S(2)}, u32[]{:S(2)}) collective-permute-start(f32[3,8,128]{2,1,0:T(8,128)S(1)} %shard_map.141), channel_id=1, source_target_pairs={{0,2},{2,0},{1,3},{3,1},{4,6},{6,4},{5,7},{7,5},{8,10},{10,8},{9,1... | collective-permute-start | bytes 36872 | tf_op jit(solution)/shard_map/ppermute | solution.py:895
  10.8 1.6 %collective-permute-start.2 = (f32[3,8,128]{2,1,0:T(8,128)S(1)}, f32[3,8,128]{2,1,0:T(8,128)S(1)}, u32[]{:S(2)}, u32[]{:S(2)}) collective-permute-start(f32[3,8,128]{2,1,0:T(8,128)S(1)} %broadcast_select_fusion.mine), channel_id=1, source_target_pairs={{0,1},{1,0},{2,3},{3,2},{4,5},{5,4},{6,7},{7,6},{8,9},{9,8},{10,11... | collective-permute-start | bytes 36872 | tf_op jit(solution)/shard_map/ppermute | solution.py:892
  12.4 2.6 %copy-start.3 = (f32[4096]{0:T(1024)S(1)}, f32[4096]{0:T(1024)}, u32[]{:S(2)}) copy-start(f32[4096]{0:T(1024)} %param.13) | copy-start | bytes 49156
  12.4 2.6 %copy-start.5 = (s32[1,3,2,256]{3,2,1,0:T(2,128)S(1)}, s32[1,3,2,256]{3,2,1,0:T(2,128)}, u32[]{:S(2)}) copy-start(s32[1,3,2,256]{3,2,1,0:T(2,128)} %nodes.2) | copy-start | bytes 18436
  14.9 0.7 %copy-start.11 = (s32[1,3,2]{1,2,0:T(2,128)S(1)}, s32[1,3,2]{1,2,0:T(2,128)}, u32[]{:S(2)}) copy-start(s32[1,3,2]{1,2,0:T(2,128)} %param.22) | copy-start | bytes 76
  14.9 1.3 %collective-permute-start.4 = (f32[3,40,128]{2,1,0:T(8,128)S(1)}, f32[3,40,128]{2,1,0:T(8,128)S(1)}, u32[]{:S(2)}, u32[]{:S(2)}) collective-permute-start(f32[3,40,128]{2,1,0:T(8,128)S(1)} %get-tuple-element.36), channel_id=1, source_target_pairs={{0,1},{1,0},{2,3},{3,2},{4,5},{5,4},{6,7},{7,6},{8,9},{9,8},{10,11... | collective-permute-start | bytes 184328 | tf_op jit(solution)/shard_map/ppermute | solution.py:892
  16.3 4.1 %collective-permute-start.6 = (f32[3,8,128]{2,1,0:T(8,128)S(1)}, f32[3,8,128]{2,1,0:T(8,128)S(1)}, u32[]{:S(2)}, u32[]{:S(2)}) collective-permute-start(f32[3,8,128]{2,1,0:T(8,128)S(1)} %slice_add_fusion), channel_id=1, source_target_pairs={{0,6},{5,3},{4,10},{9,7},{8,14},{13,11},{12,13},{1,0},{2,4},{7,1},... | collective-permute-start | bytes 36872 | tf_op jit(solution)/shard_map/ppermute | solution.py:898
  18.5 1.9 %collective-permute-start.5 = (f32[3,8,128]{2,1,0:T(8,128)S(1)}, f32[3,8,128]{2,1,0:T(8,128)S(1)}, u32[]{:S(2)}, u32[]{:S(2)}) collective-permute-start(f32[3,8,128]{2,1,0:T(8,128)S(1)} %slice_add_fusion), channel_id=1, source_target_pairs={{0,4},{5,1},{4,8},{9,5},{8,12},{13,9},{12,13},{1,0},{2,6},{7,3},{6... | collective-permute-start | bytes 36872 | tf_op jit(solution)/shard_map/ppermute | solution.py:898
  18.8 3.9 %collective-permute-start.8 = (f32[6,8,128]{2,1,0:T(8,128)S(1)}, f32[6,8,128]{2,1,0:T(8,128)S(1)}, u32[]{:S(2)}, u32[]{:S(2)}) collective-permute-start(f32[6,8,128]{2,1,0:T(8,128)S(1)} %get-tuple-element.42.link), channel_id=1, source_target_pairs={{0,2},{2,0},{1,3},{3,1},{4,6},{6,4},{5,7},{7,5},{8,10},{10,8},{9,1... | collective-permute-start | bytes 73736 | tf_op jit(solution)/shard_map/ppermute | solution.py:895
  20.4 1.2 %collective-permute-start.7 = (f32[3,8,128]{2,1,0:T(8,128)S(1)}, f32[3,8,128]{2,1,0:T(8,128)S(1)}, u32[]{:S(2)}, u32[]{:S(2)}) collective-permute-start(f32[3,8,128]{2,1,0:T(8,128)S(1)} %shard_map.145.mine), channel_id=1, source_target_pairs={{0,1},{1,0},{2,3},{3,2},{4,5},{5,4},{6,7},{7,6},{8,9},{9,8},{10,11... | collective-permute-start | bytes 36872 | tf_op jit(solution)/shard_map/ppermute | solution.py:892
  23.5 2.7 %collective-permute-start.9 = (f32[3,8,128]{2,1,0:T(8,128)S(1)}, f32[3,8,128]{2,1,0:T(8,128)S(1)}, u32[]{:S(2)}, u32[]{:S(2)}) collective-permute-start(f32[3,8,128]{2,1,0:T(8,128)S(1)} %get-tuple-element.45.middle), channel_id=1, source_target_pairs={{0,4},{5,1},{4,8},{9,5},{8,12},{13,9},{12,13},{1,0},{2,6},{7,3},{6... | collective-permute-start | bytes 36872 | tf_op jit(solution)/shard_map/ppermute | solution.py:898
  24.6 2.9 %copy-start.9 = (f32[1024]{0:T(1024)S(1)}, f32[1024]{0:T(1024)}, u32[]{:S(2)}) copy-start(f32[1024]{0:T(1024)} %param.18) | copy-start | bytes 12292
  24.6 2.9 %copy-start.10 = (f32[1024]{0:T(1024)S(1)}, f32[1024]{0:T(1024)}, u32[]{:S(2)}) copy-start(f32[1024]{0:T(1024)} %param.17) | copy-start | bytes 12292
  26.2 1.3 %copy-start.8 = (f32[1024]{0:T(1024)S(1)}, f32[1024]{0:T(1024)}, u32[]{:S(2)}) copy-start(f32[1024]{0:T(1024)} %param.19) | copy-start | bytes 12292
  26.3 1.2 %collective-permute-start.10 = (f32[3,8,128]{2,1,0:T(8,128)S(1)}, f32[3,8,128]{2,1,0:T(8,128)S(1)}, u32[]{:S(2)}, u32[]{:S(2)}) collective-permute-start(f32[3,8,128]{2,1,0:T(8,128)S(1)} %collective-permute-done.9.mine), channel_id=1, source_target_pairs={{0,1},{1,0},{2,3},{3,2},{4,5},{5,4},{6,7},{7,6},{8,9},{9,8},{10,11... | collective-permute-start | bytes 36872 | tf_op jit(solution)/shard_map/ppermute | solution.py:892
